TPU v7x, 128 devices: a whole 4x4x4 slice. The times are simulated.
128 devices in a mesh: sec: 2 (over core), dev: 64 (over x, y, z).
Axes of the slice: x: 4, y: 4, z: 4, core: 2. Of those that a mesh axis runs over, the one named last changes fastest.
Arguments:
- field_start: float32 [512, 8, 128, 128], P('dev', None, 'sec'), may hold values from -6 to 6
- forcing: float32 [512, 8, 128, 128], P('dev', None, 'sec'), may hold values from -6 to 6
- traction_start: float32 [128, 65536], P('sec', 'dev'), may hold values from -3 to 3
- conductivity: float32 [512, 8, 128], P('dev'), may hold values from 0.5 to 2
- reaction: float32 [512, 8, 128], P('dev'), may hold values from 0.1 to 2
- surface_order: int32 [65536], P('dev'), may hold values from 0 to 1023, as said below
- near_tiles: bfloat16 [128, 512, 2560], P('dev'), may hold values from -0.125 to 0.125
- col_basis: bfloat16 [128, 32, 512], P('dev'), may hold values from -0.25 to 0.25
- row_basis: bfloat16 [128, 32, 512], P('dev'), may hold values from -1 to 1
- couplings: bfloat16 [128, 32, 4096], P('dev'), may hold values from -0.125 to 0.125
- far_leaf: int32 [128, 128], P('dev'), may hold values from 0 to 1, as said below
Outputs:
- field_end: float32 [512, 8, 128, 128], P('dev', None, 'sec')
- traction_end: float32 [128, 65536], P('sec', 'dev')
Inputs may be any that keep to these rules, and one draw needn't show every extreme that they name: `surface_order`: each aligned block of 1024 entries is a permutation of 0 to 1023. `far_leaf`: 0 wherever the row and column clusters lie within 2 of each other.
All inputs are finite; a program needn't handle non-finite values.
Results may differ from a plain program's by a relative error of at most 0.014.
Values may be sent and summed in bfloat16 or wider, within the bound.
No kernel may reach another device: no remote copies, remote signals or barrier semaphores. Data moves between devices by JAX's collectives and lax.ppermute only.
A program may use at most 128 MiB of HBM per device.

v0:
```python
import jax
import jax.numpy as jnp
from jax import lax
from jax.sharding import PartitionSpec as P

CLUSTER = 512
RANK = 32
BAND = 2
SWEEPS = 4
BLOCKS = 2
CL_DEV = 2


spectrum_center = 1.0
spectrum_half = 0.95


def padded_2(cells, sides, width):
    for axis, dim in sides:
        count = lax.axis_size(axis)
        ends = count - 1
        head = lax.slice_in_dim(cells, 0, width, axis=dim)
        tail = lax.slice_in_dim(cells, cells.shape[dim] - width, cells.shape[dim], axis=dim)
        cells = jnp.concatenate(
            [
                lax.ppermute(tail, axis, [(i, (i + 1) % count) for i in range(ends)]),
                cells,
                lax.ppermute(head, axis, [((i + 1) % count, i) for i in range(ends)]),
            ],
            axis=dim,
        )
    return cells


def in_order(pieces, dim):
    lengths = list(pieces.shape[1:])
    lengths[dim] *= pieces.shape[0]
    return jnp.moveaxis(pieces, 0, dim).reshape(lengths)


def copy_for_each(value, axis):
    copies = jnp.broadcast_to(value, (lax.axis_size(axis), *value.shape))
    return lax.all_to_all(copies, axis, split_axis=0, concat_axis=0, tiled=True)


def gathered_copies(value, axis, dim):
    return in_order(copy_for_each(value, axis), dim)


def gated(active, compute, blank_fn, *operands):
    return compute(*operands)


def face_terms(conductivity, reaction):
    beside = padded_2(conductivity.astype(jnp.bfloat16), (("dev", 0),), 1).astype(
        conductivity.dtype
    )
    padded = jnp.pad(conductivity, ((0, 0), (1, 1), (1, 1)))
    ny_cells = conductivity.shape[1]
    top_mask = (jnp.arange(ny_cells) < ny_cells - 1).astype(jnp.float32)[None, :, None]
    west_face = 0.5 * (conductivity + beside[:-2])
    east_face = 0.5 * (conductivity + beside[2:])
    south_face = 0.5 * (conductivity + padded[:, :-2, 1:-1])
    north_face = 0.5 * (conductivity + padded[:, 2:, 1:-1]) * top_mask
    lower_face = 0.5 * (conductivity + padded[:, 1:-1, :-2])
    upper_face = 0.5 * (conductivity + padded[:, 1:-1, 2:])
    diagonal = west_face + east_face + south_face + north_face + lower_face + upper_face + reaction
    face_coeffs = tuple(
        (
            entry[:, :, None, :]
            for entry in (west_face, east_face, south_face, north_face, lower_face, upper_face)
        )
    )
    return (face_coeffs, (1.0 / diagonal)[:, :, None, :], diagonal[:, :, None, :])


def operate(values, face_coeffs, diagonal):
    extended = padded_2(values, (("dev", 0),), 1)

    def stencil(extended, values):
        west_face, east_face, south_face, north_face, lower_face, upper_face = face_coeffs
        padded = jnp.pad(values, ((0, 0), (1, 1), (0, 0), (1, 1)))
        nearby = west_face * extended[:-2] + east_face * extended[2:]
        nearby = nearby + south_face * padded[:, :-2, :, 1:-1] + north_face * padded[:, 2:, :, 1:-1]
        nearby = nearby + lower_face * padded[:, 1:-1, :, :-2] + upper_face * padded[:, 1:-1, :, 2:]
        return diagonal * values - nearby

    return gated(None, stencil, lambda extended, values: jnp.zeros_like(values), extended, values)


def chebyshev(solution, right_side, apply_op, inverse_diag):
    sigma_ratio = spectrum_center / spectrum_half
    residual = right_side - apply_op(solution)
    update = inverse_diag * residual / spectrum_center
    rho_now = 1.0 / sigma_ratio
    for sweep_index in range(SWEEPS):
        solution = solution + update
        if sweep_index + 1 < SWEEPS:
            residual = residual - apply_op(update)
            rho_next = 1.0 / (2.0 * sigma_ratio - rho_now)
            update = rho_next * rho_now * update + 2.0 * rho_next / spectrum_half * (
                inverse_diag * residual
            )
            rho_now = rho_next
    return solution


def volume_block(
    solution, forcing_all, traction, surface_order, face_coeffs, inverse_diag, diagonal
):
    x_cells = solution.shape[0]
    columns = solution.shape[2]
    z_cells = solution.shape[3]
    surface = (
        jnp.zeros((columns, x_cells * z_cells), jnp.float32).at[:, surface_order].set(traction)
    )
    placed = jnp.transpose(surface.reshape(columns, x_cells, z_cells), (1, 0, 2))
    right_side = forcing_all.at[:, -1, :, :].add(placed)

    def apply_op(values):
        return operate(values, face_coeffs, diagonal)

    return chebyshev(solution, right_side, apply_op, inverse_diag)


def surface_trace(solution, surface_order):
    columns = solution.shape[2]
    top_layer = jnp.transpose(solution[:, -1, :, :], (1, 0, 2)).reshape(columns, -1)
    return top_layer[:, surface_order].astype(jnp.bfloat16)


def boundary(traces, near_tiles, col_basis, row_basis, couplings, far_leaf):
    columns = traces.shape[0]
    extended = padded_2(traces, (("dev", 1),), BAND * CLUSTER)
    blocks = traces.reshape(columns, CL_DEV, CLUSTER)
    projected = jnp.einsum("nck,crk->ncr", blocks, col_basis, preferred_element_type=jnp.float32)
    projected = projected.astype(jnp.bfloat16).reshape(columns, CL_DEV * RANK)
    leaves = jnp.repeat(far_leaf, RANK, axis=1).astype(jnp.bfloat16)[:, None, :]
    masked = (couplings * leaves).reshape(CL_DEV * RANK, -1)
    summed = lax.dot_general(
        gathered_copies(projected, "dev", 1),
        masked,
        (((1,), (1,)), ((), ())),
        preferred_element_type=jnp.float32,
    )
    coupled = summed.astype(jnp.bfloat16).reshape(columns, CL_DEV, RANK)

    def finish(extended, coupled):
        pieces = []
        for slot in range(CL_DEV):
            window = extended[:, slot * CLUSTER : (slot + 2 * BAND + 1) * CLUSTER]
            pieces.append(
                lax.dot_general(
                    window,
                    near_tiles[slot],
                    (((1,), (1,)), ((), ())),
                    preferred_element_type=jnp.float32,
                )
            )
        distant = jnp.einsum("ncr,crk->nck", coupled, row_basis, preferred_element_type=jnp.float32)
        return (jnp.stack(pieces, axis=1) + distant).reshape(columns, CL_DEV * CLUSTER)

    def blank_fn(extended, coupled):
        return jnp.zeros((columns, CL_DEV * CLUSTER), jnp.float32)

    return gated(None, finish, blank_fn, extended, coupled)


def shards(
    field_start,
    forcing,
    traction_start,
    conductivity,
    reaction,
    surface_order,
    near_tiles,
    col_basis,
    row_basis,
    couplings,
    far_leaf,
):
    face_coeffs, inverse_diag, diagonal = face_terms(conductivity, reaction)
    solution = field_start
    traction = traction_start
    for block_index in range(BLOCKS):
        solution = volume_block(
            solution, forcing, traction, surface_order, face_coeffs, inverse_diag, diagonal
        )
        traces = surface_trace(solution, surface_order)
        traction = boundary(traces, near_tiles, col_basis, row_basis, couplings, far_leaf)
    return (solution, traction)


def solution(mesh):
    in_specs = (
        P("dev", None, "sec", None),
        P("dev", None, "sec", None),
        P("sec", "dev"),
        P("dev", None, None),
        P("dev", None, None),
        P("dev"),
        P("dev", None, None),
        P("dev", None, None),
        P("dev", None, None),
        P("dev", None, None),
        P("dev", None),
    )
    out_specs = (P("dev", None, "sec", None), P("sec", "dev"))
    return jax.shard_map(shards, mesh=mesh, in_specs=in_specs, out_specs=out_specs, check_vma=False)
```

profile of v0, /device:TPU:6, one launch (start us, length us, event | category | flops | bytes accessed | tf_op | source)
XLA Modules:
  0.0 245.8 jit_solution(8531704380115492149)
XLA Ops:
  2.3 3.8 %collective-permute-start = (bf16[1,8,128]{2,1,0:T(8,128)(2,1)S(1)}, bf16[1,8,128]{2,1,0:T(8,128)(2,1)S(1)}, u32[]{:S(2)}, u32[]{:S(2)}) collective-permute-start(bf16[1,8,128]{2,1,0:T(8,128)(2,1)S(1)} %get-tuple-element.62), channel_id=1, source_target_pairs={{0,1},{1,2},{2,3},{3,4},{4,5},{5,6},{6,7},{7,8},{8,9},{9,10},{10,1... | collective-permute-start | bytes 6152 | tf_op jit(solution)/shard_map/ppermute | solution.py:26
  6.2 6.8 %collective-permute-start.1 = (bf16[1,8,128]{2,1,0:T(8,128)(2,1)S(1)}, bf16[1,8,128]{2,1,0:T(8,128)(2,1)S(1)}, u32[]{:S(2)}, u32[]{:S(2)}) collective-permute-start(bf16[1,8,128]{2,1,0:T(8,128)(2,1)S(1)} %get-tuple-element.63), channel_id=1, source_target_pairs={{1,0},{2,1},{3,2},{4,3},{5,4},{6,5},{7,6},{8,7},{9,8},{10,9},{11,1... | collective-permute-start | bytes 6152 | tf_op jit(solution)/shard_map/ppermute | solution.py:28
  16.7 8.1 %collective-permute-start.3 = (f32[1,8,64,128]{3,2,1,0:T(8,128)}, f32[1,8,64,128]{3,2,1,0:T(8,128)}, u32[]{:S(2)}, u32[]{:S(2)}) collective-permute-start(f32[1,8,64,128]{3,2,1,0:T(8,128)} %get-tuple-element.61), channel_id=1, source_target_pairs={{1,0},{2,1},{3,2},{4,3},{5,4},{6,5},{7,6},{8,7},{9,8},{10,9},{11,1... | collective-permute-start | bytes 786440 | tf_op jit(solution)/shard_map/ppermute | solution.py:28
  25.1 3.2 %scatter_custom_fusion = f32[64,1024]{0,1:T(8,128)S(1)} fusion(s32[1024]{0:T(1024)S(1)} %get-tuple-element.65, f32[1024,64]{1,0:T(8,128)S(1)} %copy.38, f32[]{:T(128)} %constant.64.clone.1), kind=kCustom, calls=%fused_computation.211 | custom fusion | bytes 262148 | tf_op jit(solution)/shard_map/scatter | solution.py:115
  30.9 3.5 %broadcast_multiply_fusion.1 = (f32[8,8,64,128]{3,2,1,0:T(8,128)S(1)}, f32[8,8,64,128]{3,2,1,0:T(8,128)S(1)}) fusion(f32[8,8,128]{2,1,0:T(8,128)S(1)} %get-tuple-element.38, f32[8,8,64,128]{3,2,1,0:T(8,128)S(1)} %fusion.145, f32[8,8,128]{2,1,0:T(8,128)S(1)} %get-tuple-element.45, f32[8,8,128]{2,1,0:T(8,128)S(1)} %get-tuple-element.44, ...), kind=kLoop, calls=%fused_computation.195 | loop fusion | flops 8912896 | bytes 9175040 | tf_op jit(solution)/shard_map/mul | solution.py:94
  34.5 1.9 collective-permute-start.4
  36.4 8.1 %collective-permute-start.5 = (f32[1,8,64,128]{3,2,1,0:T(8,128)S(1)}, f32[1,8,64,128]{3,2,1,0:T(8,128)S(1)}, u32[]{:S(2)}, u32[]{:S(2)}) collective-permute-start(f32[1,8,64,128]{3,2,1,0:T(8,128)S(1)} %get-tuple-element.59), channel_id=1, source_target_pairs={{1,0},{2,1},{3,2},{4,3},{5,4},{6,5},{7,6},{8,7},{9,8},{10,9},{11,1... | collective-permute-start | bytes 786440 | tf_op jit(solution)/shard_map/ppermute | solution.py:28
  44.5 3.2 %collective-permute-done.4 = f32[1,8,64,128]{3,2,1,0:T(8,128)S(1)} collective-permute-done((f32[1,8,64,128]{3,2,1,0:T(8,128)S(1)}, f32[1,8,64,128]{3,2,1,0:T(8,128)S(1)}, u32[]{:S(2)}, u32[]{:S(2)}) %collective-permute-start.4) | collective-permute-done | bytes 262176 | tf_op jit(solution)/shard_map/ppermute | solution.py:26
  49.0 3.8 %multiply_add_fusion.3 = (f32[8,8,64,128]{3,2,1,0:T(8,128)S(1)}, f32[8,8,64,128]{3,2,1,0:T(8,128)}) fusion(f32[8,8,128]{2,1,0:T(8,128)S(1)} %get-tuple-element.38, f32[8,8,64,128]{3,2,1,0:T(8,128)S(1)} %get-tuple-element.37, f32[8,8,128]{2,1,0:T(8,128)S(1)} %get-tuple-element.45, f32[8,8,128]{2,1,0:T(8,128)S(1)} %get-tuple-element.44, ...), kind=kLoop, calls=%fused_computation.179 | loop fusion | flops 11010048 | bytes 9175040 | tf_op jit(solution)/shard_map/add | solution.py:101
  55.5 8.6 %collective-permute-start.7 = (f32[1,8,64,128]{3,2,1,0:T(8,128)S(1)}, f32[1,8,64,128]{3,2,1,0:T(8,128)S(1)}, u32[]{:S(2)}, u32[]{:S(2)}) collective-permute-start(f32[1,8,64,128]{3,2,1,0:T(8,128)S(1)} %get-tuple-element.57), channel_id=1, source_target_pairs={{1,0},{2,1},{3,2},{4,3},{5,4},{6,5},{7,6},{8,7},{9,8},{10,9},{11,1... | collective-permute-start | bytes 786440 | tf_op jit(solution)/shard_map/ppermute | solution.py:28
  64.4 2.4 collective-permute-done.6
  68.0 3.8 %multiply_add_fusion.2 = (f32[8,8,64,128]{3,2,1,0:T(8,128)S(1)}, f32[8,8,64,128]{3,2,1,0:T(8,128)S(1)}) fusion(f32[8,8,64,128]{3,2,1,0:T(8,128)S(1)} %get-tuple-element.34, f32[8,8,128]{2,1,0:T(8,128)S(1)} %get-tuple-element.38, f32[8,8,64,128]{3,2,1,0:T(8,128)} %get-tuple-element.35, f32[8,8,128]{2,1,0:T(8,128)S(1)} %get-tuple-element.45, ...), kind=kLoop, calls=%fused_computation.178 | loop fusion | flops 10485760 | bytes 9175040 | tf_op jit(solution)/shard_map/add | solution.py:101
  71.8 2.1 collective-permute-start.8
  73.9 8.6 %collective-permute-start.9 = (f32[1,8,64,128]{3,2,1,0:T(8,128)S(1)}, f32[1,8,64,128]{3,2,1,0:T(8,128)S(1)}, u32[]{:S(2)}, u32[]{:S(2)}) collective-permute-start(f32[1,8,64,128]{3,2,1,0:T(8,128)S(1)} %get-tuple-element.55), channel_id=1, source_target_pairs={{1,0},{2,1},{3,2},{4,3},{5,4},{6,5},{7,6},{8,7},{9,8},{10,9},{11,1... | collective-permute-start | bytes 786440 | tf_op jit(solution)/shard_map/ppermute | solution.py:28
  82.6 2.3 collective-permute-done.8
  86.4 3.5 %fusion.52 = f32[8,8,64,128]{3,2,1,0:T(8,128)S(1)} fusion(f32[8,8,64,128]{3,2,1,0:T(8,128)S(1)} %get-tuple-element.33, f32[8,8,64,128]{3,2,1,0:T(8,128)S(1)} %get-tuple-element.32, f32[1,8,64,128]{3,2,1,0:T(8,128)S(1)} %collective-permute-done.9, f32[1,8,64,128]{3,2,1,0:T(8,128)S(1)} %collective-permute-done.8, f32[8,8,64,128]{3,2,1,0:T(8,128)S(1)} %copy-done.2, ...), kind=kLoop, calls=%fused_computation.88 | loop fusion | flops 13107200 | bytes 13369344 | tf_op jit(solution)/shard_map/add | solution.py:97
  90.2 3.2 %gather_fusion = bf16[1024,64]{1,0:T(8,128)(2,1)S(1)} fusion(bf16[64,1024]{0,1:T(8,128)(2,1)S(1)} %bitcast.100, s32[1024]{0:T(1024)S(1)} %get-tuple-element.64), kind=kCustom, calls=%fused_computation | custom fusion | bytes 266240 | tf_op jit(solution)/shard_map/gather | solution.py:129
  93.4 1.9 collective-permute-start.10
  95.3 8.6 %collective-permute-start.11 = (bf16[64,1024]{0,1:T(8,128)(2,1)S(1)}, bf16[64,1024]{0,1:T(8,128)(2,1)}, u32[]{:S(2)}, u32[]{:S(2)}) collective-permute-start(bf16[64,1024]{0,1:T(8,128)(2,1)S(1)} %bitcast.109), channel_id=1, source_target_pairs={{1,0},{2,1},{3,2},{4,3},{5,4},{6,5},{7,6},{8,7},{9,8},{10,9},{11,1... | collective-permute-start | bytes 393224 | tf_op jit(solution)/shard_map/ppermute | solution.py:28
  106.8 3.0 %reshape.197 = bf16[64,2,2048]{2,1,0:T(2,128)(2,1)} reshape(bf16[64,64,64]{2,1,0:T(8,128)(2,1)} %broadcast_in_dim.9) | data formatting | bytes 1048576
  109.8 6.9 %all-to-all-start = ((bf16[64,2,2048]{2,1,0:T(2,128)(2,1)}), bf16[64,2,2048]{2,1,0:T(2,128)(2,1)}, u32[]{:S(2)}, u32[]{:S(2)}) async-start(bf16[64,2,2048]{2,1,0:T(2,128)(2,1)} %reshape.197), calls=%async_computation | async-start | bytes 1048576 | tf_op jit(solution)/shard_map/all_to_all | solution.py:43
  117.6 3.4 %collective-permute-start.12 = (f32[1,8,64,128]{3,2,1,0:T(8,128)}, f32[1,8,64,128]{3,2,1,0:T(8,128)}, u32[]{:S(2)}, u32[]{:S(2)}) collective-permute-start(f32[1,8,64,128]{3,2,1,0:T(8,128)} %get-tuple-element.52), channel_id=1, source_target_pairs={{0,1},{1,2},{2,3},{3,4},{4,5},{5,6},{6,7},{7,8},{8,9},{9,10},{10,1... | collective-permute-start | bytes 786440 | tf_op jit(solution)/shard_map/ppermute | solution.py:26
  121.0 6.9 %collective-permute-start.13 = (f32[1,8,64,128]{3,2,1,0:T(8,128)}, f32[1,8,64,128]{3,2,1,0:T(8,128)}, u32[]{:S(2)}, u32[]{:S(2)}) collective-permute-start(f32[1,8,64,128]{3,2,1,0:T(8,128)} %get-tuple-element.53), channel_id=1, source_target_pairs={{1,0},{2,1},{3,2},{4,3},{5,4},{6,5},{7,6},{8,7},{9,8},{10,9},{11,1... | collective-permute-start | bytes 786440 | tf_op jit(solution)/shard_map/ppermute | solution.py:28
  129.0 2.7 %fusion.128 = f32[64,1,512]{2,0,1:T(8,128)S(1)} fusion(bf16[2,512,2560]{2,1,0:T(8,128)(2,1)} %param.21, bf16[64,3072]{0,1:T(8,128)(2,1)S(1)} %pad_maximum_fusion.16), kind=kOutput, calls=%fused_computation.186 | convolution fusion | flops 167772160 | bytes 3407872 | tf_op jit(solution)/shard_map/dot_general | solution.py:153
  131.6 2.7 %fusion.134 = f32[64,1,512]{2,0,1:T(8,128)S(1)} fusion(bf16[2,512,2560]{2,1,0:T(8,128)(2,1)} %param.21, bf16[64,3072]{0,1:T(8,128)(2,1)S(1)} %pad_maximum_fusion.16), kind=kOutput, calls=%fused_computation.188 | convolution fusion | flops 167772160 | bytes 3407872 | tf_op jit(solution)/shard_map/dot_general | solution.py:153
  134.3 3.0 %reshape.198 = bf16[64,64,64]{2,1,0:T(8,128)(2,1)} reshape(bf16[64,2,2048]{2,1,0:T(2,128)(2,1)} %all-to-all-done) | data formatting | bytes 1048576
  137.3 2.9 %copy.43 = bf16[64,64,64]{2,1,0:T(8,128)(2,1)} copy(bf16[64,64,64]{2,0,1:T(8,128)(2,1)} %bitcast.104) | data formatting | bytes 1048576 | tf_op jit(solution)/shard_map/transpose | solution.py:38
  140.2 2.7 %reshape.146 = bf16[64,4096]{1,0:T(8,128)(2,1)} reshape(bf16[64,64,64]{2,1,0:T(8,128)(2,1)} %copy.43) | data formatting | bytes 1048576 | tf_op jit(solution)/shard_map/reshape | solution.py:38
  145.6 4.3 %scatter_custom_fusion.1 = f32[64,1024]{0,1:T(8,128)} fusion(s32[1024]{0:T(1024)} %copy-done.16, f32[1024,64]{1,0:T(8,128)} %copy.46, f32[]{:T(128)} %constant.64.clone.1), kind=kCustom, calls=%fused_computation.209 | custom fusion | bytes 262656 | tf_op jit(solution)/shard_map/scatter | solution.py:115
  152.8 3.5 %broadcast_multiply_fusion = (f32[8,8,64,128]{3,2,1,0:T(8,128)S(1)}, f32[8,8,64,128]{3,2,1,0:T(8,128)S(1)}) fusion(f32[8,8,128]{2,1,0:T(8,128)S(1)} %get-tuple-element.38, f32[8,8,64,128]{3,2,1,0:T(8,128)} %fusion.144, f32[8,8,128]{2,1,0:T(8,128)S(1)} %get-tuple-element.45, f32[8,8,128]{2,1,0:T(8,128)S(1)} %get-tuple-element.44, ...), kind=kLoop, calls=%fused_computation.194 | loop fusion | flops 8912896 | bytes 9175040 | tf_op jit(solution)/shard_map/mul | solution.py:94
  156.4 1.9 collective-permute-start.14
  158.3 8.1 %collective-permute-start.15 = (f32[1,8,64,128]{3,2,1,0:T(8,128)S(1)}, f32[1,8,64,128]{3,2,1,0:T(8,128)S(1)}, u32[]{:S(2)}, u32[]{:S(2)}) collective-permute-start(f32[1,8,64,128]{3,2,1,0:T(8,128)S(1)} %get-tuple-element.51), channel_id=1, source_target_pairs={{1,0},{2,1},{3,2},{4,3},{5,4},{6,5},{7,6},{8,7},{9,8},{10,9},{11,1... | collective-permute-start | bytes 786440 | tf_op jit(solution)/shard_map/ppermute | solution.py:28
  166.5 2.4 collective-permute-done.14
  170.3 2.8 %multiply_add_fusion.1 = (f32[8,8,64,128]{3,2,1,0:T(8,128)S(1)}, f32[8,8,64,128]{3,2,1,0:T(8,128)S(1)}) fusion(f32[8,8,128]{2,1,0:T(8,128)S(1)} %get-tuple-element.38, f32[8,8,64,128]{3,2,1,0:T(8,128)S(1)} %get-tuple-element.31, f32[8,8,128]{2,1,0:T(8,128)S(1)} %get-tuple-element.45, f32[8,8,128]{2,1,0:T(8,128)S(1)} %get-tuple-element.44, ...), kind=kLoop, calls=%fused_computation.177 | loop fusion | flops 11010048 | bytes 9175040 | tf_op jit(solution)/shard_map/add | solution.py:101
  173.1 1.9 collective-permute-start.16
  175.1 8.6 %collective-permute-start.17 = (f32[1,8,64,128]{3,2,1,0:T(8,128)S(1)}, f32[1,8,64,128]{3,2,1,0:T(8,128)S(1)}, u32[]{:S(2)}, u32[]{:S(2)}) collective-permute-start(f32[1,8,64,128]{3,2,1,0:T(8,128)S(1)} %get-tuple-element.49), channel_id=1, source_target_pairs={{1,0},{2,1},{3,2},{4,3},{5,4},{6,5},{7,6},{8,7},{9,8},{10,9},{11,1... | collective-permute-start | bytes 786440 | tf_op jit(solution)/shard_map/ppermute | solution.py:28
  183.7 2.4 collective-permute-done.16
  187.6 2.9 %multiply_add_fusion = (f32[8,8,64,128]{3,2,1,0:T(8,128)S(1)}, f32[8,8,64,128]{3,2,1,0:T(8,128)S(1)}) fusion(f32[8,8,64,128]{3,2,1,0:T(8,128)S(1)} %get-tuple-element.28, f32[8,8,128]{2,1,0:T(8,128)S(1)} %get-tuple-element.38, f32[8,8,64,128]{3,2,1,0:T(8,128)S(1)} %get-tuple-element.29, f32[8,8,128]{2,1,0:T(8,128)S(1)} %get-tuple-element.45, ...), kind=kLoop, calls=%fused_computation.176 | loop fusion | flops 10485760 | bytes 9175040 | tf_op jit(solution)/shard_map/add | solution.py:101
  190.5 1.9 collective-permute-start.18
  192.4 8.8 %collective-permute-start.19 = (f32[1,8,64,128]{3,2,1,0:T(8,128)S(1)}, f32[1,8,64,128]{3,2,1,0:T(8,128)S(1)}, u32[]{:S(2)}, u32[]{:S(2)}) collective-permute-start(f32[1,8,64,128]{3,2,1,0:T(8,128)S(1)} %get-tuple-element.47), channel_id=1, source_target_pairs={{1,0},{2,1},{3,2},{4,3},{5,4},{6,5},{7,6},{8,7},{9,8},{10,9},{11,1... | collective-permute-start | bytes 786440 | tf_op jit(solution)/shard_map/ppermute | solution.py:28
  201.3 2.2 collective-permute-done.18
  204.9 3.5 %fusion.96 = f32[8,8,64,128]{3,2,1,0:T(8,128)S(1)} fusion(f32[8,8,64,128]{3,2,1,0:T(8,128)S(1)} %get-tuple-element.27, f32[8,8,64,128]{3,2,1,0:T(8,128)S(1)} %get-tuple-element.26, f32[1,8,64,128]{3,2,1,0:T(8,128)S(1)} %collective-permute-done.19, f32[1,8,64,128]{3,2,1,0:T(8,128)S(1)} %collective-permute-done.18, ...), kind=kLoop, calls=%fused_computation.132 | loop fusion | flops 13107200 | bytes 13369344 | tf_op jit(solution)/shard_map/add | solution.py:97
  209.9 3.2 %gather_fusion.1 = bf16[1024,64]{1,0:T(8,128)(2,1)S(1)} fusion(bf16[64,1024]{0,1:T(8,128)(2,1)S(1)} %bitcast.101, s32[1024]{0:T(1024)S(1)} %copy-done.14), kind=kCustom, calls=%fused_computation.1 | custom fusion | bytes 266240 | tf_op jit(solution)/shard_map/gather | solution.py:129
  215.1 8.6 %collective-permute-start.21 = (bf16[64,1024]{0,1:T(8,128)(2,1)S(1)}, bf16[64,1024]{0,1:T(8,128)(2,1)S(1)}, u32[]{:S(2)}, u32[]{:S(2)}) collective-permute-start(bf16[64,1024]{0,1:T(8,128)(2,1)S(1)} %bitcast.113), channel_id=1, source_target_pairs={{1,0},{2,1},{3,2},{4,3},{5,4},{6,5},{7,6},{8,7},{9,8},{10,9},{11,1... | collective-permute-start | bytes 393224 | tf_op jit(solution)/shard_map/ppermute | solution.py:28
  225.8 6.7 %all-to-all-start.1 = ((bf16[64,2,2048]{2,1,0:T(2,128)(2,1)}), bf16[64,2,2048]{2,1,0:T(2,128)(2,1)S(1)}, u32[]{:S(2)}, u32[]{:S(2)}) async-start(bf16[64,2,2048]{2,1,0:T(2,128)(2,1)} %reshape.199), calls=%async_computation.1 | async-start | bytes 1048576 | tf_op jit(solution)/shard_map/all_to_all | solution.py:43
  232.7 2.7 %fusion.131 = f32[64,1,512]{2,0,1:T(8,128)S(1)} fusion(bf16[2,512,2560]{2,1,0:T(8,128)(2,1)} %param.21, bf16[64,3072]{0,1:T(8,128)(2,1)S(1)} %pad_maximum_fusion.17), kind=kOutput, calls=%fused_computation.187 | convolution fusion | flops 167772160 | bytes 3407872 | tf_op jit(solution)/shard_map/dot_general | solution.py:153
  235.3 2.7 %fusion.137 = f32[64,1,512]{2,0,1:T(8,128)S(1)} fusion(bf16[2,512,2560]{2,1,0:T(8,128)(2,1)} %param.21, bf16[64,3072]{0,1:T(8,128)(2,1)S(1)} %pad_maximum_fusion.17), kind=kOutput, calls=%fused_computation.189 | convolution fusion | flops 167772160 | bytes 3407872 | tf_op jit(solution)/shard_map/dot_general | solution.py:153
  238.0 4.2 %all-to-all-done.1 = bf16[64,2,2048]{2,1,0:T(2,128)(2,1)S(1)} async-done(((bf16[64,2,2048]{2,1,0:T(2,128)(2,1)}), bf16[64,2,2048]{2,1,0:T(2,128)(2,1)S(1)}, u32[]{:S(2)}, u32[]{:S(2)}) %all-to-all-start.1) | async-done | bytes 524320 | tf_op jit(solution)/shard_map/all_to_all | solution.py:43
  (107 shorter events, 39.4 us)
Async XLA Ops:
  0.6 143.7 %copy-start = (bf16[2,32,512]{2,1,0:T(8,128)(2,1)S(1)}, bf16[2,32,512]{2,1,0:T(8,128)(2,1)}, u32[]{:S(2)}) copy-start(bf16[2,32,512]{2,1,0:T(8,128)(2,1)} %param.23) | copy-start | bytes 196612
  0.6 24.2 %copy-start.9 = (f32[64,1024]{1,0:T(8,128)S(1)}, f32[64,1024]{1,0:T(8,128)}, u32[]{:S(2)}) copy-start(f32[64,1024]{1,0:T(8,128)} %param.17) | copy-start | bytes 786436
  0.7 1.7 copy-start.11
  0.7 24.2 %copy-start.15 = (s32[1024]{0:T(1024)S(1)}, s32[1024]{0:T(1024)}, u32[]{:S(2)}) copy-start(s32[1024]{0:T(1024)} %param.20) | copy-start | bytes 12292
  2.3 27.6 %collective-permute-start = (bf16[1,8,128]{2,1,0:T(8,128)(2,1)S(1)}, bf16[1,8,128]{2,1,0:T(8,128)(2,1)S(1)}, u32[]{:S(2)}, u32[]{:S(2)}) collective-permute-start(bf16[1,8,128]{2,1,0:T(8,128)(2,1)S(1)} %get-tuple-element.62), channel_id=1, source_target_pairs={{0,1},{1,2},{2,3},{3,4},{4,5},{5,6},{6,7},{7,8},{8,9},{9,10},{10,1... | collective-permute-start | bytes 6152 | tf_op jit(solution)/shard_map/ppermute | solution.py:26
  6.2 23.8 %collective-permute-start.1 = (bf16[1,8,128]{2,1,0:T(8,128)(2,1)S(1)}, bf16[1,8,128]{2,1,0:T(8,128)(2,1)S(1)}, u32[]{:S(2)}, u32[]{:S(2)}) collective-permute-start(bf16[1,8,128]{2,1,0:T(8,128)(2,1)S(1)} %get-tuple-element.63), channel_id=1, source_target_pairs={{1,0},{2,1},{3,2},{4,3},{5,4},{6,5},{7,6},{8,7},{9,8},{10,9},{11,1... | collective-permute-start | bytes 6152 | tf_op jit(solution)/shard_map/ppermute | solution.py:28
  14.8 15.3 %collective-permute-start.2 = (f32[1,8,64,128]{3,2,1,0:T(8,128)}, f32[1,8,64,128]{3,2,1,0:T(8,128)S(1)}, u32[]{:S(2)}, u32[]{:S(2)}) collective-permute-start(f32[1,8,64,128]{3,2,1,0:T(8,128)} %get-tuple-element.60), channel_id=1, source_target_pairs={{0,1},{1,2},{2,3},{3,4},{4,5},{5,6},{6,7},{7,8},{8,9},{9,10},{10,1... | collective-permute-start | bytes 786440 | tf_op jit(solution)/shard_map/ppermute | solution.py:26
  16.7 13.4 %collective-permute-start.3 = (f32[1,8,64,128]{3,2,1,0:T(8,128)}, f32[1,8,64,128]{3,2,1,0:T(8,128)}, u32[]{:S(2)}, u32[]{:S(2)}) collective-permute-start(f32[1,8,64,128]{3,2,1,0:T(8,128)} %get-tuple-element.61), channel_id=1, source_target_pairs={{1,0},{2,1},{3,2},{4,3},{5,4},{6,5},{7,6},{8,7},{9,8},{10,9},{11,1... | collective-permute-start | bytes 786440 | tf_op jit(solution)/shard_map/ppermute | solution.py:28
  24.9 5.0 %copy-start.16 = (s32[1024]{0:T(1024)}, s32[1024]{0:T(1024)S(1)}, u32[]{:S(2)}) copy-start(s32[1024]{0:T(1024)S(1)} %get-tuple-element.65) | copy-start | bytes 12292
  24.9 65.3 %copy-start.13 = (s32[1024]{0:T(1024)}, s32[1024]{0:T(1024)S(1)}, u32[]{:S(2)}) copy-start(s32[1024]{0:T(1024)S(1)} %get-tuple-element.64) | copy-start | bytes 12292
  28.5 1.5 copy-start.12
  28.5 2.4 copy-start.5
  34.4 18.3 %copy-start.3 = (f32[8,8,64,128]{3,2,1,0:T(8,128)}, f32[8,8,64,128]{3,2,1,0:T(8,128)S(1)}, u32[]{:S(2)}) copy-start(f32[8,8,64,128]{3,2,1,0:T(8,128)S(1)} %get-tuple-element.37) | copy-start | bytes 6291460
  34.5 13.3 %collective-permute-start.4 = (f32[1,8,64,128]{3,2,1,0:T(8,128)S(1)}, f32[1,8,64,128]{3,2,1,0:T(8,128)S(1)}, u32[]{:S(2)}, u32[]{:S(2)}) collective-permute-start(f32[1,8,64,128]{3,2,1,0:T(8,128)S(1)} %get-tuple-element.58), channel_id=1, source_target_pairs={{0,1},{1,2},{2,3},{3,4},{4,5},{5,6},{6,7},{7,8},{8,9},{9,10},{10,1... | collective-permute-start | bytes 786440 | tf_op jit(solution)/shard_map/ppermute | solution.py:26
  36.4 12.6 %collective-permute-start.5 = (f32[1,8,64,128]{3,2,1,0:T(8,128)S(1)}, f32[1,8,64,128]{3,2,1,0:T(8,128)S(1)}, u32[]{:S(2)}, u32[]{:S(2)}) collective-permute-start(f32[1,8,64,128]{3,2,1,0:T(8,128)S(1)} %get-tuple-element.59), channel_id=1, source_target_pairs={{1,0},{2,1},{3,2},{4,3},{5,4},{6,5},{7,6},{8,7},{9,8},{10,9},{11,1... | collective-permute-start | bytes 786440 | tf_op jit(solution)/shard_map/ppermute | solution.py:28
  49.0 15.1 %copy-start.17 = (s32[2,128]{1,0:T(2,128)S(1)}, s32[2,128]{1,0:T(2,128)}, u32[]{:S(2)}) copy-start(s32[2,128]{1,0:T(2,128)} %param.25) | copy-start | bytes 3076
  52.7 19.1 %copy-start.1 = (f32[8,8,64,128]{3,2,1,0:T(8,128)}, f32[8,8,64,128]{3,2,1,0:T(8,128)S(1)}, u32[]{:S(2)}) copy-start(f32[8,8,64,128]{3,2,1,0:T(8,128)S(1)} %get-tuple-element.34) | copy-start | bytes 6291460
  53.6 13.2 %collective-permute-start.6 = (f32[1,8,64,128]{3,2,1,0:T(8,128)}, f32[1,8,64,128]{3,2,1,0:T(8,128)S(1)}, u32[]{:S(2)}, u32[]{:S(2)}) collective-permute-start(f32[1,8,64,128]{3,2,1,0:T(8,128)} %get-tuple-element.56), channel_id=1, source_target_pairs={{0,1},{1,2},{2,3},{3,4},{4,5},{5,6},{6,7},{7,8},{8,9},{9,10},{10,1... | collective-permute-start | bytes 786440 | tf_op jit(solution)/shard_map/ppermute | solution.py:26
  55.5 12.5 %collective-permute-start.7 = (f32[1,8,64,128]{3,2,1,0:T(8,128)S(1)}, f32[1,8,64,128]{3,2,1,0:T(8,128)S(1)}, u32[]{:S(2)}, u32[]{:S(2)}) collective-permute-start(f32[1,8,64,128]{3,2,1,0:T(8,128)S(1)} %get-tuple-element.57), channel_id=1, source_target_pairs={{1,0},{2,1},{3,2},{4,3},{5,4},{6,5},{7,6},{8,7},{9,8},{10,9},{11,1... | collective-permute-start | bytes 786440 | tf_op jit(solution)/shard_map/ppermute | solution.py:28
  68.0 14.6 %copy-start.8 = (bf16[2,32,4096]{2,1,0:T(8,128)(2,1)S(1)}, bf16[2,32,4096]{2,1,0:T(8,128)(2,1)}, u32[]{:S(2)}) copy-start(bf16[2,32,4096]{2,1,0:T(8,128)(2,1)} %param.24) | copy-start | bytes 1572868
  68.0 18.4 %copy-start.4 = (f32[8,8,64,128]{3,2,1,0:T(8,128)S(1)}, f32[8,8,64,128]{3,2,1,0:T(8,128)}, u32[]{:S(2)}) copy-start(f32[8,8,64,128]{3,2,1,0:T(8,128)} %copy-done.3) | copy-start | bytes 6291460
  68.0 18.4 %copy-start.6 = (f32[8,8,64,128]{3,2,1,0:T(8,128)S(1)}, f32[8,8,64,128]{3,2,1,0:T(8,128)}, u32[]{:S(2)}) copy-start(f32[8,8,64,128]{3,2,1,0:T(8,128)} %param.15) | copy-start | bytes 6291460
  71.8 14.6 %copy-start.2 = (f32[8,8,64,128]{3,2,1,0:T(8,128)S(1)}, f32[8,8,64,128]{3,2,1,0:T(8,128)}, u32[]{:S(2)}) copy-start(f32[8,8,64,128]{3,2,1,0:T(8,128)} %copy-done.1) | copy-start | bytes 6291460
  71.8 13.1 %collective-permute-start.8 = (f32[1,8,64,128]{3,2,1,0:T(8,128)S(1)}, f32[1,8,64,128]{3,2,1,0:T(8,128)S(1)}, u32[]{:S(2)}, u32[]{:S(2)}) collective-permute-start(f32[1,8,64,128]{3,2,1,0:T(8,128)S(1)} %get-tuple-element.54), channel_id=1, source_target_pairs={{0,1},{1,2},{2,3},{3,4},{4,5},{5,6},{6,7},{7,8},{8,9},{9,10},{10,1... | collective-permute-start | bytes 786440 | tf_op jit(solution)/shard_map/ppermute | solution.py:26
  73.9 12.5 %collective-permute-start.9 = (f32[1,8,64,128]{3,2,1,0:T(8,128)S(1)}, f32[1,8,64,128]{3,2,1,0:T(8,128)S(1)}, u32[]{:S(2)}, u32[]{:S(2)}) collective-permute-start(f32[1,8,64,128]{3,2,1,0:T(8,128)S(1)} %get-tuple-element.55), channel_id=1, source_target_pairs={{1,0},{2,1},{3,2},{4,3},{5,4},{6,5},{7,6},{8,7},{9,8},{10,9},{11,1... | collective-permute-start | bytes 786440 | tf_op jit(solution)/shard_map/ppermute | solution.py:28
  86.4 17.5 %copy-start.10 = (bf16[2,32,512]{2,1,0:T(8,128)(2,1)S(1)}, bf16[2,32,512]{2,1,0:T(8,128)(2,1)}, u32[]{:S(2)}) copy-start(bf16[2,32,512]{2,1,0:T(8,128)(2,1)} %param.22) | copy-start | bytes 196612
  93.4 34.4 %collective-permute-start.10 = (bf16[64,1024]{0,1:T(8,128)(2,1)S(1)}, bf16[64,1024]{0,1:T(8,128)(2,1)S(1)}, u32[]{:S(2)}, u32[]{:S(2)}) collective-permute-start(bf16[64,1024]{0,1:T(8,128)(2,1)S(1)} %bitcast.108), channel_id=1, source_target_pairs={{0,1},{1,2},{2,3},{3,4},{4,5},{5,6},{6,7},{7,8},{8,9},{9,10},{10,1... | collective-permute-start | bytes 393224 | tf_op jit(solution)/shard_map/ppermute | solution.py:26
  95.3 32.5 %collective-permute-start.11 = (bf16[64,1024]{0,1:T(8,128)(2,1)S(1)}, bf16[64,1024]{0,1:T(8,128)(2,1)}, u32[]{:S(2)}, u32[]{:S(2)}) collective-permute-start(bf16[64,1024]{0,1:T(8,128)(2,1)S(1)} %bitcast.109), channel_id=1, source_target_pairs={{1,0},{2,1},{3,2},{4,3},{5,4},{6,5},{7,6},{8,7},{9,8},{10,9},{11,1... | collective-permute-start | bytes 393224 | tf_op jit(solution)/shard_map/ppermute | solution.py:28
  109.8 24.5 %all-to-all-start = ((bf16[64,2,2048]{2,1,0:T(2,128)(2,1)}), bf16[64,2,2048]{2,1,0:T(2,128)(2,1)}, u32[]{:S(2)}, u32[]{:S(2)}) async-start(bf16[64,2,2048]{2,1,0:T(2,128)(2,1)} %reshape.197), calls=%async_computation | async-start | bytes 1048576 | tf_op jit(solution)/shard_map/all_to_all | solution.py:43
  117.6 35.2 %collective-permute-start.12 = (f32[1,8,64,128]{3,2,1,0:T(8,128)}, f32[1,8,64,128]{3,2,1,0:T(8,128)}, u32[]{:S(2)}, u32[]{:S(2)}) collective-permute-start(f32[1,8,64,128]{3,2,1,0:T(8,128)} %get-tuple-element.52), channel_id=1, source_target_pairs={{0,1},{1,2},{2,3},{3,4},{4,5},{5,6},{6,7},{7,8},{8,9},{9,10},{10,1... | collective-permute-start | bytes 786440 | tf_op jit(solution)/shard_map/ppermute | solution.py:26
  121.0 31.9 %collective-permute-start.13 = (f32[1,8,64,128]{3,2,1,0:T(8,128)}, f32[1,8,64,128]{3,2,1,0:T(8,128)}, u32[]{:S(2)}, u32[]{:S(2)}) collective-permute-start(f32[1,8,64,128]{3,2,1,0:T(8,128)} %get-tuple-element.53), channel_id=1, source_target_pairs={{1,0},{2,1},{3,2},{4,3},{5,4},{6,5},{7,6},{8,7},{9,8},{10,9},{11,1... | collective-permute-start | bytes 786440 | tf_op jit(solution)/shard_map/ppermute | solution.py:28
  156.4 12.5 %collective-permute-start.14 = (f32[1,8,64,128]{3,2,1,0:T(8,128)S(1)}, f32[1,8,64,128]{3,2,1,0:T(8,128)S(1)}, u32[]{:S(2)}, u32[]{:S(2)}) collective-permute-start(f32[1,8,64,128]{3,2,1,0:T(8,128)S(1)} %get-tuple-element.50), channel_id=1, source_target_pairs={{0,1},{1,2},{2,3},{3,4},{4,5},{5,6},{6,7},{7,8},{8,9},{9,10},{10,1... | collective-permute-start | bytes 786440 | tf_op jit(solution)/shard_map/ppermute | solution.py:26
  158.3 12.0 %collective-permute-start.15 = (f32[1,8,64,128]{3,2,1,0:T(8,128)S(1)}, f32[1,8,64,128]{3,2,1,0:T(8,128)S(1)}, u32[]{:S(2)}, u32[]{:S(2)}) collective-permute-start(f32[1,8,64,128]{3,2,1,0:T(8,128)S(1)} %get-tuple-element.51), channel_id=1, source_target_pairs={{1,0},{2,1},{3,2},{4,3},{5,4},{6,5},{7,6},{8,7},{9,8},{10,9},{11,1... | collective-permute-start | bytes 786440 | tf_op jit(solution)/shard_map/ppermute | solution.py:28
  173.1 13.0 %collective-permute-start.16 = (f32[1,8,64,128]{3,2,1,0:T(8,128)S(1)}, f32[1,8,64,128]{3,2,1,0:T(8,128)S(1)}, u32[]{:S(2)}, u32[]{:S(2)}) collective-permute-start(f32[1,8,64,128]{3,2,1,0:T(8,128)S(1)} %get-tuple-element.48), channel_id=1, source_target_pairs={{0,1},{1,2},{2,3},{3,4},{4,5},{5,6},{6,7},{7,8},{8,9},{9,10},{10,1... | collective-permute-start | bytes 786440 | tf_op jit(solution)/shard_map/ppermute | solution.py:26
  175.1 12.5 %collective-permute-start.17 = (f32[1,8,64,128]{3,2,1,0:T(8,128)S(1)}, f32[1,8,64,128]{3,2,1,0:T(8,128)S(1)}, u32[]{:S(2)}, u32[]{:S(2)}) collective-permute-start(f32[1,8,64,128]{3,2,1,0:T(8,128)S(1)} %get-tuple-element.49), channel_id=1, source_target_pairs={{1,0},{2,1},{3,2},{4,3},{5,4},{6,5},{7,6},{8,7},{9,8},{10,9},{11,1... | collective-permute-start | bytes 786440 | tf_op jit(solution)/shard_map/ppermute | solution.py:28
  190.5 13.0 %collective-permute-start.18 = (f32[1,8,64,128]{3,2,1,0:T(8,128)S(1)}, f32[1,8,64,128]{3,2,1,0:T(8,128)S(1)}, u32[]{:S(2)}, u32[]{:S(2)}) collective-permute-start(f32[1,8,64,128]{3,2,1,0:T(8,128)S(1)} %get-tuple-element.46), channel_id=1, source_target_pairs={{0,1},{1,2},{2,3},{3,4},{4,5},{5,6},{6,7},{7,8},{8,9},{9,10},{10,1... | collective-permute-start | bytes 786440 | tf_op jit(solution)/shard_map/ppermute | solution.py:26
  192.4 12.5 %collective-permute-start.19 = (f32[1,8,64,128]{3,2,1,0:T(8,128)S(1)}, f32[1,8,64,128]{3,2,1,0:T(8,128)S(1)}, u32[]{:S(2)}, u32[]{:S(2)}) collective-permute-start(f32[1,8,64,128]{3,2,1,0:T(8,128)S(1)} %get-tuple-element.47), channel_id=1, source_target_pairs={{1,0},{2,1},{3,2},{4,3},{5,4},{6,5},{7,6},{8,7},{9,8},{10,9},{11,1... | collective-permute-start | bytes 786440 | tf_op jit(solution)/shard_map/ppermute | solution.py:28
  204.9 5.0 %copy-start.14 = (s32[1024]{0:T(1024)S(1)}, s32[1024]{0:T(1024)}, u32[]{:S(2)}) copy-start(s32[1024]{0:T(1024)} %copy-done.13) | copy-start | bytes 12292
  208.4 1.3 copy-start.7
  213.1 19.4 %collective-permute-start.20 = (bf16[64,1024]{0,1:T(8,128)(2,1)S(1)}, bf16[64,1024]{0,1:T(8,128)(2,1)S(1)}, u32[]{:S(2)}, u32[]{:S(2)}) collective-permute-start(bf16[64,1024]{0,1:T(8,128)(2,1)S(1)} %bitcast.112), channel_id=1, source_target_pairs={{0,1},{1,2},{2,3},{3,4},{4,5},{5,6},{6,7},{7,8},{8,9},{9,10},{10,1... | collective-permute-start | bytes 393224 | tf_op jit(solution)/shard_map/ppermute | solution.py:26
  215.1 17.4 %collective-permute-start.21 = (bf16[64,1024]{0,1:T(8,128)(2,1)S(1)}, bf16[64,1024]{0,1:T(8,128)(2,1)S(1)}, u32[]{:S(2)}, u32[]{:S(2)}) collective-permute-start(bf16[64,1024]{0,1:T(8,128)(2,1)S(1)} %bitcast.113), channel_id=1, source_target_pairs={{1,0},{2,1},{3,2},{4,3},{5,4},{6,5},{7,6},{8,7},{9,8},{10,9},{11,1... | collective-permute-start | bytes 393224 | tf_op jit(solution)/shard_map/ppermute | solution.py:28
  225.8 16.5 %all-to-all-start.1 = ((bf16[64,2,2048]{2,1,0:T(2,128)(2,1)}), bf16[64,2,2048]{2,1,0:T(2,128)(2,1)S(1)}, u32[]{:S(2)}, u32[]{:S(2)}) async-start(bf16[64,2,2048]{2,1,0:T(2,128)(2,1)} %reshape.199), calls=%async_computation.1 | async-start | bytes 1048576 | tf_op jit(solution)/shard_map/all_to_all | solution.py:43
where the time goes:
time: 249 us; the launch traced here: 246 us
  starting transfers between devices  128 us (51%)
  local copies, waits for them, and re-layouts  44.6 us (18%)
  other arithmetic  30.4 us (12%)
  waiting for transfers between devices  27.5 us (11%)
  matrix products  13.7 us (6%)
    ppermute x11, starting transfers between devices, padded_2(): lax.ppermute(head, axis, [((i + 1) % count, i) for i in range(ends)])  89.9 us
    ppermute x11, starting transfers between devices, padded_2(): lax.ppermute(tail, axis, [(i, (i + 1) % count) for i in range(ends)])  24.6 us
    ppermute x11, waiting for transfers between devices, padded_2(): lax.ppermute(tail, axis, [(i, (i + 1) % count) for i in range(ends)])  15 us
    all_to_all x2, starting transfers between devices, copy_for_each(): return lax.all_to_all(copies, axis, split_axis=0, concat_axis=0, tiled=True)  13.6 us
    unnamed x43, local copies, waits for them, and re-layouts  13.5 us
    add x4, other arithmetic, chebyshev(): rho_next * rho_now * update  13.2 us
    dot_general x4, matrix products, finish(): lax.dot_general(window, near_tiles[slot], (((1,), (1,)), ((), ())), prefe...  10.7 us
    ppermute x11, waiting for transfers between devices, padded_2(): lax.ppermute(head, axis, [((i + 1) % count, i) for i in range(ends)])  8.31 us
  transfers between devices with their start and end apart: 24, of which 13 were waited for; matrix products, arithmetic and copies ran while one was open for 19% of the time, Pallas kernels for 0%

commit v1 on v0

v1 whole, which is shorter than its diff:
```python
import jax
import jax.numpy as jnp
from jax import lax
from jax.experimental import pallas as pl
from jax.experimental.pallas import tpu as pltpu
from jax.sharding import PartitionSpec as P

CLUSTER = 512
RANK = 32
NDEV = 64
XL = 8
NY = 8
COLS = 64
NZ = 128
SROW = XL * NZ
EXT = XL + 6

f32 = jnp.float32
bf16 = jnp.bfloat16

WEST, EAST, SOUTH, NORTH, LOWER, UPPER = range(6)
NT = (((1,), (1,)), ((), ()))
NN = (((1,), (0,)), ((), ()))


def chebyshev_factors():
    delta = 0.95
    rho = delta
    factors = []
    for _ in range(3):
        following = 1.0 / (2.0 / delta - rho)
        factors.append((following * rho, 2.0 * following / delta))
        rho = following
    return factors


SWAP_A = [(i, i ^ 1) for i in range(NDEV)]
SWAP_B = [(i, i + 1) for i in range(1, NDEV - 1, 2)] + [(i + 1, i) for i in range(1, NDEV - 1, 2)]


def swap(a, b):
    return lax.ppermute(a, "dev", SWAP_A), lax.ppermute(b, "dev", SWAP_B)


def dot(a, b, dims):
    return lax.dot_general(a, b, dims, preferred_element_type=f32)


def faces(c, west, east, reaction):
    iy = lax.broadcasted_iota(jnp.int32, (NY, NZ), 0)
    iz = lax.broadcasted_iota(jnp.int32, (NY, NZ), 1)
    south = jnp.where(iy == 0, 0.0, pltpu.roll(c, 1, 0))
    north = pltpu.roll(c, NY - 1, 0)
    lower = jnp.where(iz == 0, 0.0, pltpu.roll(c, 1, 1))
    upper = jnp.where(iz == NZ - 1, 0.0, pltpu.roll(c, NZ - 1, 1))
    fw = 0.5 * (c + west)
    fe = 0.5 * (c + east)
    fs = 0.5 * (c + south)
    fn = jnp.where(iy == NY - 1, 0.0, 0.5 * (c + north))
    fl = 0.5 * (c + lower)
    fu = 0.5 * (c + upper)
    rest = fs + fn + fl + fu + reaction
    fl = jnp.where(iz == 0, 0.0, fl)
    fu = jnp.where(iz == NZ - 1, 0.0, fu)
    return (fw, fe, fs, fn, fl, fu), rest


def row(coef, kind, e, y):
    return coef[kind, e, y : y + 1, :]


def neighbours(values, west, here, east, coef, e, y):
    v = values[here, y]
    acc = row(coef, WEST, e, y) * values[west, y] + row(coef, EAST, e, y) * values[east, y]
    acc = acc + row(coef, LOWER, e, y) * pltpu.roll(v, 1, 1)
    acc = acc + row(coef, UPPER, e, y) * pltpu.roll(v, NZ - 1, 1)
    if y > 0:
        acc = acc + row(coef, SOUTH, e, y) * values[here, y - 1]
    if y < NY - 1:
        acc = acc + row(coef, NORTH, e, y) * values[here, y + 1]
    return v, acc


def build_onehot(order, onehot):
    wanted = order[...]
    for x in range(XL):
        cell = lax.broadcasted_iota(jnp.int32, (NZ, SROW), 0) + x * NZ
        onehot[x * NZ : (x + 1) * NZ, :] = jnp.where(cell == wanted, 1.0, 0.0).astype(bf16)


def place(traction, onehot):
    high = traction.astype(bf16)
    low = (traction - high.astype(f32)).astype(bf16)
    both = dot(jnp.concatenate([high, low], axis=0), onehot[...], NT)
    return both[:COLS] + both[COLS:]


def residual(values, forcing, cond, reac, raw, out, placed):
    for x in range(XL):
        c = cond[x]
        zero = jnp.zeros_like(c)
        west = cond[x - 1] if x > 0 else zero
        east = cond[x + 1] if x < XL - 1 else zero
        sides, rest = faces(c, west, east, reac[x])
        sides = list(sides)
        if x == 0:
            sides[WEST] = zero
        if x == XL - 1:
            sides[EAST] = zero
        for kind in range(6):
            raw[kind, x] = sides[kind]
        raw[6, x] = rest + sides[WEST] + sides[EAST]

    def layer(x, carry):
        west = jnp.maximum(x - 1, 0)
        east = jnp.minimum(x + 1, XL - 1)
        for y in range(NY):
            v, acc = neighbours(values, west, x, east, raw, x, y)
            res = forcing[x, y] + acc - row(raw, 6, x, y) * v
            if placed is not None and y == NY - 1:
                res = res + placed[x]
            out[x, y] = res
        return carry

    lax.fori_loop(0, XL, layer, 0)


def pack(odd, values, res, cond, reac, send_a, send_b, with_coef):
    for send, toward_right in ((send_a, odd == 0), (send_b, odd != 0)):

        def source(h):
            return jnp.where(toward_right, XL - h, h - 1)

        def copy(y, carry):
            send[y] = values[source(1), y].astype(bf16)
            for h in (1, 2, 3):
                send[h * NY + y] = res[source(h), y].astype(bf16)
            return carry

        lax.fori_loop(0, NY, copy, 0)
        if with_coef:
            rows = [cond[source(h)] for h in (1, 2, 3, 4)] + [reac[source(h)] for h in (1, 2, 3)]
            rows.append(jnp.zeros_like(rows[0]))
            send[4 * NY] = jnp.concatenate(rows, axis=0).astype(bf16)


def first_kernel(
    scal, values, forcing, traction, order, cond, reac, res, send_a, send_b, raw, onehot, placed
):
    build_onehot(order, onehot)
    cells = place(traction[...], onehot)
    for x in range(XL):
        placed[x] = cells[:, x * NZ : (x + 1) * NZ]
    residual(values, forcing, cond, reac, raw, res, placed)
    pack(scal[0], values, res, cond, reac, send_a, send_b, True)


def second_kernel(scal, values, forcing, cond, reac, res, send_a, send_b, raw):
    residual(values, forcing, cond, reac, raw, res, None)
    pack(scal[0], values, res, cond, reac, send_a, send_b, False)


def sides_of(odd, recv_a, recv_b):
    return ((recv_a, odd == 0), (recv_b, odd != 0))


def coefficients(scal, recv_a, recv_b, cond, reac, cond_ext, reac_ext, coef, inv):
    odd = scal[0]
    for x in range(XL):
        cond_ext[x + 4] = cond[x]
        reac_ext[x + 3] = reac[x]
    for recv, right in sides_of(odd, recv_a, recv_b):
        rows = recv[4 * NY].astype(f32)
        for h in (1, 2, 3, 4):
            cond_ext[jnp.where(right, 11 + h, 4 - h)] = rows[(h - 1) * NY : h * NY]
        for h in (1, 2, 3):
            reac_ext[jnp.where(right, 10 + h, 3 - h)] = rows[(h + 3) * NY : (h + 4) * NY]
    for e in range(EXT):
        sides, rest = faces(cond_ext[e + 1], cond_ext[e], cond_ext[e + 2], reac_ext[e])
        diagonal = rest + sides[WEST] + sides[EAST]
        scale = 1.0 / jnp.where(diagonal > 0.0, diagonal, 1.0)
        if e < 3:
            scale = jnp.where(scal[1] > 0, scale, 0.0)
        if e >= XL + 3:
            scale = jnp.where(scal[2] > 0, scale, 0.0)
        for kind in range(6):
            coef[kind, e] = sides[kind] * scale
        inv[e] = scale


def start_of_sweeps(odd, values, res, recv_a, recv_b, coef, inv, first, placed, tract_a, tract_b):
    def own(x, carry):
        for y in range(NY):
            r = res[x, y]
            if placed is not None and y == NY - 1:
                r = r + placed[x]
            first[x + 3, y] = r * inv[x + 3, y : y + 1, :]
        return carry

    lax.fori_loop(0, XL, own, 0)
    for (recv, right), tract in zip(sides_of(odd, recv_a, recv_b), (tract_a, tract_b)):
        edge = jnp.where(right, XL - 1, 0)
        toward = jnp.where(right, EAST, WEST)
        back = jnp.where(right, WEST, EAST)

        def halo(h):
            return jnp.where(right, XL + 2 + h, 3 - h)

        for y in range(NY):
            gap = recv[y].astype(f32) - values[edge, y]
            e = edge + 3
            first[e, y] = first[e, y] + row(coef, toward, e, y) * gap
            for h in (1, 2, 3):
                e = halo(h)
                r = recv[h * NY + y].astype(f32)
                if tract is not None and y == NY - 1:
                    r = r + tract[h - 1].astype(f32)
                s = r * inv[e, y : y + 1, :]
                if h == 1:
                    s = s - row(coef, back, e, y) * gap
                first[e, y] = s


def sweeps(values, coef, first, second, third, out):
    (a1, b1), (a2, b2), (a3, b3) = chebyshev_factors()

    def step_2(e, carry):
        for y in range(NY):
            v, acc = neighbours(first, e - 1, e, e + 1, coef, e, y)
            second[e, y] = (1.0 + a1) * v + b1 * acc
        return carry

    def step_3(e, carry):
        for y in range(NY):
            v, acc = neighbours(second, e - 1, e, e + 1, coef, e, y)
            third[e, y] = (1.0 + a2 - b2) * v + (b2 - a2) * first[e, y] + b2 * acc
        return carry

    def step_4(e, carry):
        for y in range(NY):
            v, acc = neighbours(third, e - 1, e, e + 1, coef, e, y)
            d = (1.0 + a3 - b3) * v - a3 * second[e, y] + b3 * (first[e, y] + acc)
            out[e - 3, y] = values[e - 3, y] + d
        return carry

    lax.fori_loop(1, EXT - 1, step_2, 0)
    lax.fori_loop(2, EXT - 2, step_3, 0)
    lax.fori_loop(3, EXT - 3, step_4, 0)


def surface(out, order, col_basis, onehot, traces, spread):
    build_onehot(order, onehot)
    top = jnp.concatenate([out[x, NY - 1] for x in range(XL)], axis=1).astype(bf16)
    tr = dot(top, onehot[...], NN).astype(bf16)
    traces[...] = tr
    parts = [
        dot(col_basis[c], tr[:, c * CLUSTER : (c + 1) * CLUSTER], NT) for c in range(2)
    ]
    packed = jnp.concatenate(parts, axis=1).astype(bf16)

    def copy(i, carry):
        spread[i] = packed
        return carry

    lax.fori_loop(0, NDEV, copy, 0)


def sweep_1_kernel(
    scal, values, res, recv_a, recv_b, cond, reac, order, col_basis,
    out, traces, spread, coef, inv,
    cond_ext, reac_ext, first, second, third, onehot,
):
    coefficients(scal, recv_a, recv_b, cond, reac, cond_ext, reac_ext, coef, inv)
    start_of_sweeps(scal[0], values, res, recv_a, recv_b, coef, inv, first, None, None, None)
    sweeps(values, coef, first, second, third, out)
    surface(out, order, col_basis, onehot, traces, spread)


def sweep_2_kernel(
    scal, values, res, recv_a, recv_b, placed, tract_a, tract_b, order, col_basis, coef, inv,
    out, traces, spread,
    first, second, third, onehot,
):
    start_of_sweeps(
        scal[0], values, res, recv_a, recv_b, coef, inv, first, placed, tract_a, tract_b
    )
    sweeps(values, coef, first, second, third, out)
    surface(out, order, col_basis, onehot, traces, spread)


def mask_kernel(couplings, leaf, masked):
    wide = NDEV * 2 * RANK
    cluster = lax.broadcasted_iota(jnp.int32, (NDEV * 2, wide), 0)
    lane = lax.broadcasted_iota(jnp.int32, (NDEV * 2, wide), 1)
    spread = jnp.where(lane // RANK == cluster, 1.0, 0.0).astype(bf16)
    for c in range(2):
        flags = jnp.broadcast_to(leaf[c : c + 1, :].astype(f32), (16, NDEV * 2)).astype(bf16)
        weights = dot(flags, spread, NN)[0:1]
        rows = couplings[c * RANK : (c + 1) * RANK, :].astype(f32)
        masked[c * RANK : (c + 1) * RANK, :] = (rows * weights).astype(bf16)


def near_kernel(scal, traces, recv_a, recv_b, tiles, out, window):
    odd = scal[0]
    window[1] = traces[...]
    for recv, right in sides_of(odd, recv_a, recv_b):
        window[jnp.where(right, 2, 0)] = recv[...]
    half = CLUSTER
    acc = dot(window[0], tiles[0, :, : 2 * half], NT)
    acc = acc + dot(window[1], tiles[0, :, 2 * half : 4 * half], NT)
    acc = acc + dot(window[2, :, :half], tiles[0, :, 4 * half :], NT)
    out[:, :half] = acc
    acc = dot(window[0, :, half:], tiles[1, :, :half], NT)
    acc = acc + dot(window[1], tiles[1, :, half : 3 * half], NT)
    acc = acc + dot(window[2], tiles[1, :, 3 * half :], NT)
    out[:, half:] = acc


def far_part(gathered, masked, row_basis, nearby, out):
    g = gathered[...]
    turned = jnp.concatenate([g[:, :, COLS:], g[:, :, :COLS]], axis=2)
    g = jnp.concatenate([g, turned], axis=1).reshape(NDEV * 2 * RANK, NZ)
    coupled = dot(masked[...], g, NN)
    coupled = jnp.transpose(coupled)[:COLS].astype(bf16)
    for c in range(2):
        cut = slice(c * CLUSTER, (c + 1) * CLUSTER)
        part = dot(coupled[:, c * RANK : (c + 1) * RANK], row_basis[c], NN)
        out[:, cut] = nearby[:, cut] + part


def far_kernel_place(
    scal, gathered, masked, row_basis, nearby, order, placed, send_a, send_b, onehot, total
):
    far_part(gathered, masked, row_basis, nearby, total)
    build_onehot(order, onehot)
    cells = place(total[...], onehot)
    for x in range(XL):
        placed[x] = cells[:, x * NZ : (x + 1) * NZ]
    for send, right in ((send_a, scal[0] == 0), (send_b, scal[0] != 0)):
        for h in (1, 2, 3):
            send[h - 1] = placed[jnp.where(right, XL - h, h - 1)].astype(bf16)


def far_kernel_last(gathered, masked, row_basis, nearby, out):
    far_part(gathered, masked, row_basis, nearby, out)


def struct(shape, dtype):
    return jax.ShapeDtypeStruct(shape, dtype)


def call(kernel, outs, scratch, *operands, scalars=None):
    specs = [pl.BlockSpec() for _ in operands]
    if scalars is not None:
        specs = [pl.BlockSpec(memory_space=pltpu.SMEM)] + specs
        operands = (scalars,) + operands
    return pl.pallas_call(
        kernel,
        out_shape=outs,
        in_specs=specs,
        out_specs=jax.tree.map(lambda _: pl.BlockSpec(), outs),
        scratch_shapes=scratch,
        compiler_params=pltpu.CompilerParams(vmem_limit_bytes=56 << 20),
        name=kernel.__name__,
    )(*operands)


FIELD = (XL, NY, COLS, NZ)
EXT_FIELD = pltpu.VMEM((EXT, NY, COLS, NZ), f32)
ONEHOT = pltpu.VMEM((SROW, SROW), bf16)
RAW = pltpu.VMEM((7, XL, NY, NZ), f32)


def exchange_boundary(scal, traces, spread, tiles):
    near_a, near_b = swap(traces, traces)
    gathered = lax.all_to_all(spread, "dev", split_axis=0, concat_axis=0, tiled=True)
    nearby = call(
        near_kernel,
        struct((COLS, SROW), f32),
        [pltpu.VMEM((3, COLS, SROW), bf16)],
        traces, near_a, near_b, tiles,
        scalars=scal,
    )
    return gathered, nearby


def shards(
    field_start, forcing, traction_start, conductivity, reaction, surface_order,
    near_tiles, col_basis, row_basis, couplings, far_leaf,
):
    index = lax.axis_index("dev").astype(jnp.int32)
    scal = jnp.stack(
        [index % 2, (index > 0).astype(jnp.int32), (index < NDEV - 1).astype(jnp.int32)]
    )
    order = surface_order.reshape(1, SROW)
    message = struct((4 * NY + 1, COLS, NZ), bf16)
    res, send_a, send_b = call(
        first_kernel,
        (struct(FIELD, f32), message, message),
        [RAW, ONEHOT, pltpu.VMEM((XL, COLS, NZ), f32)],
        field_start, forcing, traction_start, order, conductivity, reaction,
        scalars=scal,
    )
    recv_a, recv_b = swap(send_a, send_b)
    masked = call(
        mask_kernel,
        struct((2 * RANK, NDEV * 2 * RANK), bf16),
        [],
        couplings.reshape(2 * RANK, NDEV * 2 * RANK), far_leaf,
    )
    coef_shape = struct((6, EXT, NY, NZ), f32)
    inv_shape = struct((EXT, NY, NZ), f32)
    surface_outs = (
        struct(FIELD, f32), struct((COLS, SROW), bf16), struct((NDEV, RANK, NZ), bf16),
    )
    field, traces, spread, coef, inv = call(
        sweep_1_kernel,
        surface_outs + (coef_shape, inv_shape),
        [
            pltpu.VMEM((XL + 8, NY, NZ), f32), pltpu.VMEM((EXT, NY, NZ), f32),
            EXT_FIELD, EXT_FIELD, EXT_FIELD, ONEHOT,
        ],
        field_start, res, recv_a, recv_b, conductivity, reaction, order, col_basis,
        scalars=scal,
    )
    gathered, nearby = exchange_boundary(scal, traces, spread, near_tiles)
    message = struct((4 * NY, COLS, NZ), bf16)
    res, send_a, send_b = call(
        second_kernel,
        (struct(FIELD, f32), message, message),
        [RAW],
        field, forcing, conductivity, reaction,
        scalars=scal,
    )
    recv_a, recv_b = swap(send_a, send_b)
    tract = struct((3, COLS, NZ), bf16)
    placed, send_a, send_b = call(
        far_kernel_place,
        (struct((XL, COLS, NZ), f32), tract, tract),
        [ONEHOT, pltpu.VMEM((COLS, SROW), f32)],
        gathered, masked, row_basis, nearby, order,
        scalars=scal,
    )
    tract_a, tract_b = swap(send_a, send_b)
    field, traces, spread = call(
        sweep_2_kernel,
        surface_outs,
        [EXT_FIELD, EXT_FIELD, EXT_FIELD, ONEHOT],
        field, res, recv_a, recv_b, placed, tract_a, tract_b, order, col_basis, coef, inv,
        scalars=scal,
    )
    gathered, nearby = exchange_boundary(scal, traces, spread, near_tiles)
    traction = call(
        far_kernel_last,
        struct((COLS, SROW), f32),
        [],
        gathered, masked, row_basis, nearby,
    )
    return field, traction


def solution(mesh):
    in_specs = (
        P("dev", None, "sec", None),
        P("dev", None, "sec", None),
        P("sec", "dev"),
        P("dev", None, None),
        P("dev", None, None),
        P("dev"),
        P("dev", None, None),
        P("dev", None, None),
        P("dev", None, None),
        P("dev", None, None),
        P("dev", None),
    )
    out_specs = (P("dev", None, "sec", None), P("sec", "dev"))
    return jax.shard_map(shards, mesh=mesh, in_specs=in_specs, out_specs=out_specs, check_vma=False)
```

time: 249 us -> 146 us (0.59); the launches traced: 246 us -> 146 us
  starting transfers between devices: 128 us -> 53.2 us
  Pallas kernels: 0 us -> 55.6 us
  local copies, waits for them, and re-layouts: 44.6 us -> 4.97 us
  other arithmetic: 30.4 us -> 0.56 us
  matrix products: 13.7 us -> 0 us
  waiting for transfers between devices: 27.5 us -> 30.5 us
    ppermute x22 -> x10, starting transfers between devices: 115 us -> 34.1 us  [swap(): return (lax.ppermute(a, 'dev', SWAP_A), lax.ppermute(b, 'dev', SWAP_B))]
    pallas_call x0 -> x9, Pallas kernels: none -> 55.6 us  [call(): pl.pallas_call(kernel, out_shape=outs, in_specs=specs, out_specs=jax.tree...]
    add x7 -> x0, other arithmetic: 20.2 us -> none  [the longest x4 13.2 us: chebyshev(): rho_next * rho_now * update]
    dot_general x10 -> x0, matrix products: 13.7 us -> none  [the longest x4 10.7 us: finish(): lax.dot_general(window, near_tiles[slot], (((1,), (1,)), ((), ())), prefe...]
    unnamed x43 -> x26, local copies, waits for them, and re-layouts: 13.5 us -> 4.97 us
    reshape x9 -> x0, local copies, waits for them, and re-layouts: 7.56 us -> none  [the longest x2 3.51 us: in_order(): return jnp.moveaxis(pieces, 0, dim).reshape(lengths)]
    scatter x2 -> x0, local copies, waits for them, and re-layouts: 7.47 us -> none  [volume_block(): jnp.zeros((columns, x_cells * z_cells), jnp.float32).at[:, surface_order]]
    ppermute x22 -> x10, waiting for transfers between devices: 23.3 us -> 30.5 us  [swap(): return (lax.ppermute(a, 'dev', SWAP_A), lax.ppermute(b, 'dev', SWAP_B))]
  transfers between devices with their start and end apart: 24 -> 12, of which waited for: 13 -> 6; matrix products, arithmetic and copies ran while one was open for 19% -> 0% of each run, Pallas kernels for 0% -> 15%
where the time goes in v1:
time: 146 us
  Pallas kernels  55.6 us (38%)
  starting transfers between devices  53.2 us (36%)
  waiting for transfers between devices  30.5 us (21%)
  local copies, waits for them, and re-layouts  4.97 us (3%)
    pallas_call x9, Pallas kernels, call(): pl.pallas_call(kernel, out_shape=outs, in_specs=specs, out_specs=jax.tree...  55.6 us
    ppermute x10, starting transfers between devices, swap(): return (lax.ppermute(a, 'dev', SWAP_A), lax.ppermute(b, 'dev', SWAP_B))  34.1 us
    ppermute x10, waiting for transfers between devices, swap(): return (lax.ppermute(a, 'dev', SWAP_A), lax.ppermute(b, 'dev', SWAP_B))  30.5 us
    all_to_all x2, starting transfers between devices, exchange_boundary(): lax.all_to_all(spread, 'dev', split_axis=0, concat_axis=0, tiled=True)  19.1 us
    unnamed x26, local copies, waits for them, and re-layouts  4.97 us
  transfers between devices with their start and end apart: 12, of which 6 were waited for; matrix products, arithmetic and copies ran while one was open for 0% of the time, Pallas kernels for 15%

profile of v1, /device:TPU:6, one launch (start us, length us, event | category | flops | bytes accessed | tf_op | source)
XLA Modules:
  0.0 145.6 jit_solution(12775431075269560751)
XLA Ops:
  0.6 0.6 pad_add_fusion.scal
  1.2 6.7 %first_kernel.1 = (f32[8,8,64,128]{3,2,1,0:T(8,128)}, bf16[33,64,128]{2,1,0:T(8,128)(2,1)}, bf16[33,64,128]{2,1,0:T(8,128)(2,1)}) custom-call(s32[3]{0:T(128)} %pad_add_fusion.scal, f32[8,8,64,128]{3,2,1,0:T(8,128)} %values.3, f32[8,8,64,128]{3,2,1,0:T(8,128)} %forcing.3, f32[64,1024]{1,0:T(8,128)} %traction.1, s32[1,1024]{1,0:T(1,128)} %bitcast.6, ...), custom_call_target="tpu_custom_call" | custom-call | tf_op jit(solution)/shard_map/first_kernel/pallas_call | solution.py:357
  7.9 1.9 %collective-permute-start = (bf16[33,64,128]{2,1,0:T(8,128)(2,1)}, bf16[33,64,128]{2,1,0:T(8,128)(2,1)S(1)}, u32[]{:S(2)}, u32[]{:S(2)}) collective-permute-start(bf16[33,64,128]{2,1,0:T(8,128)(2,1)} %get-tuple-element.20), channel_id=1, source_target_pairs={{0,1},{1,0},{2,3},{3,2},{4,5},{5,4},{6,7},{7,6},{8,9},{9,8},{10,11... | collective-permute-start | bytes 1622024 | tf_op jit(solution)/shard_map/ppermute | solution.py:42
  9.8 7.1 %collective-permute-start.1 = (bf16[33,64,128]{2,1,0:T(8,128)(2,1)}, bf16[33,64,128]{2,1,0:T(8,128)(2,1)S(1)}, u32[]{:S(2)}, u32[]{:S(2)}) collective-permute-start(bf16[33,64,128]{2,1,0:T(8,128)(2,1)} %get-tuple-element.21), channel_id=1, source_target_pairs={{1,2},{3,4},{5,6},{7,8},{9,10},{11,12},{13,14},{15,16},{17,18},{19... | collective-permute-start | bytes 1622024 | tf_op jit(solution)/shard_map/ppermute | solution.py:42
  16.9 5.3 %collective-permute-done.recv_a = bf16[33,64,128]{2,1,0:T(8,128)(2,1)S(1)} collective-permute-done((bf16[33,64,128]{2,1,0:T(8,128)(2,1)}, bf16[33,64,128]{2,1,0:T(8,128)(2,1)S(1)}, u32[]{:S(2)}, u32[]{:S(2)}) %collective-permute-start) | collective-permute-done | bytes 540704 | tf_op jit(solution)/shard_map/ppermute | solution.py:42
  22.3 7.6 %collective-permute-done.1.recv_b = bf16[33,64,128]{2,1,0:T(8,128)(2,1)S(1)} collective-permute-done((bf16[33,64,128]{2,1,0:T(8,128)(2,1)}, bf16[33,64,128]{2,1,0:T(8,128)(2,1)S(1)}, u32[]{:S(2)}, u32[]{:S(2)}) %collective-permute-start.1) | collective-permute-done | bytes 540704 | tf_op jit(solution)/shard_map/ppermute | solution.py:42
  29.8 0.0 copy-done.2
  29.8 0.8 copy-done.3
  30.6 12.5 %sweep_1_kernel.1 = (f32[8,8,64,128]{3,2,1,0:T(8,128)}, bf16[64,1024]{1,0:T(8,128)(2,1)}, bf16[64,32,128]{2,1,0:T(8,128)(2,1)}, f32[6,14,8,128]{3,2,1,0:T(8,128)}, f32[14,8,128]{2,1,0:T(8,128)}) custom-call(s32[3]{0:T(128)} %pad_add_fusion.scal, f32[8,8,64,128]{3,2,1,0:T(8,128)} %values.3, f32[8,8,64,128]{3,2,1,0:T(8,128)} %get-tuple-element.19.res, ...), custom_call_target="tpu_custom_call" | custom-call | tf_op jit(solution)/shard_map/sweep_1_kernel/pallas_call | solution.py:357
  43.1 9.9 %all-to-all-start = ((bf16[64,32,128]{2,1,0:T(8,128)(2,1)}), bf16[64,32,128]{2,1,0:T(8,128)(2,1)S(1)}, u32[]{:S(2)}, u32[]{:S(2)}) async-start(bf16[64,32,128]{2,1,0:T(8,128)(2,1)} %get-tuple-element.26), calls=%async_computation | async-start | bytes 1048576 | tf_op jit(solution)/shard_map/all_to_all | solution.py:376
  53.0 0.0 copy-start.6
  53.0 5.9 %second_kernel.1 = (f32[8,8,64,128]{3,2,1,0:T(8,128)}, bf16[32,64,128]{2,1,0:T(8,128)(2,1)}, bf16[32,64,128]{2,1,0:T(8,128)(2,1)}) custom-call(s32[3]{0:T(128)} %pad_add_fusion.scal, f32[8,8,64,128]{3,2,1,0:T(8,128)} %get-tuple-element.22.values, f32[8,8,64,128]{3,2,1,0:T(8,128)} %forcing.3, f32[8,8,128]{2,1,0:T(8,128)} %cond.5, f32[8,8,128]{2,1,0:T(8,128)} %reac.5), custom_call_target="tpu_custom_call" | custom-call | tf_op jit(solution)/shard_map/second_kernel/pallas_call | solution.py:357
  59.0 1.5 %collective-permute-start.2 = (bf16[32,64,128]{2,1,0:T(8,128)(2,1)}, bf16[32,64,128]{2,1,0:T(8,128)(2,1)S(1)}, u32[]{:S(2)}, u32[]{:S(2)}) collective-permute-start(bf16[32,64,128]{2,1,0:T(8,128)(2,1)} %get-tuple-element.24), channel_id=1, source_target_pairs={{0,1},{1,0},{2,3},{3,2},{4,5},{5,4},{6,7},{7,6},{8,9},{9,8},{10,11... | collective-permute-start | bytes 1572872 | tf_op jit(solution)/shard_map/ppermute | solution.py:42
  60.5 6.3 %collective-permute-start.3 = (bf16[32,64,128]{2,1,0:T(8,128)(2,1)}, bf16[32,64,128]{2,1,0:T(8,128)(2,1)S(1)}, u32[]{:S(2)}, u32[]{:S(2)}) collective-permute-start(bf16[32,64,128]{2,1,0:T(8,128)(2,1)} %get-tuple-element.25), channel_id=1, source_target_pairs={{1,2},{3,4},{5,6},{7,8},{9,10},{11,12},{13,14},{15,16},{17,18},{19... | collective-permute-start | bytes 1572872 | tf_op jit(solution)/shard_map/ppermute | solution.py:42
  66.8 0.0 copy-done.6
  66.8 3.7 %collective-permute-start.5 = (bf16[64,1024]{1,0:T(8,128)(2,1)S(1)}, bf16[64,1024]{1,0:T(8,128)(2,1)S(1)}, u32[]{:S(2)}, u32[]{:S(2)}) collective-permute-start(bf16[64,1024]{1,0:T(8,128)(2,1)S(1)} %copy-done.6), channel_id=1, source_target_pairs={{1,2},{3,4},{5,6},{7,8},{9,10},{11,12},{13,14},{15,16},{17,18},{19... | collective-permute-start | bytes 393224 | tf_op jit(solution)/shard_map/ppermute | solution.py:42
  70.5 0.1 collective-permute-start.4
  70.6 2.2 %mask_kernel.1.masked = bf16[64,4096]{1,0:T(8,128)(2,1)} custom-call(bf16[64,4096]{1,0:T(8,128)(2,1)} %bitcast.5, s32[2,128]{1,0:T(2,128)} %leaf.1), custom_call_target="tpu_custom_call" | custom-call | tf_op jit(solution)/shard_map/mask_kernel/pallas_call | solution.py:357
  72.8 8.5 %collective-permute-done.5.recv_b = bf16[64,1024]{1,0:T(8,128)(2,1)S(1)} collective-permute-done((bf16[64,1024]{1,0:T(8,128)(2,1)S(1)}, bf16[64,1024]{1,0:T(8,128)(2,1)S(1)}, u32[]{:S(2)}, u32[]{:S(2)}) %collective-permute-start.5) | collective-permute-done | bytes 131104 | tf_op jit(solution)/shard_map/ppermute | solution.py:42
  81.3 0.0 collective-permute-done.4.recv_a
  81.3 0.6 copy-done.7
  81.9 0.6 copy-done.9
  82.6 5.1 %near_kernel.2.nearby = f32[64,1024]{1,0:T(8,128)} custom-call(s32[3]{0:T(128)} %pad_add_fusion.scal, bf16[64,1024]{1,0:T(8,128)(2,1)} %get-tuple-element.27.traces, bf16[64,1024]{1,0:T(8,128)(2,1)} %copy-done.9, bf16[64,1024]{1,0:T(8,128)(2,1)} %copy-done.7, bf16[2,512,2560]{2,1,0:T(8,128)(2,1)} %tiles.3), custom_call_target="tpu_custom_call" | custom-call | tf_op jit(solution)/shard_map/near_kernel/pallas_call | solution.py:357
  87.7 0.0 all-to-all-done.gathered
  87.7 0.8 copy-done
  88.5 3.4 %far_kernel_place.1 = (f32[8,64,128]{2,1,0:T(8,128)}, bf16[3,64,128]{2,1,0:T(8,128)(2,1)}, bf16[3,64,128]{2,1,0:T(8,128)(2,1)}) custom-call(s32[3]{0:T(128)} %pad_add_fusion.scal, bf16[64,32,128]{2,1,0:T(8,128)(2,1)} %copy-done, bf16[64,4096]{1,0:T(8,128)(2,1)} %mask_kernel.1.masked, bf16[2,32,512]{2,1,0:T(8,128)(2,1)} %row_basis.3, ...), custom_call_target="tpu_custom_call" | custom-call | tf_op jit(solution)/shard_map/far_kernel_place/pallas_call | solution.py:357
  91.9 0.0 collective-permute-start.6
  91.9 6.3 %collective-permute-start.7 = (bf16[3,64,128]{2,1,0:T(8,128)(2,1)}, bf16[3,64,128]{2,1,0:T(8,128)(2,1)S(1)}, u32[]{:S(2)}, u32[]{:S(2)}) collective-permute-start(bf16[3,64,128]{2,1,0:T(8,128)(2,1)} %get-tuple-element.30), channel_id=1, source_target_pairs={{1,2},{3,4},{5,6},{7,8},{9,10},{11,12},{13,14},{15,16},{17,18},{19... | collective-permute-start | bytes 147464 | tf_op jit(solution)/shard_map/ppermute | solution.py:42
  98.2 0.0 collective-permute-done.2.recv_a
  98.2 0.0 copy-start.4
  98.2 0.0 collective-permute-done.3.recv_b
  98.2 0.0 copy-start.5
  98.3 0.0 collective-permute-done.6.tract_a
  98.3 0.0 copy-start.11
  98.3 4.0 %collective-permute-done.7.tract_b = bf16[3,64,128]{2,1,0:T(8,128)(2,1)S(1)} collective-permute-done((bf16[3,64,128]{2,1,0:T(8,128)(2,1)}, bf16[3,64,128]{2,1,0:T(8,128)(2,1)S(1)}, u32[]{:S(2)}, u32[]{:S(2)}) %collective-permute-start.7) | collective-permute-done | bytes 49184 | tf_op jit(solution)/shard_map/ppermute | solution.py:42
  102.3 0.0 copy-done.4
  102.3 0.6 copy-done.12
  102.9 12.1 %sweep_2_kernel.1 = (f32[8,8,64,128]{3,2,1,0:T(8,128)}, bf16[64,1024]{1,0:T(8,128)(2,1)}, bf16[64,32,128]{2,1,0:T(8,128)(2,1)}) custom-call(s32[3]{0:T(128)} %pad_add_fusion.scal, f32[8,8,64,128]{3,2,1,0:T(8,128)} %get-tuple-element.22.values, f32[8,8,64,128]{3,2,1,0:T(8,128)} %get-tuple-element.23.res, bf16[32,64,128]{2,1,0:T(8,128)(2,1)} %copy-done.4, ...), custom_call_target="tpu_custom_call" | custom-call | tf_op jit(solution)/shard_map/sweep_2_kernel/pallas_call | solution.py:357
  115.0 9.2 %all-to-all-start.1 = ((bf16[64,32,128]{2,1,0:T(8,128)(2,1)}), bf16[64,32,128]{2,1,0:T(8,128)(2,1)S(1)}, u32[]{:S(2)}, u32[]{:S(2)}) async-start(bf16[64,32,128]{2,1,0:T(8,128)(2,1)} %get-tuple-element.34), calls=%async_computation.1 | async-start | bytes 1048576 | tf_op jit(solution)/shard_map/all_to_all | solution.py:376
  124.2 7.0 %collective-permute-start.9 = (bf16[64,1024]{1,0:T(8,128)(2,1)}, bf16[64,1024]{1,0:T(8,128)(2,1)S(1)}, u32[]{:S(2)}, u32[]{:S(2)}) collective-permute-start(bf16[64,1024]{1,0:T(8,128)(2,1)} %get-tuple-element.35.traces), channel_id=1, source_target_pairs={{1,2},{3,4},{5,6},{7,8},{9,10},{11,12},{13,14},{15,16},{17,18},{19... | collective-permute-start | bytes 393224 | tf_op jit(solution)/shard_map/ppermute | solution.py:42
  131.2 0.1 collective-permute-start.8
  131.3 4.2 %collective-permute-done.9.recv_b = bf16[64,1024]{1,0:T(8,128)(2,1)S(1)} collective-permute-done((bf16[64,1024]{1,0:T(8,128)(2,1)}, bf16[64,1024]{1,0:T(8,128)(2,1)S(1)}, u32[]{:S(2)}, u32[]{:S(2)}) %collective-permute-start.9) | collective-permute-done | bytes 131104 | tf_op jit(solution)/shard_map/ppermute | solution.py:42
  135.5 1.0 collective-permute-done.8.recv_a
  136.4 0.7 copy-done.10
  137.1 5.1 %near_kernel.3.nearby = f32[64,1024]{1,0:T(8,128)} custom-call(s32[3]{0:T(128)} %pad_add_fusion.scal, bf16[64,1024]{1,0:T(8,128)(2,1)} %get-tuple-element.35.traces, bf16[64,1024]{1,0:T(8,128)(2,1)} %copy-done.10, bf16[64,1024]{1,0:T(8,128)(2,1)} %copy-done.8, bf16[2,512,2560]{2,1,0:T(8,128)(2,1)} %tiles.3), custom_call_target="tpu_custom_call" | custom-call | tf_op jit(solution)/shard_map/near_kernel/pallas_call | solution.py:357
  142.2 0.0 all-to-all-done.1.gathered
  142.2 0.8 copy-done.1
  143.0 2.6 %far_kernel_last.1 = f32[64,1024]{1,0:T(8,128)} custom-call(bf16[64,32,128]{2,1,0:T(8,128)(2,1)} %copy-done.1, bf16[64,4096]{1,0:T(8,128)(2,1)} %mask_kernel.1.masked, bf16[2,32,512]{2,1,0:T(8,128)(2,1)} %row_basis.3, f32[64,1024]{1,0:T(8,128)} %near_kernel.3.nearby), custom_call_target="tpu_custom_call" | custom-call | tf_op jit(solution)/shard_map/far_kernel_last/pallas_call | solution.py:357
  (12 shorter events, 0.0 us)
Async XLA Ops:
  7.9 14.4 %collective-permute-start = (bf16[33,64,128]{2,1,0:T(8,128)(2,1)}, bf16[33,64,128]{2,1,0:T(8,128)(2,1)S(1)}, u32[]{:S(2)}, u32[]{:S(2)}) collective-permute-start(bf16[33,64,128]{2,1,0:T(8,128)(2,1)} %get-tuple-element.20), channel_id=1, source_target_pairs={{0,1},{1,0},{2,3},{3,2},{4,5},{5,4},{6,7},{7,6},{8,9},{9,8},{10,11... | collective-permute-start | bytes 1622024 | tf_op jit(solution)/shard_map/ppermute | solution.py:42
  9.8 20.0 %collective-permute-start.1 = (bf16[33,64,128]{2,1,0:T(8,128)(2,1)}, bf16[33,64,128]{2,1,0:T(8,128)(2,1)S(1)}, u32[]{:S(2)}, u32[]{:S(2)}) collective-permute-start(bf16[33,64,128]{2,1,0:T(8,128)(2,1)} %get-tuple-element.21), channel_id=1, source_target_pairs={{1,2},{3,4},{5,6},{7,8},{9,10},{11,12},{13,14},{15,16},{17,18},{19... | collective-permute-start | bytes 1622024 | tf_op jit(solution)/shard_map/ppermute | solution.py:42
  22.3 7.6 %copy-start.2 = (bf16[33,64,128]{2,1,0:T(8,128)(2,1)}, bf16[33,64,128]{2,1,0:T(8,128)(2,1)S(1)}, u32[]{:S(2)}) copy-start(bf16[33,64,128]{2,1,0:T(8,128)(2,1)S(1)} %collective-permute-done.recv_a) | copy-start | bytes 1622020
  29.8 0.8 copy-start.3
  43.1 44.6 %all-to-all-start = ((bf16[64,32,128]{2,1,0:T(8,128)(2,1)}), bf16[64,32,128]{2,1,0:T(8,128)(2,1)S(1)}, u32[]{:S(2)}, u32[]{:S(2)}) async-start(bf16[64,32,128]{2,1,0:T(8,128)(2,1)} %get-tuple-element.26), calls=%async_computation | async-start | bytes 1048576 | tf_op jit(solution)/shard_map/all_to_all | solution.py:376
  53.0 13.8 %copy-start.6 = (bf16[64,1024]{1,0:T(8,128)(2,1)S(1)}, bf16[64,1024]{1,0:T(8,128)(2,1)}, u32[]{:S(2)}) copy-start(bf16[64,1024]{1,0:T(8,128)(2,1)} %get-tuple-element.27.traces) | copy-start | bytes 393220
  59.0 39.2 %collective-permute-start.2 = (bf16[32,64,128]{2,1,0:T(8,128)(2,1)}, bf16[32,64,128]{2,1,0:T(8,128)(2,1)S(1)}, u32[]{:S(2)}, u32[]{:S(2)}) collective-permute-start(bf16[32,64,128]{2,1,0:T(8,128)(2,1)} %get-tuple-element.24), channel_id=1, source_target_pairs={{0,1},{1,0},{2,3},{3,2},{4,5},{5,4},{6,7},{7,6},{8,9},{9,8},{10,11... | collective-permute-start | bytes 1572872 | tf_op jit(solution)/shard_map/ppermute | solution.py:42
  60.5 37.8 %collective-permute-start.3 = (bf16[32,64,128]{2,1,0:T(8,128)(2,1)}, bf16[32,64,128]{2,1,0:T(8,128)(2,1)S(1)}, u32[]{:S(2)}, u32[]{:S(2)}) collective-permute-start(bf16[32,64,128]{2,1,0:T(8,128)(2,1)} %get-tuple-element.25), channel_id=1, source_target_pairs={{1,2},{3,4},{5,6},{7,8},{9,10},{11,12},{13,14},{15,16},{17,18},{19... | collective-permute-start | bytes 1572872 | tf_op jit(solution)/shard_map/ppermute | solution.py:42
  66.8 14.4 %collective-permute-start.5 = (bf16[64,1024]{1,0:T(8,128)(2,1)S(1)}, bf16[64,1024]{1,0:T(8,128)(2,1)S(1)}, u32[]{:S(2)}, u32[]{:S(2)}) collective-permute-start(bf16[64,1024]{1,0:T(8,128)(2,1)S(1)} %copy-done.6), channel_id=1, source_target_pairs={{1,2},{3,4},{5,6},{7,8},{9,10},{11,12},{13,14},{15,16},{17,18},{19... | collective-permute-start | bytes 393224 | tf_op jit(solution)/shard_map/ppermute | solution.py:42
  70.5 10.7 %collective-permute-start.4 = (bf16[64,1024]{1,0:T(8,128)(2,1)S(1)}, bf16[64,1024]{1,0:T(8,128)(2,1)S(1)}, u32[]{:S(2)}, u32[]{:S(2)}) collective-permute-start(bf16[64,1024]{1,0:T(8,128)(2,1)S(1)} %copy-done.6), channel_id=1, source_target_pairs={{0,1},{1,0},{2,3},{3,2},{4,5},{5,4},{6,7},{7,6},{8,9},{9,8},{10,11... | collective-permute-start | bytes 393224 | tf_op jit(solution)/shard_map/ppermute | solution.py:42
  81.3 0.7 copy-start.7
  81.9 0.7 copy-start.9
  87.7 0.8 copy-start
  91.9 6.4 %collective-permute-start.6 = (bf16[3,64,128]{2,1,0:T(8,128)(2,1)}, bf16[3,64,128]{2,1,0:T(8,128)(2,1)S(1)}, u32[]{:S(2)}, u32[]{:S(2)}) collective-permute-start(bf16[3,64,128]{2,1,0:T(8,128)(2,1)} %get-tuple-element.29), channel_id=1, source_target_pairs={{0,1},{1,0},{2,3},{3,2},{4,5},{5,4},{6,7},{7,6},{8,9},{9,8},{10,11... | collective-permute-start | bytes 147464 | tf_op jit(solution)/shard_map/ppermute | solution.py:42
  91.9 10.4 %collective-permute-start.7 = (bf16[3,64,128]{2,1,0:T(8,128)(2,1)}, bf16[3,64,128]{2,1,0:T(8,128)(2,1)S(1)}, u32[]{:S(2)}, u32[]{:S(2)}) collective-permute-start(bf16[3,64,128]{2,1,0:T(8,128)(2,1)} %get-tuple-element.30), channel_id=1, source_target_pairs={{1,2},{3,4},{5,6},{7,8},{9,10},{11,12},{13,14},{15,16},{17,18},{19... | collective-permute-start | bytes 147464 | tf_op jit(solution)/shard_map/ppermute | solution.py:42
  98.2 4.0 %copy-start.4 = (bf16[32,64,128]{2,1,0:T(8,128)(2,1)}, bf16[32,64,128]{2,1,0:T(8,128)(2,1)S(1)}, u32[]{:S(2)}) copy-start(bf16[32,64,128]{2,1,0:T(8,128)(2,1)S(1)} %collective-permute-done.2.recv_a) | copy-start | bytes 1572868
  98.2 4.0 %copy-start.5 = (bf16[32,64,128]{2,1,0:T(8,128)(2,1)}, bf16[32,64,128]{2,1,0:T(8,128)(2,1)S(1)}, u32[]{:S(2)}) copy-start(bf16[32,64,128]{2,1,0:T(8,128)(2,1)S(1)} %collective-permute-done.3.recv_b) | copy-start | bytes 1572868
  98.3 4.0 %copy-start.11 = (bf16[3,64,128]{2,1,0:T(8,128)(2,1)}, bf16[3,64,128]{2,1,0:T(8,128)(2,1)S(1)}, u32[]{:S(2)}) copy-start(bf16[3,64,128]{2,1,0:T(8,128)(2,1)S(1)} %collective-permute-done.6.tract_a) | copy-start | bytes 147460
  102.3 0.6 copy-start.12
  115.0 27.2 %all-to-all-start.1 = ((bf16[64,32,128]{2,1,0:T(8,128)(2,1)}), bf16[64,32,128]{2,1,0:T(8,128)(2,1)S(1)}, u32[]{:S(2)}, u32[]{:S(2)}) async-start(bf16[64,32,128]{2,1,0:T(8,128)(2,1)} %get-tuple-element.34), calls=%async_computation.1 | async-start | bytes 1048576 | tf_op jit(solution)/shard_map/all_to_all | solution.py:376
  124.2 11.3 %collective-permute-start.9 = (bf16[64,1024]{1,0:T(8,128)(2,1)}, bf16[64,1024]{1,0:T(8,128)(2,1)S(1)}, u32[]{:S(2)}, u32[]{:S(2)}) collective-permute-start(bf16[64,1024]{1,0:T(8,128)(2,1)} %get-tuple-element.35.traces), channel_id=1, source_target_pairs={{1,2},{3,4},{5,6},{7,8},{9,10},{11,12},{13,14},{15,16},{17,18},{19... | collective-permute-start | bytes 393224 | tf_op jit(solution)/shard_map/ppermute | solution.py:42
  131.2 5.3 %collective-permute-start.8 = (bf16[64,1024]{1,0:T(8,128)(2,1)}, bf16[64,1024]{1,0:T(8,128)(2,1)S(1)}, u32[]{:S(2)}, u32[]{:S(2)}) collective-permute-start(bf16[64,1024]{1,0:T(8,128)(2,1)} %get-tuple-element.35.traces), channel_id=1, source_target_pairs={{0,1},{1,0},{2,3},{3,2},{4,5},{5,4},{6,7},{7,6},{8,9},{9,8},{10,11... | collective-permute-start | bytes 393224 | tf_op jit(solution)/shard_map/ppermute | solution.py:42
  135.5 1.0 copy-start.8
  136.4 0.7 copy-start.10
  142.2 0.8 copy-start.1

commit v2 on v1

v2 whole, which is shorter than its diff:
```python
import jax
import jax.numpy as jnp
from jax import lax
from jax.experimental import pallas as pl
from jax.experimental.pallas import tpu as pltpu
from jax.sharding import PartitionSpec as P


CLUSTER = 512
RANK = 32
NDEV = 64
XL = 8
NY = 8
COLS = 64
NZ = 128
SROW = XL * NZ
EXT = XL + 6

f32 = jnp.float32
bf16 = jnp.bfloat16

WEST, EAST, SOUTH, NORTH, LOWER, UPPER = range(6)
NT = (((1,), (1,)), ((), ()))
NN = (((1,), (0,)), ((), ()))


def chebyshev_factors():
    delta = 0.95
    rho = delta
    factors = []
    for _ in range(3):
        following = 1.0 / (2.0 / delta - rho)
        factors.append((following * rho, 2.0 * following / delta))
        rho = following
    return factors


SWAP_A = [(i, i ^ 1) for i in range(NDEV)]
SWAP_B = [(i, i + 1) for i in range(1, NDEV - 1, 2)] + [(i + 1, i) for i in range(1, NDEV - 1, 2)]


def swap(a, b):
    return lax.ppermute(a, "dev", SWAP_A), lax.ppermute(b, "dev", SWAP_B)


def dot(a, b, dims):
    return lax.dot_general(a, b, dims, preferred_element_type=f32)


def faces(c, west, east, reaction):
    iy = lax.broadcasted_iota(jnp.int32, (NY, NZ), 0)
    iz = lax.broadcasted_iota(jnp.int32, (NY, NZ), 1)
    south = jnp.where(iy == 0, 0.0, pltpu.roll(c, 1, 0))
    north = pltpu.roll(c, NY - 1, 0)
    lower = jnp.where(iz == 0, 0.0, pltpu.roll(c, 1, 1))
    upper = jnp.where(iz == NZ - 1, 0.0, pltpu.roll(c, NZ - 1, 1))
    fw = 0.5 * (c + west)
    fe = 0.5 * (c + east)
    fs = 0.5 * (c + south)
    fn = jnp.where(iy == NY - 1, 0.0, 0.5 * (c + north))
    fl = 0.5 * (c + lower)
    fu = 0.5 * (c + upper)
    rest = fs + fn + fl + fu + reaction
    fl = jnp.where(iz == 0, 0.0, fl)
    fu = jnp.where(iz == NZ - 1, 0.0, fu)
    return (fw, fe, fs, fn, fl, fu), rest


def row(coef, kind, e, y):
    return coef[kind, e, y : y + 1, :]


def tile(values, e, y):
    return values[e, y].reshape(COLS // 8, 8, NZ)


def put(out, e, y, value):
    out[e, y] = value.reshape(COLS, NZ)


def neighbours(values, west, here, east, coef, e, y):
    v = tile(values, here, y)
    acc = row(coef, WEST, e, y) * tile(values, west, y)
    acc = acc + row(coef, EAST, e, y) * tile(values, east, y)
    acc = acc + row(coef, LOWER, e, y) * pltpu.roll(v, 1, 2)
    acc = acc + row(coef, UPPER, e, y) * pltpu.roll(v, NZ - 1, 2)
    if y > 0:
        acc = acc + row(coef, SOUTH, e, y) * tile(values, here, y - 1)
    if y < NY - 1:
        acc = acc + row(coef, NORTH, e, y) * tile(values, here, y + 1)
    return v, acc


def build_onehot(order, onehot):
    wanted = order[...]

    def rows(x, carry):
        cell = lax.broadcasted_iota(jnp.int32, (NZ, SROW), 0) + x * NZ
        onehot[pl.ds(pl.multiple_of(x * NZ, NZ), NZ), :] = jnp.where(
            cell == wanted, 1.0, 0.0
        ).astype(bf16)
        return carry

    lax.fori_loop(0, XL, rows, 0)


def place(traction, onehot):
    high = traction.astype(bf16)
    low = (traction - high.astype(f32)).astype(bf16)
    both = dot(jnp.concatenate([high, low], axis=0), onehot[...], NT)
    return both[:COLS] + both[COLS:]


def raw_faces(cond, reac, raw):
    def layer(x, carry):
        sides, rest = faces(
            cond[x], cond[jnp.maximum(x - 1, 0)], cond[jnp.minimum(x + 1, XL - 1)], reac[x]
        )
        sides = list(sides)
        sides[WEST] = jnp.where(x == 0, 0.0, sides[WEST])
        sides[EAST] = jnp.where(x == XL - 1, 0.0, sides[EAST])
        for kind in range(6):
            raw[kind, x] = sides[kind]
        raw[6, x] = rest + sides[WEST] + sides[EAST]
        return carry

    lax.fori_loop(0, XL, layer, 0, unroll=8)


def residual_layer(x, values, forcing, raw, out, placed):
    west = jnp.maximum(x - 1, 0)
    east = jnp.minimum(x + 1, XL - 1)
    for y in range(NY):
        v, acc = neighbours(values, west, x, east, raw, x, y)
        res = tile(forcing, x, y) + acc - row(raw, 6, x, y) * v
        if placed is not None and y == NY - 1:
            res = res + placed[x].reshape(COLS // 8, 8, NZ)
        put(out, x, y, res)


def pack(odd, values, res, sends_near, sends_far, base):
    for near, far, right in zip(sends_near, sends_far, (odd == 0, odd != 0)):

        def source(h):
            return jnp.where(right, XL - h, h - 1)

        def copy(y, carry):
            near[y] = values[source(1), y].astype(bf16)
            near[NY + y] = res[source(1), y].astype(bf16)
            for h in (2, 3):
                far[base + (h - 2) * NY + y] = res[source(h), y].astype(bf16)
            return carry

        lax.fori_loop(0, NY, copy, 0, unroll=2)


def pack_coefficients(odd, cond, reac, send_a, send_b):
    for send, right in ((send_a, odd == 0), (send_b, odd != 0)):

        def source(h):
            return jnp.where(right, XL - h, h - 1)

        rows = [cond[source(h)] for h in (1, 2, 3, 4)] + [reac[source(h)] for h in (1, 2, 3)]
        rows.append(jnp.zeros_like(rows[0]))
        send[2 * NY] = jnp.concatenate(rows, axis=0).astype(bf16)


def position():
    index = lax.axis_index("dev")
    return index, lax.rem(index, 2)


def first_kernel(
    values_hbm, forcing_hbm, traction_hbm, order_hbm, cond_hbm, reac_hbm,
    values, forcing, cond, reac, res, send_a, send_b, far_a, far_b,
    order, traction, raw, onehot, placed, small_sems, sems,
):
    _, odd = position()
    small = [
        pltpu.make_async_copy(source, target, small_sems.at[i])
        for i, (source, target) in enumerate(
            ((order_hbm, order), (traction_hbm, traction), (cond_hbm, cond), (reac_hbm, reac))
        )
    ]
    for copy in small:
        copy.start()

    def layer_copies(x):
        return (
            pltpu.make_async_copy(values_hbm.at[x], values.at[x], sems.at[0, x]),
            pltpu.make_async_copy(forcing_hbm.at[x], forcing.at[x], sems.at[1, x]),
        )

    for x in range(XL):
        for copy in layer_copies(x):
            copy.start()
    small[0].wait()
    build_onehot(order, onehot)
    small[1].wait()
    cells = place(traction[...], onehot)
    for x in range(XL):
        placed[x] = cells[:, x * NZ : (x + 1) * NZ]
    small[2].wait()
    small[3].wait()
    raw_faces(cond, reac, raw)
    pack_coefficients(odd, cond, reac, send_a, send_b)
    for copy in layer_copies(0):
        copy.wait()

    def layer(x, carry):
        @pl.when(x < XL - 1)
        def _():
            for copy in layer_copies(x + 1):
                copy.wait()

        residual_layer(x, values, forcing, raw, res, placed)
        return carry

    lax.fori_loop(0, XL, layer, 0)
    pack(odd, values, res, (send_a, send_b), (far_a, far_b), 0)


def sides_of(odd, recv_a, recv_b):
    return ((recv_a, odd == 0), (recv_b, odd != 0))


def extend(odd, recv_a, recv_b, cond, reac, cond_ext, reac_ext):
    for x in range(XL):
        cond_ext[x + 4] = cond[x]
        reac_ext[x + 3] = reac[x]
    for recv, right in sides_of(odd, recv_a, recv_b):
        rows = recv[2 * NY].astype(f32)
        for h in (1, 2, 3, 4):
            cond_ext[jnp.where(right, 11 + h, 4 - h)] = rows[(h - 1) * NY : h * NY]
        for h in (1, 2, 3):
            reac_ext[jnp.where(right, 10 + h, 3 - h)] = rows[(h + 3) * NY : (h + 4) * NY]


def normalise(index, cond_ext, reac_ext, coef, inv):

    def layer(e, carry):
        sides, rest = faces(cond_ext[e + 1], cond_ext[e], cond_ext[e + 2], reac_ext[e])
        diagonal = rest + sides[WEST] + sides[EAST]
        scale = 1.0 / jnp.where(diagonal > 0.0, diagonal, 1.0)
        outside = ((index == 0) & (e < 3)) | ((index == NDEV - 1) & (e >= XL + 3))
        scale = jnp.where(outside, 0.0, scale)
        for kind in range(6):
            coef[kind, e] = sides[kind] * scale
        inv[0, e] = scale
        return carry

    lax.fori_loop(0, EXT, layer, 0, unroll=7)


def widen(value):
    return value.astype(f32).reshape(COLS // 8, 8, NZ)


def start_own(odd, values, res, recv_a, recv_b, coef, inv, first, placed):
    def own(x, carry):
        for y in range(NY):
            r = tile(res, x, y)
            if placed is not None and y == NY - 1:
                r = r + placed[x].reshape(COLS // 8, 8, NZ)
            put(first, x + 3, y, r * row(inv, 0, x + 3, y))
        return carry

    lax.fori_loop(0, XL, own, 0, unroll=2)
    for recv, right in sides_of(odd, recv_a, recv_b):
        edge = jnp.where(right, XL - 1, 0)
        toward = jnp.where(right, EAST, WEST)
        e = edge + 3
        for y in range(NY):
            gap = widen(recv[y]) - tile(values, edge, y)
            put(first, e, y, tile(first, e, y) + row(coef, toward, e, y) * gap)


def start_halo(h, odd, values, recvs, far, coef, inv, first, tracts):
    messages, base = far
    for side, right in enumerate((odd == 0, odd != 0)):
        edge = jnp.where(right, XL - 1, 0)
        back = jnp.where(right, WEST, EAST)
        e = jnp.where(right, XL + 2 + h, 3 - h)
        for y in range(NY):
            if h == 1:
                r = widen(recvs[side][NY + y])
            else:
                r = widen(messages[side][base + (h - 2) * NY + y])
            if tracts is not None and y == NY - 1:
                r = r + widen(tracts[side][h - 1])
            s = r * row(inv, 0, e, y)
            if h == 1:
                gap = widen(recvs[side][y]) - tile(values, edge, y)
                s = s - row(coef, back, e, y) * gap
            put(first, e, y, s)


def sweeps(known, values, coef, first, second, third, out):
    (a1, b1), (a2, b2), (a3, b3) = chebyshev_factors()

    def step_2(e):
        for y in range(NY):
            v, acc = neighbours(first, e - 1, e, e + 1, coef, e, y)
            put(second, e, y, ((1.0 + a1) / b1) * v + acc)

    def step_3(e):
        for y in range(NY):
            v, acc = neighbours(second, e - 1, e, e + 1, coef, e, y)
            s = tile(first, e, y)
            put(third, e, y, ((1.0 + a2 - b2) / b2) * v + ((b2 - a2) / (b1 * b2)) * s + acc)

    def step_4(e):
        for y in range(NY):
            v, acc = neighbours(third, e - 1, e, e + 1, coef, e, y)
            d = ((1.0 + a3 - b3) / b3) * v - (a3 / (b2 * b3)) * tile(second, e, y) + acc
            d = (b1 * b2 * b3) * d + b3 * tile(first, e, y)
            put(out, e - 3, y, tile(values, e - 3, y) + d)

    for level, step in ((1, step_2), (2, step_3), (3, step_4)):
        low, high = 3 + level - known[0], XL + 3 - level + known[0]

        if known[1]:
            left = low - level

            def later(i, carry):
                step(jnp.where(i < left, level + i, high + i - left))
                return carry

            lax.fori_loop(0, 2 * left, later, 0, unroll=2)
        else:

            def now(e, carry):
                step(e)
                return carry

            lax.fori_loop(low, high, now, 0, unroll=2)


def surface(out, order, col_basis, onehot, traces, spread):
    build_onehot(order, onehot)
    top = jnp.concatenate([out[x, NY - 1] for x in range(XL)], axis=1).astype(bf16)
    tr = dot(top, onehot[...], NN).astype(bf16)
    traces[...] = tr
    parts = [
        dot(col_basis[c], tr[:, c * CLUSTER : (c + 1) * CLUSTER], NT) for c in range(2)
    ]
    packed = jnp.concatenate(parts, axis=1).astype(bf16)

    def copy(i, carry):
        spread[i] = packed
        return carry

    lax.fori_loop(0, NDEV, copy, 0, unroll=8)


BLOCK_1 = 1
BLOCK_2 = 0


def sweep_1a_kernel(
    values, cond, reac, res, recv_a, recv_b,
    cond_ext, reac_ext, coef, inv, first, second, third, out,
):
    index, odd = position()
    extend(odd, recv_a, recv_b, cond, reac, cond_ext, reac_ext)
    normalise(index, cond_ext, reac_ext, coef, inv)
    start_own(odd, values, res, recv_a, recv_b, coef, inv, first, None)
    start_halo(1, odd, values, (recv_a, recv_b), (None, 0), coef, inv, first, None)
    sweeps((BLOCK_1, False), values, coef, first, second, third, out)


def sweep_1b_kernel(
    values, forcing, cond, reac, far_a, far_b, coef, inv, order, col_basis,
    first_in, second_in, third_in, out_in,
    out_hbm, res_hbm, traces, send_a, send_b, spread, first, second, third, out,
    raw, onehot, sems,
):
    _, odd = position()
    for h in (2, 3):
        start_halo(h, odd, values, None, ((far_a, far_b), 0), coef, inv, first, None)
    sweeps((BLOCK_1, True), values, coef, first, second, third, out)
    out_copy = pltpu.make_async_copy(out, out_hbm, sems.at[0])
    out_copy.start()
    surface(out, order, col_basis, onehot, traces, spread)
    raw_faces(cond, reac, raw)

    def layer(x, carry):
        residual_layer(x, out, forcing, raw, second, None)
        return carry

    lax.fori_loop(0, XL, layer, 0, unroll=2)
    res_copy = pltpu.make_async_copy(second.at[pl.ds(0, XL)], res_hbm, sems.at[1])
    res_copy.start()
    pack(odd, out, second, (send_a, send_b), (send_a, send_b), 2 * NY)
    out_copy.wait()
    res_copy.wait()


def sweep_2a_kernel(
    values_hbm, res, cond_ext, reac_ext, recv_a, recv_b, placed,
    values, coef, inv, first, second, third, out,
    sems,
):
    index, odd = position()
    inner = pl.ds(1, XL - 2)
    loads = [
        pltpu.make_async_copy(values_hbm.at[x], values.at[x], sems.at[i])
        for i, x in enumerate((0, XL - 1))
    ]
    loads.append(pltpu.make_async_copy(values_hbm.at[inner], values.at[inner], sems.at[2]))
    for load in loads:
        load.start()
    normalise(index, cond_ext, reac_ext, coef, inv)
    for load in loads:
        load.wait()
    start_own(odd, values, res, recv_a, recv_b, coef, inv, first, placed)
    sweeps((BLOCK_2, False), values, coef, first, second, third, out)


def sweep_2b_kernel(
    values, recv_a, recv_b, tract_a, tract_b, coef, inv, order, col_basis,
    first_in, second_in, third_in, out_in,
    out_hbm, traces, spread, first, second, third, out,
    onehot, sem,
):
    _, odd = position()
    recvs = (recv_a, recv_b)
    for h in (1, 2, 3):
        start_halo(
            h, odd, values, recvs, (recvs, 2 * NY), coef, inv, first, (tract_a, tract_b)
        )
    sweeps((BLOCK_2, True), values, coef, first, second, third, out)
    out_copy = pltpu.make_async_copy(out, out_hbm, sem)
    out_copy.start()
    surface(out, order, col_basis, onehot, traces, spread)
    out_copy.wait()


def mask_kernel(couplings, leaf, masked):
    wide = NDEV * 2 * RANK
    cluster = lax.broadcasted_iota(jnp.int32, (NDEV * 2, wide), 0)
    lane = lax.broadcasted_iota(jnp.int32, (NDEV * 2, wide), 1)
    spread = jnp.where(lane // RANK == cluster, 1.0, 0.0).astype(bf16)
    for c in range(2):
        flags = jnp.broadcast_to(leaf[c : c + 1, :].astype(f32), (16, NDEV * 2)).astype(bf16)
        weights = dot(flags, spread, NN)[0:1]
        rows = couplings[c * RANK : (c + 1) * RANK, :].astype(f32)
        masked[c * RANK : (c + 1) * RANK, :] = (rows * weights).astype(bf16)


NEAR_CHUNK = 256


def near_windows(traces, recv_a, recv_b, window):
    _, odd = position()
    window[1] = traces[...]
    for recv, right in sides_of(odd, recv_a, recv_b):
        window[jnp.where(right, 2, 0)] = recv[...]
    left, own, right = window[0], window[1], window[2]
    return (
        jnp.concatenate([left, own, right[:, :CLUSTER]], axis=1),
        jnp.concatenate([left[:, CLUSTER:], own, right], axis=1),
    )


def near_1_kernel(traces, recv_a, recv_b, tiles, out, window):
    wide = near_windows(traces, recv_a, recv_b, window)
    for c in range(2):
        out[:, c * CLUSTER : (c + 1) * CLUSTER] = dot(wide[c], tiles[c], NT)


def near_2_kernel(traces, recv_a, recv_b, tiles_hbm, out, window, tiles, sems):
    chunks = [
        pltpu.make_async_copy(
            tiles_hbm.at[i // 2, pl.ds((i % 2) * NEAR_CHUNK, NEAR_CHUNK), :],
            tiles.at[i],
            sems.at[i],
        )
        for i in range(4)
    ]
    for chunk in chunks:
        chunk.start()
    wide = near_windows(traces, recv_a, recv_b, window)
    for i, chunk in enumerate(chunks):
        chunk.wait()
        out[:, i * NEAR_CHUNK : (i + 1) * NEAR_CHUNK] = dot(wide[i // 2], tiles[i], NT)


def far_part(gathered, masked, row_basis, nearby, out):
    g = gathered[...]
    turned = jnp.concatenate([g[:, :, COLS:], g[:, :, :COLS]], axis=2)
    g = jnp.concatenate([g, turned], axis=1).reshape(NDEV * 2 * RANK, NZ)
    coupled = dot(masked[...], g, NN)
    coupled = jnp.transpose(coupled)[:COLS].astype(bf16)
    for c in range(2):
        cut = slice(c * CLUSTER, (c + 1) * CLUSTER)
        part = dot(coupled[:, c * RANK : (c + 1) * RANK], row_basis[c], NN)
        out[:, cut] = nearby[:, cut] + part


def far_1_kernel(
    gathered, masked, row_basis, nearby, order, res_hbm,
    res, placed, send_a, send_b,
    onehot, total, sem,
):
    _, odd = position()
    load = pltpu.make_async_copy(res_hbm, res, sem)
    load.start()
    far_part(gathered, masked, row_basis, nearby, total)
    build_onehot(order, onehot)
    cells = place(total[...], onehot)
    for x in range(XL):
        placed[x] = cells[:, x * NZ : (x + 1) * NZ]
    for send, right in ((send_a, odd == 0), (send_b, odd != 0)):
        for h in (1, 2, 3):
            send[h - 1] = placed[jnp.where(right, XL - h, h - 1)].astype(bf16)
    load.wait()


def far_2_kernel(gathered, masked, row_basis, nearby, out):
    far_part(gathered, masked, row_basis, nearby, out)


class Hbm:
    def __init__(self, value):
        self.value = value


def call(kernel, outs, scratch, *operands, aliases={}):
    vmem = pl.BlockSpec(memory_space=pltpu.VMEM)
    hbm = pl.BlockSpec(memory_space=pltpu.HBM)
    given = [
        pltpu.with_memory_space_constraint(x.value, pltpu.HBM)
        if isinstance(x, Hbm)
        else pltpu.with_memory_space_constraint(x, pltpu.VMEM)
        for x in operands
    ]
    return pl.pallas_call(
        kernel,
        out_shape=[
            pltpu.HBM(x.value.shape, x.value.dtype)
            if isinstance(x, Hbm)
            else pltpu.VMEM(x.shape, x.dtype)
            for x in outs
        ],
        in_specs=[hbm if isinstance(x, Hbm) else vmem for x in operands],
        out_specs=[hbm if isinstance(x, Hbm) else vmem for x in outs],
        scratch_shapes=scratch,
        input_output_aliases=aliases,
        compiler_params=pltpu.CompilerParams(vmem_limit_bytes=24 << 20),
    )(*given)


struct = jax.ShapeDtypeStruct
FIELD = struct((XL, NY, COLS, NZ), f32)
EXT_FIELD = struct((EXT, NY, COLS, NZ), f32)
ONEHOT = pltpu.VMEM((SROW, SROW), bf16)
RAW = pltpu.VMEM((7, XL, NY, NZ), f32)
COEF = struct((6, EXT, NY, NZ), f32)
INV = struct((1, EXT, NY, NZ), f32)
DMA = pltpu.SemaphoreType.DMA


def gather(spread):
    return lax.all_to_all(spread, "dev", split_axis=0, concat_axis=0, tiled=True)


def block_steps(
    field_start, forcing, traction_start, conductivity, reaction, surface_order,
    near_tiles, col_basis, row_basis, couplings, far_leaf,
):
    order = surface_order.reshape(1, SROW)
    wide = NDEV * 2 * RANK
    layer = struct((XL, NY, NZ), f32)
    message = struct((2 * NY + 1, COLS, NZ), bf16)
    far_message = struct((2 * NY, COLS, NZ), bf16)
    values, forcing_near, cond, reac, res, send_a, send_b, far_a, far_b = call(
        first_kernel,
        [FIELD, FIELD, layer, layer, FIELD, message, message, far_message, far_message],
        [
            pltpu.VMEM((1, SROW), jnp.int32), pltpu.VMEM((COLS, SROW), f32), RAW, ONEHOT,
            pltpu.VMEM((XL, COLS, NZ), f32), DMA((4,)), DMA((2, XL)),
        ],
        Hbm(field_start), Hbm(forcing), Hbm(traction_start), Hbm(order),
        Hbm(conductivity), Hbm(reaction),
    )
    recv_a, recv_b = swap(send_a, send_b)
    far_a, far_b = swap(far_a, far_b)
    (masked,) = call(
        mask_kernel,
        [struct((2 * RANK, wide), bf16)],
        [],
        couplings.reshape(2 * RANK, wide), far_leaf,
    )
    message = struct((4 * NY, COLS, NZ), bf16)
    spread_shape = struct((NDEV, RANK, NZ), bf16)
    traces_shape = struct((COLS, SROW), bf16)
    near_shape = struct((COLS, SROW), f32)
    window = pltpu.VMEM((3, COLS, SROW), bf16)
    steps = [EXT_FIELD, EXT_FIELD, EXT_FIELD, FIELD]
    cond_ext, reac_ext, coef, inv, *state = call(
        sweep_1a_kernel,
        [struct((XL + 8, NY, NZ), f32), struct((EXT, NY, NZ), f32), COEF, INV] + steps,
        [],
        values, cond, reac, res, recv_a, recv_b,
    )
    field, res, traces, send_a, send_b, spread, *_ = call(
        sweep_1b_kernel,
        [Hbm(FIELD), Hbm(FIELD), traces_shape, message, message, spread_shape] + steps,
        [RAW, ONEHOT, DMA((2,))],
        values, forcing_near, cond, reac, far_a, far_b, coef, inv, order, col_basis, *state,
        aliases={10 + i: 6 + i for i in range(4)},
    )
    near_a, near_b = swap(traces, traces)
    gathered = gather(spread)
    recv_a, recv_b = swap(send_a, send_b)
    (nearby,) = call(
        near_1_kernel, [near_shape], [window], traces, near_a, near_b, near_tiles
    )
    tract = struct((3, COLS, NZ), bf16)
    res, placed, tract_a, tract_b = call(
        far_1_kernel,
        [FIELD, struct((XL, COLS, NZ), f32), tract, tract],
        [ONEHOT, pltpu.VMEM((COLS, SROW), f32), DMA],
        gathered, masked, row_basis, nearby, order, Hbm(res),
    )
    tract_a, tract_b = swap(tract_a, tract_b)
    values, coef, inv, *state = call(
        sweep_2a_kernel,
        [FIELD, COEF, INV] + steps,
        [DMA((3,))],
        Hbm(field), res, cond_ext, reac_ext, recv_a, recv_b, placed,
    )
    field, traces, spread, *_ = call(
        sweep_2b_kernel,
        [Hbm(FIELD), traces_shape, spread_shape] + steps,
        [ONEHOT, DMA],
        values, recv_a, recv_b, tract_a, tract_b, coef, inv, order, col_basis, *state,
        aliases={9 + i: 3 + i for i in range(4)},
    )
    near_a, near_b = swap(traces, traces)
    gathered = gather(spread)
    (nearby,) = call(
        near_2_kernel,
        [near_shape],
        [window, pltpu.VMEM((4, NEAR_CHUNK, 5 * CLUSTER), bf16), DMA((4,))],
        traces, near_a, near_b, Hbm(near_tiles),
    )
    (traction,) = call(
        far_2_kernel,
        [struct((COLS, SROW), f32)],
        [],
        gathered, masked, row_basis, nearby,
    )
    return field, traction


def solution(mesh):
    in_specs = (
        P("dev", None, "sec", None),
        P("dev", None, "sec", None),
        P("sec", "dev"),
        P("dev", None, None),
        P("dev", None, None),
        P("dev"),
        P("dev", None, None),
        P("dev", None, None),
        P("dev", None, None),
        P("dev", None, None),
        P("dev", None),
    )
    out_specs = (P("dev", None, "sec", None), P("sec", "dev"))
    return jax.shard_map(
        block_steps, mesh=mesh, in_specs=in_specs, out_specs=out_specs, check_vma=False
    )
```

time: 146 us -> 118 us (0.81)
  Pallas kernels: 55.6 us -> 35.3 us
  waiting for transfers between devices: 30.5 us -> 23.5 us
  local copies, waits for them, and re-layouts: 4.97 us -> 3.21 us
    pallas_call x9 -> x10, Pallas kernels: 55.6 us -> 35.3 us  [call(): pl.pallas_call(kernel, out_shape=[pltpu.HBM(x.value.shape, x.value.dtype)...]
    ppermute x10 -> x12, waiting for transfers between devices: 30.5 us -> 23.5 us  [swap(): return (lax.ppermute(a, 'dev', SWAP_A), lax.ppermute(b, 'dev', SWAP_B))]
    ppermute x10 -> x12, starting transfers between devices: 34.1 us -> 37.3 us  [swap(): return (lax.ppermute(a, 'dev', SWAP_A), lax.ppermute(b, 'dev', SWAP_B))]
    all_to_all x2, starting transfers between devices: 19.1 us -> 16.9 us  [gather(): lax.all_to_all(spread, 'dev', split_axis=0, concat_axis=0, tiled=True)]
    unnamed x26 -> x13, local copies, waits for them, and re-layouts: 4.97 us -> 3.21 us
  transfers between devices with their start and end apart: 12 -> 14, of which waited for: 6 -> 7; matrix products, arithmetic and copies ran while one was open for 0% -> 0% of each run, Pallas kernels for 15% -> 14%
where the time goes in v2:
time: 118 us; the launch traced here: 117 us
  starting transfers between devices  54.2 us (46%)
  Pallas kernels  35.3 us (30%)
  waiting for transfers between devices  23.5 us (20%)
  local copies, waits for them, and re-layouts  3.21 us (3%)
    ppermute x12, starting transfers between devices, swap(): return (lax.ppermute(a, 'dev', SWAP_A), lax.ppermute(b, 'dev', SWAP_B))  37.3 us
    pallas_call x10, Pallas kernels, call(): pl.pallas_call(kernel, out_shape=[pltpu.HBM(x.value.shape, x.value.dtype)...  35.3 us
    ppermute x12, waiting for transfers between devices, swap(): return (lax.ppermute(a, 'dev', SWAP_A), lax.ppermute(b, 'dev', SWAP_B))  23.5 us
    all_to_all x2, starting transfers between devices, gather(): lax.all_to_all(spread, 'dev', split_axis=0, concat_axis=0, tiled=True)  16.9 us
    unnamed x13, local copies, waits for them, and re-layouts  3.21 us
  transfers between devices with their start and end apart: 14, of which 7 were waited for; matrix products, arithmetic and copies ran while one was open for 0% of the time, Pallas kernels for 14%

profile of v2, /device:TPU:6, one launch (start us, length us, event | category | flops | bytes accessed | tf_op | source)
XLA Modules:
  0.0 117.1 jit_solution(18195118833677711735)
XLA Ops:
  0.6 5.1 %shard_map.122 = (f32[8,8,64,128]{3,2,1,0:T(8,128)S(1)}, f32[8,8,64,128]{3,2,1,0:T(8,128)S(1)}, f32[8,8,128]{2,1,0:T(8,128)S(1)}, f32[8,8,128]{2,1,0:T(8,128)S(1...) custom-call(f32[8,8,64,128]{3,2,1,0:T(8,128)} %values_hbm.1, ...), custom_call_target="tpu_custom_call" | custom-call | tf_op jit(solution)/shard_map/pallas_call | solution.py:538
  5.7 2.0 %collective-permute-start.2 = (bf16[17,64,128]{2,1,0:T(8,128)(2,1)S(1)}, bf16[17,64,128]{2,1,0:T(8,128)(2,1)S(1)}, u32[]{:S(2)}, u32[]{:S(2)}) collective-permute-start(bf16[17,64,128]{2,1,0:T(8,128)(2,1)S(1)} %get-tuple-element.46), channel_id=1, source_target_pairs={{0,1},{1,0},{2,3},{3,2},{4,5},{5,4},{6,7},{7,6},{8,9},{9,8},{10,11... | collective-permute-start | bytes 835592 | tf_op jit(solution)/shard_map/ppermute | solution.py:43
  7.7 7.1 %collective-permute-start.3 = (bf16[17,64,128]{2,1,0:T(8,128)(2,1)S(1)}, bf16[17,64,128]{2,1,0:T(8,128)(2,1)S(1)}, u32[]{:S(2)}, u32[]{:S(2)}) collective-permute-start(bf16[17,64,128]{2,1,0:T(8,128)(2,1)S(1)} %get-tuple-element.47), channel_id=1, source_target_pairs={{1,2},{3,4},{5,6},{7,8},{9,10},{11,12},{13,14},{15,16},{17,18},{19... | collective-permute-start | bytes 835592 | tf_op jit(solution)/shard_map/ppermute | solution.py:43
  14.9 0.1 collective-permute-start
  15.0 3.5 %collective-permute-start.1 = (bf16[16,64,128]{2,1,0:T(8,128)(2,1)S(1)}, bf16[16,64,128]{2,1,0:T(8,128)(2,1)S(1)}, u32[]{:S(2)}, u32[]{:S(2)}) collective-permute-start(bf16[16,64,128]{2,1,0:T(8,128)(2,1)S(1)} %get-tuple-element.44), channel_id=1, source_target_pairs={{1,2},{3,4},{5,6},{7,8},{9,10},{11,12},{13,14},{15,16},{17,18},{19... | collective-permute-start | bytes 786440 | tf_op jit(solution)/shard_map/ppermute | solution.py:43
  18.5 0.0 collective-permute-done.2.recv_a
  18.5 3.4 %collective-permute-done.3.recv_b = bf16[17,64,128]{2,1,0:T(8,128)(2,1)S(1)} collective-permute-done((bf16[17,64,128]{2,1,0:T(8,128)(2,1)S(1)}, bf16[17,64,128]{2,1,0:T(8,128)(2,1)S(1)}, u32[]{:S(2)}, u32[]{:S(2)}) %collective-permute-start.3) | collective-permute-done | bytes 278560 | tf_op jit(solution)/shard_map/ppermute | solution.py:43
  21.9 0.0 copy-start.4
  21.9 4.0 %shard_map.123 = (f32[16,8,128]{2,1,0:T(8,128)S(1)}, f32[14,8,128]{2,1,0:T(8,128)S(1)}, f32[6,14,8,128]{3,2,1,0:T(8,128)S(1)}, f32[1,14,8,128]{3,2,1,0:T(8,128)S...) custom-call(f32[8,8,64,128]{3,2,1,0:T(8,128)S(1)} %get-tuple-element, ...), custom_call_target="tpu_custom_call" | custom-call | tf_op jit(solution)/shard_map/pallas_call | solution.py:538
  26.0 0.0 collective-permute-done.far_a
  26.0 2.6 %collective-permute-done.1.far_b = bf16[16,64,128]{2,1,0:T(8,128)(2,1)S(1)} collective-permute-done((bf16[16,64,128]{2,1,0:T(8,128)(2,1)S(1)}, bf16[16,64,128]{2,1,0:T(8,128)(2,1)S(1)}, u32[]{:S(2)}, u32[]{:S(2)}) %collective-permute-start.1) | collective-permute-done | bytes 262176 | tf_op jit(solution)/shard_map/ppermute | solution.py:43
  28.6 0.0 copy-done.2
  28.6 0.0 copy-done.4
  28.6 0.0 copy-start.1
  28.6 7.4 %shard_map.124 = (f32[8,8,64,128]{3,2,1,0:T(8,128)}, f32[8,8,64,128]{3,2,1,0:T(8,128)}, bf16[64,1024]{1,0:T(8,128)(2,1)S(1)}, bf16[32,64,128]{2,1,0:T(8,128)(2,1...) custom-call(f32[8,8,64,128]{3,2,1,0:T(8,128)S(1)} %get-tuple-element, ...), custom_call_target="tpu_custom_call", output_to_operand_aliasing={{6}: (10, {}), {7}: (11, {}), {8}: (12, {}), {9}: (13, {})} | custom-call | tf_op jit(solution)/shard_map/pallas_call | solution.py:538
  36.0 9.0 %all-to-all-start = ((bf16[64,32,128]{2,1,0:T(8,128)(2,1)}), bf16[64,32,128]{2,1,0:T(8,128)(2,1)S(1)}, u32[]{:S(2)}, u32[]{:S(2)}) async-start(bf16[64,32,128]{2,1,0:T(8,128)(2,1)} %get-tuple-element.55), calls=%async_computation | async-start | bytes 1048576 | tf_op jit(solution)/shard_map/all_to_all | solution.py:565
  45.0 1.5 %collective-permute-start.6 = (bf16[32,64,128]{2,1,0:T(8,128)(2,1)}, bf16[32,64,128]{2,1,0:T(8,128)(2,1)S(1)}, u32[]{:S(2)}, u32[]{:S(2)}) collective-permute-start(bf16[32,64,128]{2,1,0:T(8,128)(2,1)} %get-tuple-element.61), channel_id=1, source_target_pairs={{0,1},{1,0},{2,3},{3,2},{4,5},{5,4},{6,7},{7,6},{8,9},{9,8},{10,11... | collective-permute-start | bytes 1572872 | tf_op jit(solution)/shard_map/ppermute | solution.py:43
  46.5 6.3 %collective-permute-start.7 = (bf16[32,64,128]{2,1,0:T(8,128)(2,1)S(1)}, bf16[32,64,128]{2,1,0:T(8,128)(2,1)S(1)}, u32[]{:S(2)}, u32[]{:S(2)}) collective-permute-start(bf16[32,64,128]{2,1,0:T(8,128)(2,1)S(1)} %get-tuple-element.62), channel_id=1, source_target_pairs={{1,2},{3,4},{5,6},{7,8},{9,10},{11,12},{13,14},{15,16},{17,18},{19... | collective-permute-start | bytes 1572872 | tf_op jit(solution)/shard_map/ppermute | solution.py:43
  52.9 0.1 collective-permute-start.4
  53.0 3.7 %collective-permute-start.5 = (bf16[64,1024]{1,0:T(8,128)(2,1)S(1)}, bf16[64,1024]{1,0:T(8,128)(2,1)S(1)}, u32[]{:S(2)}, u32[]{:S(2)}) collective-permute-start(bf16[64,1024]{1,0:T(8,128)(2,1)S(1)} %get-tuple-element.56.traces), channel_id=1, source_target_pairs={{1,2},{3,4},{5,6},{7,8},{9,10},{11,12},{13,14},{15,16},{17,18},{19... | collective-permute-start | bytes 393224 | tf_op jit(solution)/shard_map/ppermute | solution.py:43
  56.7 0.0 copy-done.1
  56.7 0.0 copy-done.5
  56.7 0.0 copy-start.3
  56.7 0.3 shard_map.125.masked
  57.0 8.3 %collective-permute-done.4.recv_a = bf16[64,1024]{1,0:T(8,128)(2,1)S(1)} collective-permute-done((bf16[64,1024]{1,0:T(8,128)(2,1)S(1)}, bf16[64,1024]{1,0:T(8,128)(2,1)S(1)}, u32[]{:S(2)}, u32[]{:S(2)}) %collective-permute-start.4) | collective-permute-done | bytes 131104 | tf_op jit(solution)/shard_map/ppermute | solution.py:43
  65.3 3.2 %collective-permute-done.5.recv_b = bf16[64,1024]{1,0:T(8,128)(2,1)S(1)} collective-permute-done((bf16[64,1024]{1,0:T(8,128)(2,1)S(1)}, bf16[64,1024]{1,0:T(8,128)(2,1)S(1)}, u32[]{:S(2)}, u32[]{:S(2)}) %collective-permute-start.5) | collective-permute-done | bytes 131104 | tf_op jit(solution)/shard_map/ppermute | solution.py:43
  68.5 2.5 %copy-done = bf16[2,512,2560]{2,1,0:T(8,128)(2,1)S(1)} copy-done((bf16[2,512,2560]{2,1,0:T(8,128)(2,1)S(1)}, bf16[2,512,2560]{2,1,0:T(8,128)(2,1)}, u32[]{:S(2)}) %copy-start) | copy-done | bytes 5242904
  71.0 1.7 %shard_map.126.nearby = f32[64,1024]{1,0:T(8,128)S(1)} custom-call(bf16[64,1024]{1,0:T(8,128)(2,1)S(1)} %get-tuple-element.56.traces, bf16[64,1024]{1,0:T(8,128)(2,1)S(1)} %collective-permute-done.4.recv_a, bf16[64,1024]{1,0:T(8,128)(2,1)S(1)} %collective-permute-done.5.recv_b, bf16[2,512,2560]{2,1,0:T(8,128)(2,1)S(1)} %copy-done), custom_call_target="tpu_custom_call" | custom-call | tf_op jit(solution)/shard_map/pallas_call | solution.py:538
  72.7 0.0 all-to-all-done.gathered
  72.7 0.0 copy-done.3
  72.7 1.9 %shard_map.127 = (f32[8,8,64,128]{3,2,1,0:T(8,128)S(1)}, f32[8,64,128]{2,1,0:T(8,128)S(1)}, bf16[3,64,128]{2,1,0:T(8,128)(2,1)S(1)}, bf16[3,64,128]{2,1,0:T(8,128)(2,1)S(1)}) custom-call(bf16[64,32,128]{2,1,0:T(8,128)(2,1)S(1)} %all-to-all-done.gathered, bf16[64,4096]{1,0:T(8,128)(2,1)S(1)} %shard_map.125.masked, bf16[2,32,512]{2,1,0:T(8,128)(2,1)S(1)} %copy-done.3, ...), custom_call_target="tpu_custom_call" | custom-call | tf_op jit(solution)/shard_map/pallas_call | solution.py:538
  74.7 0.1 collective-permute-start.8
  74.8 4.9 %collective-permute-start.9 = (bf16[3,64,128]{2,1,0:T(8,128)(2,1)S(1)}, bf16[3,64,128]{2,1,0:T(8,128)(2,1)S(1)}, u32[]{:S(2)}, u32[]{:S(2)}) collective-permute-start(bf16[3,64,128]{2,1,0:T(8,128)(2,1)S(1)} %get-tuple-element.66), channel_id=1, source_target_pairs={{1,2},{3,4},{5,6},{7,8},{9,10},{11,12},{13,14},{15,16},{17,18},{19... | collective-permute-start | bytes 147464 | tf_op jit(solution)/shard_map/ppermute | solution.py:43
  79.7 0.0 collective-permute-done.6.recv_a
  79.7 0.0 collective-permute-done.7.recv_b
  79.7 4.0 %shard_map.128 = (f32[8,8,64,128]{3,2,1,0:T(8,128)S(1)}, f32[6,14,8,128]{3,2,1,0:T(8,128)S(1)}, f32[1,14,8,128]{3,2,1,0:T(8,128)S(1)}, f32[14,8,64,128]{3,2,1,0:...) custom-call(f32[8,8,64,128]{3,2,1,0:T(8,128)} %get-tuple-element.54.valu, ...), custom_call_target="tpu_custom_call" | custom-call | tf_op jit(solution)/shard_map/pallas_call | solution.py:538
  83.7 0.0 collective-permute-done.8.tract_a
  83.7 1.2 %collective-permute-done.9.tract_b = bf16[3,64,128]{2,1,0:T(8,128)(2,1)S(1)} collective-permute-done((bf16[3,64,128]{2,1,0:T(8,128)(2,1)S(1)}, bf16[3,64,128]{2,1,0:T(8,128)(2,1)S(1)}, u32[]{:S(2)}, u32[]{:S(2)}) %collective-permute-start.9) | collective-permute-done | bytes 49184 | tf_op jit(solution)/shard_map/ppermute | solution.py:43
  85.0 5.7 %shard_map.129 = (f32[8,8,64,128]{3,2,1,0:T(8,128)}, bf16[64,1024]{1,0:T(8,128)(2,1)S(1)}, bf16[64,32,128]{2,1,0:T(8,128)(2,1)}, f32[14,8,64,128]{3,2,1,0:T(8,12...) custom-call(f32[8,8,64,128]{3,2,1,0:T(8,128)S(1)} %get-tuple-element, ...), custom_call_target="tpu_custom_call", output_to_operand_aliasing={{3}: (9, {}), {4}: (10, {}), {5}: (11, {}), {6}: (12, {})} | custom-call | tf_op jit(solution)/shard_map/pallas_call | solution.py:538
  90.6 7.9 %all-to-all-start.1 = ((bf16[64,32,128]{2,1,0:T(8,128)(2,1)}), bf16[64,32,128]{2,1,0:T(8,128)(2,1)S(1)}, u32[]{:S(2)}, u32[]{:S(2)}) async-start(bf16[64,32,128]{2,1,0:T(8,128)(2,1)} %get-tuple-element.74), calls=%async_computation.1 | async-start | bytes 1048576 | tf_op jit(solution)/shard_map/all_to_all | solution.py:565
  98.6 1.5 %collective-permute-start.10 = (bf16[64,1024]{1,0:T(8,128)(2,1)S(1)}, bf16[64,1024]{1,0:T(8,128)(2,1)S(1)}, u32[]{:S(2)}, u32[]{:S(2)}) collective-permute-start(bf16[64,1024]{1,0:T(8,128)(2,1)S(1)} %get-tuple-element.75.traces), channel_id=1, source_target_pairs={{0,1},{1,0},{2,3},{3,2},{4,5},{5,4},{6,7},{7,6},{8,9},{9,8},{10,11... | collective-permute-start | bytes 393224 | tf_op jit(solution)/shard_map/ppermute | solution.py:43
  100.1 6.3 %collective-permute-start.11 = (bf16[64,1024]{1,0:T(8,128)(2,1)S(1)}, bf16[64,1024]{1,0:T(8,128)(2,1)S(1)}, u32[]{:S(2)}, u32[]{:S(2)}) collective-permute-start(bf16[64,1024]{1,0:T(8,128)(2,1)S(1)} %get-tuple-element.75.traces), channel_id=1, source_target_pairs={{1,2},{3,4},{5,6},{7,8},{9,10},{11,12},{13,14},{15,16},{17,18},{19... | collective-permute-start | bytes 393224 | tf_op jit(solution)/shard_map/ppermute | solution.py:43
  106.5 0.1 collective-permute-done.10.recv_a
  106.5 4.7 %collective-permute-done.11.recv_b = bf16[64,1024]{1,0:T(8,128)(2,1)S(1)} collective-permute-done((bf16[64,1024]{1,0:T(8,128)(2,1)S(1)}, bf16[64,1024]{1,0:T(8,128)(2,1)S(1)}, u32[]{:S(2)}, u32[]{:S(2)}) %collective-permute-start.11) | collective-permute-done | bytes 131104 | tf_op jit(solution)/shard_map/ppermute | solution.py:43
  111.2 4.6 %shard_map.130.nearby = f32[64,1024]{1,0:T(8,128)S(1)} custom-call(bf16[64,1024]{1,0:T(8,128)(2,1)S(1)} %get-tuple-element.75.traces, bf16[64,1024]{1,0:T(8,128)(2,1)S(1)} %collective-permute-done.10.recv_a, bf16[64,1024]{1,0:T(8,128)(2,1)S(1)} %collective-permute-done.11.recv_b, bf16[2,512,2560]{2,1,0:T(8,128)(2,1)} %tiles_hbm.1), custom_call_target="tpu_custom_call" | custom-call | tf_op jit(solution)/shard_map/pallas_call | solution.py:538
  115.8 0.0 all-to-all-done.1.gathered
  115.8 0.6 shard_map.131
  116.4 0.7 copy.29
  (3 shorter events, 0.0 us)
Async XLA Ops:
  5.7 12.8 %collective-permute-start.2 = (bf16[17,64,128]{2,1,0:T(8,128)(2,1)S(1)}, bf16[17,64,128]{2,1,0:T(8,128)(2,1)S(1)}, u32[]{:S(2)}, u32[]{:S(2)}) collective-permute-start(bf16[17,64,128]{2,1,0:T(8,128)(2,1)S(1)} %get-tuple-element.46), channel_id=1, source_target_pairs={{0,1},{1,0},{2,3},{3,2},{4,5},{5,4},{6,7},{7,6},{8,9},{9,8},{10,11... | collective-permute-start | bytes 835592 | tf_op jit(solution)/shard_map/ppermute | solution.py:43
  7.7 14.2 %collective-permute-start.3 = (bf16[17,64,128]{2,1,0:T(8,128)(2,1)S(1)}, bf16[17,64,128]{2,1,0:T(8,128)(2,1)S(1)}, u32[]{:S(2)}, u32[]{:S(2)}) collective-permute-start(bf16[17,64,128]{2,1,0:T(8,128)(2,1)S(1)} %get-tuple-element.47), channel_id=1, source_target_pairs={{1,2},{3,4},{5,6},{7,8},{9,10},{11,12},{13,14},{15,16},{17,18},{19... | collective-permute-start | bytes 835592 | tf_op jit(solution)/shard_map/ppermute | solution.py:43
  14.9 11.1 %collective-permute-start = (bf16[16,64,128]{2,1,0:T(8,128)(2,1)S(1)}, bf16[16,64,128]{2,1,0:T(8,128)(2,1)S(1)}, u32[]{:S(2)}, u32[]{:S(2)}) collective-permute-start(bf16[16,64,128]{2,1,0:T(8,128)(2,1)S(1)} %get-tuple-element.43), channel_id=1, source_target_pairs={{0,1},{1,0},{2,3},{3,2},{4,5},{5,4},{6,7},{7,6},{8,9},{9,8},{10,11... | collective-permute-start | bytes 786440 | tf_op jit(solution)/shard_map/ppermute | solution.py:43
  15.0 13.6 %collective-permute-start.1 = (bf16[16,64,128]{2,1,0:T(8,128)(2,1)S(1)}, bf16[16,64,128]{2,1,0:T(8,128)(2,1)S(1)}, u32[]{:S(2)}, u32[]{:S(2)}) collective-permute-start(bf16[16,64,128]{2,1,0:T(8,128)(2,1)S(1)} %get-tuple-element.44), channel_id=1, source_target_pairs={{1,2},{3,4},{5,6},{7,8},{9,10},{11,12},{13,14},{15,16},{17,18},{19... | collective-permute-start | bytes 786440 | tf_op jit(solution)/shard_map/ppermute | solution.py:43
  21.9 6.6 %copy-start.2 = (bf16[2,32,512]{2,1,0:T(8,128)(2,1)S(1)}, bf16[2,32,512]{2,1,0:T(8,128)(2,1)}, u32[]{:S(2)}) copy-start(bf16[2,32,512]{2,1,0:T(8,128)(2,1)} %col_basis.3) | copy-start | bytes 196612
  21.9 6.6 %copy-start.4 = (s32[1024]{0:T(1024)S(1)}, s32[1024]{0:T(1024)}, u32[]{:S(2)}) copy-start(s32[1024]{0:T(1024)} %param.16) | copy-start | bytes 12292
  28.6 28.1 %copy-start.1 = (bf16[2,32,4096]{2,1,0:T(8,128)(2,1)S(1)}, bf16[2,32,4096]{2,1,0:T(8,128)(2,1)}, u32[]{:S(2)}) copy-start(bf16[2,32,4096]{2,1,0:T(8,128)(2,1)} %param.20) | copy-start | bytes 1572868
  28.6 28.1 %copy-start.5 = (s32[2,128]{1,0:T(2,128)S(1)}, s32[2,128]{1,0:T(2,128)}, u32[]{:S(2)}) copy-start(s32[2,128]{1,0:T(2,128)} %leaf.1) | copy-start | bytes 3076
  36.0 36.7 %all-to-all-start = ((bf16[64,32,128]{2,1,0:T(8,128)(2,1)}), bf16[64,32,128]{2,1,0:T(8,128)(2,1)S(1)}, u32[]{:S(2)}, u32[]{:S(2)}) async-start(bf16[64,32,128]{2,1,0:T(8,128)(2,1)} %get-tuple-element.55), calls=%async_computation | async-start | bytes 1048576 | tf_op jit(solution)/shard_map/all_to_all | solution.py:565
  45.0 34.7 %collective-permute-start.6 = (bf16[32,64,128]{2,1,0:T(8,128)(2,1)}, bf16[32,64,128]{2,1,0:T(8,128)(2,1)S(1)}, u32[]{:S(2)}, u32[]{:S(2)}) collective-permute-start(bf16[32,64,128]{2,1,0:T(8,128)(2,1)} %get-tuple-element.61), channel_id=1, source_target_pairs={{0,1},{1,0},{2,3},{3,2},{4,5},{5,4},{6,7},{7,6},{8,9},{9,8},{10,11... | collective-permute-start | bytes 1572872 | tf_op jit(solution)/shard_map/ppermute | solution.py:43
  46.5 33.2 %collective-permute-start.7 = (bf16[32,64,128]{2,1,0:T(8,128)(2,1)S(1)}, bf16[32,64,128]{2,1,0:T(8,128)(2,1)S(1)}, u32[]{:S(2)}, u32[]{:S(2)}) collective-permute-start(bf16[32,64,128]{2,1,0:T(8,128)(2,1)S(1)} %get-tuple-element.62), channel_id=1, source_target_pairs={{1,2},{3,4},{5,6},{7,8},{9,10},{11,12},{13,14},{15,16},{17,18},{19... | collective-permute-start | bytes 1572872 | tf_op jit(solution)/shard_map/ppermute | solution.py:43
  52.9 12.4 %collective-permute-start.4 = (bf16[64,1024]{1,0:T(8,128)(2,1)S(1)}, bf16[64,1024]{1,0:T(8,128)(2,1)S(1)}, u32[]{:S(2)}, u32[]{:S(2)}) collective-permute-start(bf16[64,1024]{1,0:T(8,128)(2,1)S(1)} %get-tuple-element.56.traces), channel_id=1, source_target_pairs={{0,1},{1,0},{2,3},{3,2},{4,5},{5,4},{6,7},{7,6},{8,9},{9,8},{10,11... | collective-permute-start | bytes 393224 | tf_op jit(solution)/shard_map/ppermute | solution.py:43
  53.0 15.6 %collective-permute-start.5 = (bf16[64,1024]{1,0:T(8,128)(2,1)S(1)}, bf16[64,1024]{1,0:T(8,128)(2,1)S(1)}, u32[]{:S(2)}, u32[]{:S(2)}) collective-permute-start(bf16[64,1024]{1,0:T(8,128)(2,1)S(1)} %get-tuple-element.56.traces), channel_id=1, source_target_pairs={{1,2},{3,4},{5,6},{7,8},{9,10},{11,12},{13,14},{15,16},{17,18},{19... | collective-permute-start | bytes 393224 | tf_op jit(solution)/shard_map/ppermute | solution.py:43
  56.7 16.0 %copy-start.3 = (bf16[2,32,512]{2,1,0:T(8,128)(2,1)S(1)}, bf16[2,32,512]{2,1,0:T(8,128)(2,1)}, u32[]{:S(2)}) copy-start(bf16[2,32,512]{2,1,0:T(8,128)(2,1)} %row_basis.3) | copy-start | bytes 196612
  68.5 2.5 %copy-start = (bf16[2,512,2560]{2,1,0:T(8,128)(2,1)S(1)}, bf16[2,512,2560]{2,1,0:T(8,128)(2,1)}, u32[]{:S(2)}) copy-start(bf16[2,512,2560]{2,1,0:T(8,128)(2,1)} %tiles_hbm.1) | copy-start | bytes 15728644
  74.7 9.1 %collective-permute-start.8 = (bf16[3,64,128]{2,1,0:T(8,128)(2,1)S(1)}, bf16[3,64,128]{2,1,0:T(8,128)(2,1)S(1)}, u32[]{:S(2)}, u32[]{:S(2)}) collective-permute-start(bf16[3,64,128]{2,1,0:T(8,128)(2,1)S(1)} %get-tuple-element.65), channel_id=1, source_target_pairs={{0,1},{1,0},{2,3},{3,2},{4,5},{5,4},{6,7},{7,6},{8,9},{9,8},{10,11... | collective-permute-start | bytes 147464 | tf_op jit(solution)/shard_map/ppermute | solution.py:43
  74.8 10.2 %collective-permute-start.9 = (bf16[3,64,128]{2,1,0:T(8,128)(2,1)S(1)}, bf16[3,64,128]{2,1,0:T(8,128)(2,1)S(1)}, u32[]{:S(2)}, u32[]{:S(2)}) collective-permute-start(bf16[3,64,128]{2,1,0:T(8,128)(2,1)S(1)} %get-tuple-element.66), channel_id=1, source_target_pairs={{1,2},{3,4},{5,6},{7,8},{9,10},{11,12},{13,14},{15,16},{17,18},{19... | collective-permute-start | bytes 147464 | tf_op jit(solution)/shard_map/ppermute | solution.py:43
  90.6 25.2 %all-to-all-start.1 = ((bf16[64,32,128]{2,1,0:T(8,128)(2,1)}), bf16[64,32,128]{2,1,0:T(8,128)(2,1)S(1)}, u32[]{:S(2)}, u32[]{:S(2)}) async-start(bf16[64,32,128]{2,1,0:T(8,128)(2,1)} %get-tuple-element.74), calls=%async_computation.1 | async-start | bytes 1048576 | tf_op jit(solution)/shard_map/all_to_all | solution.py:565
  98.6 8.0 %collective-permute-start.10 = (bf16[64,1024]{1,0:T(8,128)(2,1)S(1)}, bf16[64,1024]{1,0:T(8,128)(2,1)S(1)}, u32[]{:S(2)}, u32[]{:S(2)}) collective-permute-start(bf16[64,1024]{1,0:T(8,128)(2,1)S(1)} %get-tuple-element.75.traces), channel_id=1, source_target_pairs={{0,1},{1,0},{2,3},{3,2},{4,5},{5,4},{6,7},{7,6},{8,9},{9,8},{10,11... | collective-permute-start | bytes 393224 | tf_op jit(solution)/shard_map/ppermute | solution.py:43
  100.1 11.1 %collective-permute-start.11 = (bf16[64,1024]{1,0:T(8,128)(2,1)S(1)}, bf16[64,1024]{1,0:T(8,128)(2,1)S(1)}, u32[]{:S(2)}, u32[]{:S(2)}) collective-permute-start(bf16[64,1024]{1,0:T(8,128)(2,1)S(1)} %get-tuple-element.75.traces), channel_id=1, source_target_pairs={{1,2},{3,4},{5,6},{7,8},{9,10},{11,12},{13,14},{15,16},{17,18},{19... | collective-permute-start | bytes 393224 | tf_op jit(solution)/shard_map/ppermute | solution.py:43

commit v3 on v2

--- a/solution.py
+++ b/solution.py
@@ -40,7 +40,9 @@
 
 
 def swap(a, b):
-    return lax.ppermute(a, "dev", SWAP_A), lax.ppermute(b, "dev", SWAP_B)
+    a = lax.ppermute(a, "dev", SWAP_A)
+    b = lax.ppermute(b, "dev", SWAP_B)
+    return a, b
 
 
 def dot(a, b, dims):
@@ -93,15 +95,15 @@
 
 def build_onehot(order, onehot):
     wanted = order[...]
-
-    def rows(x, carry):
-        cell = lax.broadcasted_iota(jnp.int32, (NZ, SROW), 0) + x * NZ
-        onehot[pl.ds(pl.multiple_of(x * NZ, NZ), NZ), :] = jnp.where(
-            cell == wanted, 1.0, 0.0
-        ).astype(bf16)
-        return carry
-
-    lax.fori_loop(0, XL, rows, 0)
+    line = wanted // NZ
+    inner = wanted - line * NZ
+    cell = lax.broadcasted_iota(jnp.int32, (NZ, SROW), 0).astype(f32).astype(bf16)
+    one = jnp.ones((NZ, SROW), bf16)
+    for x in range(XL):
+        here = jnp.where(line == x, inner, -1).astype(f32).astype(bf16)
+        onehot[x * NZ : (x + 1) * NZ, :] = jnp.where(
+            cell == jnp.broadcast_to(here, (NZ, SROW)), one, jnp.zeros_like(one)
+        )
 
 
 def place(traction, onehot):
@@ -172,8 +174,8 @@
 
 def first_kernel(
     values_hbm, forcing_hbm, traction_hbm, order_hbm, cond_hbm, reac_hbm,
-    values, forcing, cond, reac, res, send_a, send_b, far_a, far_b,
-    order, traction, raw, onehot, placed, small_sems, sems,
+    values, forcing, cond, reac, onehot, res, send_a, send_b, far_a, far_b,
+    order, traction, raw, placed, small_sems, sems,
 ):
     _, odd = position()
     small = [
@@ -256,7 +258,7 @@
     return value.astype(f32).reshape(COLS // 8, 8, NZ)
 
 
-def start_own(odd, values, res, recv_a, recv_b, coef, inv, first, placed):
+def start_own(res, inv, first, placed):
     def own(x, carry):
         for y in range(NY):
             r = tile(res, x, y)
@@ -266,6 +268,9 @@
         return carry
 
     lax.fori_loop(0, XL, own, 0, unroll=2)
+
+
+def start_edges(odd, values, recv_a, recv_b, coef, first):
     for recv, right in sides_of(odd, recv_a, recv_b):
         edge = jnp.where(right, XL - 1, 0)
         toward = jnp.where(right, EAST, WEST)
@@ -295,7 +300,7 @@
             put(first, e, y, s)
 
 
-def sweeps(known, values, coef, first, second, third, out):
+def sweeps(done, known, values, coef, first, second, third, out, loads=(), stores=None):
     (a1, b1), (a2, b2), (a3, b3) = chebyshev_factors()
 
     def step_2(e):
@@ -316,28 +321,31 @@
             d = (b1 * b2 * b3) * d + b3 * tile(first, e, y)
             put(out, e - 3, y, tile(values, e - 3, y) + d)
 
+    middle = EXT // 2
     for level, step in ((1, step_2), (2, step_3), (3, step_4)):
-        low, high = 3 + level - known[0], XL + 3 - level + known[0]
-
-        if known[1]:
-            left = low - level
-
-            def later(i, carry):
-                step(jnp.where(i < left, level + i, high + i - left))
-                return carry
-
-            lax.fori_loop(0, 2 * left, later, 0, unroll=2)
-        else:
-
-            def now(e, carry):
-                step(e)
-                return carry
-
-            lax.fori_loop(low, high, now, 0, unroll=2)
-
-
-def surface(out, order, col_basis, onehot, traces, spread):
-    build_onehot(order, onehot)
+        low = 3 + level - known
+        skip = middle if done is None else min(3 + level - done, middle)
+        left = skip - low
+        if level == 3:
+            for load in loads:
+                load.wait()
+            if stores is not None:
+                for e in range(skip, EXT - skip):
+                    stores(e - 3).start()
+        if left <= 0:
+            continue
+
+        def layer(i, carry):
+            e = jnp.where(i < left, low + i, EXT - skip + i - left)
+            step(e)
+            if level == 3 and stores is not None:
+                stores(e - 3).start()
+            return carry
+
+        lax.fori_loop(0, 2 * left, layer, 0, unroll=2)
+
+
+def surface(out, col_basis, onehot, traces, spread):
     top = jnp.concatenate([out[x, NY - 1] for x in range(XL)], axis=1).astype(bf16)
     tr = dot(top, onehot[...], NN).astype(bf16)
     traces[...] = tr
@@ -353,10 +361,6 @@
     lax.fori_loop(0, NDEV, copy, 0, unroll=8)
 
 
-BLOCK_1 = 1
-BLOCK_2 = 0
-
-
 def sweep_1a_kernel(
     values, cond, reac, res, recv_a, recv_b,
     cond_ext, reac_ext, coef, inv, first, second, third, out,
@@ -364,24 +368,27 @@
     index, odd = position()
     extend(odd, recv_a, recv_b, cond, reac, cond_ext, reac_ext)
     normalise(index, cond_ext, reac_ext, coef, inv)
-    start_own(odd, values, res, recv_a, recv_b, coef, inv, first, None)
+    start_own(res, inv, first, None)
+    start_edges(odd, values, recv_a, recv_b, coef, first)
     start_halo(1, odd, values, (recv_a, recv_b), (None, 0), coef, inv, first, None)
-    sweeps((BLOCK_1, False), values, coef, first, second, third, out)
+    sweeps(None, 1, values, coef, first, second, third, out)
 
 
 def sweep_1b_kernel(
-    values, forcing, cond, reac, far_a, far_b, coef, inv, order, col_basis,
+    values, forcing, cond, reac, far_a, far_b, coef, inv, onehot, col_basis,
     first_in, second_in, third_in, out_in,
     out_hbm, res_hbm, traces, send_a, send_b, spread, first, second, third, out,
-    raw, onehot, sems,
+    raw, sems,
 ):
     _, odd = position()
     for h in (2, 3):
         start_halo(h, odd, values, None, ((far_a, far_b), 0), coef, inv, first, None)
-    sweeps((BLOCK_1, True), values, coef, first, second, third, out)
-    out_copy = pltpu.make_async_copy(out, out_hbm, sems.at[0])
-    out_copy.start()
-    surface(out, order, col_basis, onehot, traces, spread)
+
+    def out_copy(x):
+        return pltpu.make_async_copy(out.at[x], out_hbm.at[x], sems.at[x])
+
+    sweeps(1, 3, values, coef, first, second, third, out, stores=out_copy)
+    surface(out, col_basis, onehot, traces, spread)
     raw_faces(cond, reac, raw)
 
     def layer(x, carry):
@@ -389,39 +396,49 @@
         return carry
 
     lax.fori_loop(0, XL, layer, 0, unroll=2)
-    res_copy = pltpu.make_async_copy(second.at[pl.ds(0, XL)], res_hbm, sems.at[1])
+    res_copy = pltpu.make_async_copy(second.at[pl.ds(0, XL)], res_hbm, sems.at[XL])
     res_copy.start()
     pack(odd, out, second, (send_a, send_b), (send_a, send_b), 2 * NY)
-    out_copy.wait()
+    for x in range(XL):
+        out_copy(x).wait()
     res_copy.wait()
 
 
 def sweep_2a_kernel(
-    values_hbm, res, cond_ext, reac_ext, recv_a, recv_b, placed,
-    values, coef, inv, first, second, third, out,
+    res, cond_ext, reac_ext, placed,
+    coef, inv, first, second, third,
+):
+    index, _ = position()
+    normalise(index, cond_ext, reac_ext, coef, inv)
+    start_own(res, inv, first, placed)
+    sweeps(None, -1, None, coef, first, second, third, None)
+
+
+def sweep_2b_kernel(
+    values_hbm, recv_a, recv_b, coef, first_in, second_in, third_in,
+    values, first, second, third, out,
     sems,
 ):
-    index, odd = position()
-    inner = pl.ds(1, XL - 2)
-    loads = [
+    _, odd = position()
+    edges = [
         pltpu.make_async_copy(values_hbm.at[x], values.at[x], sems.at[i])
         for i, x in enumerate((0, XL - 1))
     ]
-    loads.append(pltpu.make_async_copy(values_hbm.at[inner], values.at[inner], sems.at[2]))
-    for load in loads:
+    inner = pl.ds(1, XL - 2)
+    inner = pltpu.make_async_copy(values_hbm.at[inner], values.at[inner], sems.at[2])
+    for load in edges + [inner]:
         load.start()
-    normalise(index, cond_ext, reac_ext, coef, inv)
-    for load in loads:
+    for load in edges:
         load.wait()
-    start_own(odd, values, res, recv_a, recv_b, coef, inv, first, placed)
-    sweeps((BLOCK_2, False), values, coef, first, second, third, out)
-
-
-def sweep_2b_kernel(
-    values, recv_a, recv_b, tract_a, tract_b, coef, inv, order, col_basis,
+    start_edges(odd, values, recv_a, recv_b, coef, first)
+    sweeps(-1, 0, values, coef, first, second, third, out, loads=[inner])
+
+
+def sweep_2c_kernel(
+    values, recv_a, recv_b, tract_a, tract_b, coef, inv, onehot, col_basis,
     first_in, second_in, third_in, out_in,
     out_hbm, traces, spread, first, second, third, out,
-    onehot, sem,
+    sems,
 ):
     _, odd = position()
     recvs = (recv_a, recv_b)
@@ -429,11 +446,14 @@
         start_halo(
             h, odd, values, recvs, (recvs, 2 * NY), coef, inv, first, (tract_a, tract_b)
         )
-    sweeps((BLOCK_2, True), values, coef, first, second, third, out)
-    out_copy = pltpu.make_async_copy(out, out_hbm, sem)
-    out_copy.start()
-    surface(out, order, col_basis, onehot, traces, spread)
-    out_copy.wait()
+
+    def out_copy(x):
+        return pltpu.make_async_copy(out.at[x], out_hbm.at[x], sems.at[x])
+
+    sweeps(0, 3, values, coef, first, second, third, out, stores=out_copy)
+    surface(out, col_basis, onehot, traces, spread)
+    for x in range(XL):
+        out_copy(x).wait()
 
 
 def mask_kernel(couplings, leaf, masked):
@@ -500,8 +520,8 @@
 
 def far_1_kernel(
     gathered, masked, row_basis, nearby, order, res_hbm,
-    res, placed, send_a, send_b,
-    onehot, total, sem,
+    res, onehot, placed, send_a, send_b,
+    total, sem,
 ):
     _, odd = position()
     load = pltpu.make_async_copy(res_hbm, res, sem)
@@ -517,8 +537,11 @@
     load.wait()
 
 
-def far_2_kernel(gathered, masked, row_basis, nearby, out):
+def far_2_kernel(gathered, masked, row_basis, nearby, out_hbm, out, sem):
     far_part(gathered, masked, row_basis, nearby, out)
+    copy = pltpu.make_async_copy(out, out_hbm, sem)
+    copy.start()
+    copy.wait()
 
 
 class Hbm:
@@ -526,7 +549,7 @@
         self.value = value
 
 
-def call(kernel, outs, scratch, *operands, aliases={}):
+def call(kernel, outs, scratch, *operands, aliases={}, cost=None):
     vmem = pl.BlockSpec(memory_space=pltpu.VMEM)
     hbm = pl.BlockSpec(memory_space=pltpu.HBM)
     given = [
@@ -547,6 +570,7 @@
         out_specs=[hbm if isinstance(x, Hbm) else vmem for x in outs],
         scratch_shapes=scratch,
         input_output_aliases=aliases,
+        cost_estimate=cost,
         compiler_params=pltpu.CompilerParams(vmem_limit_bytes=24 << 20),
     )(*given)
 
@@ -554,7 +578,7 @@
 struct = jax.ShapeDtypeStruct
 FIELD = struct((XL, NY, COLS, NZ), f32)
 EXT_FIELD = struct((EXT, NY, COLS, NZ), f32)
-ONEHOT = pltpu.VMEM((SROW, SROW), bf16)
+ONEHOT = struct((SROW, SROW), bf16)
 RAW = pltpu.VMEM((7, XL, NY, NZ), f32)
 COEF = struct((6, EXT, NY, NZ), f32)
 INV = struct((1, EXT, NY, NZ), f32)
@@ -574,11 +598,11 @@
     layer = struct((XL, NY, NZ), f32)
     message = struct((2 * NY + 1, COLS, NZ), bf16)
     far_message = struct((2 * NY, COLS, NZ), bf16)
-    values, forcing_near, cond, reac, res, send_a, send_b, far_a, far_b = call(
+    values, forcing_near, cond, reac, onehot, res, send_a, send_b, far_a, far_b = call(
         first_kernel,
-        [FIELD, FIELD, layer, layer, FIELD, message, message, far_message, far_message],
+        [FIELD, FIELD, layer, layer, ONEHOT, FIELD, message, message, far_message, far_message],
         [
-            pltpu.VMEM((1, SROW), jnp.int32), pltpu.VMEM((COLS, SROW), f32), RAW, ONEHOT,
+            pltpu.VMEM((1, SROW), jnp.int32), pltpu.VMEM((COLS, SROW), f32), RAW,
             pltpu.VMEM((XL, COLS, NZ), f32), DMA((4,)), DMA((2, XL)),
         ],
         Hbm(field_start), Hbm(forcing), Hbm(traction_start), Hbm(order),
@@ -607,8 +631,8 @@
     field, res, traces, send_a, send_b, spread, *_ = call(
         sweep_1b_kernel,
         [Hbm(FIELD), Hbm(FIELD), traces_shape, message, message, spread_shape] + steps,
-        [RAW, ONEHOT, DMA((2,))],
-        values, forcing_near, cond, reac, far_a, far_b, coef, inv, order, col_basis, *state,
+        [RAW, DMA((XL + 1,))],
+        values, forcing_near, cond, reac, far_a, far_b, coef, inv, onehot, col_basis, *state,
         aliases={10 + i: 6 + i for i in range(4)},
     )
     near_a, near_b = swap(traces, traces)
@@ -618,24 +642,31 @@
         near_1_kernel, [near_shape], [window], traces, near_a, near_b, near_tiles
     )
     tract = struct((3, COLS, NZ), bf16)
-    res, placed, tract_a, tract_b = call(
+    res, onehot, placed, tract_a, tract_b = call(
         far_1_kernel,
-        [FIELD, struct((XL, COLS, NZ), f32), tract, tract],
-        [ONEHOT, pltpu.VMEM((COLS, SROW), f32), DMA],
+        [FIELD, ONEHOT, struct((XL, COLS, NZ), f32), tract, tract],
+        [pltpu.VMEM((COLS, SROW), f32), DMA],
         gathered, masked, row_basis, nearby, order, Hbm(res),
     )
     tract_a, tract_b = swap(tract_a, tract_b)
-    values, coef, inv, *state = call(
+    coef, inv, *state = call(
         sweep_2a_kernel,
-        [FIELD, COEF, INV] + steps,
+        [COEF, INV, EXT_FIELD, EXT_FIELD, EXT_FIELD],
+        [],
+        res, cond_ext, reac_ext, placed,
+    )
+    values, *state = call(
+        sweep_2b_kernel,
+        [FIELD] + steps,
         [DMA((3,))],
-        Hbm(field), res, cond_ext, reac_ext, recv_a, recv_b, placed,
+        Hbm(field), recv_a, recv_b, coef, *state,
+        aliases={4 + i: 1 + i for i in range(3)},
     )
     field, traces, spread, *_ = call(
-        sweep_2b_kernel,
+        sweep_2c_kernel,
         [Hbm(FIELD), traces_shape, spread_shape] + steps,
-        [ONEHOT, DMA],
-        values, recv_a, recv_b, tract_a, tract_b, coef, inv, order, col_basis, *state,
+        [DMA((XL,))],
+        values, recv_a, recv_b, tract_a, tract_b, coef, inv, onehot, col_basis, *state,
         aliases={9 + i: 3 + i for i in range(4)},
     )
     near_a, near_b = swap(traces, traces)
@@ -648,8 +679,8 @@
     )
     (traction,) = call(
         far_2_kernel,
-        [struct((COLS, SROW), f32)],
-        [],
+        [Hbm(struct((COLS, SROW), f32))],
+        [pltpu.VMEM((COLS, SROW), f32), DMA],
         gathered, masked, row_basis, nearby,
     )
     return field, traction

time: 118 us -> 117 us (level)
    unnamed x13 -> x12, local copies, waits for them, and re-layouts: 3.21 us -> 2.51 us
    pallas_call x10 -> x11, Pallas kernels: 35.3 us -> 35.1 us  [call(): pl.pallas_call(kernel, out_shape=[pltpu.HBM(x.value.shape, x.value.dtype)...]
where the time goes in v3:
time: 117 us
  starting transfers between devices  54.3 us (46%)
  Pallas kernels  35.1 us (30%)
  waiting for transfers between devices  23.6 us (20%)
  local copies, waits for them, and re-layouts  2.51 us (2%)
    pallas_call x11, Pallas kernels, call(): pl.pallas_call(kernel, out_shape=[pltpu.HBM(x.value.shape, x.value.dtype)...  35.1 us
    ppermute x6, starting transfers between devices, swap(): b = lax.ppermute(b, 'dev', SWAP_B)  32.2 us
    all_to_all x2, starting transfers between devices, gather(): lax.all_to_all(spread, 'dev', split_axis=0, concat_axis=0, tiled=True)  16.7 us
    ppermute x6, waiting for transfers between devices, swap(): b = lax.ppermute(b, 'dev', SWAP_B)  15.2 us
    ppermute x6, waiting for transfers between devices, swap(): a = lax.ppermute(a, 'dev', SWAP_A)  8.37 us
    ppermute x6, starting transfers between devices, swap(): a = lax.ppermute(a, 'dev', SWAP_A)  5.35 us
    unnamed x12, local copies, waits for them, and re-layouts  2.51 us
  transfers between devices with their start and end apart: 14, of which 7 were waited for; matrix products, arithmetic and copies ran while one was open for 0% of the time, Pallas kernels for 14%

profile of v3, /device:TPU:6, one launch (start us, length us, event | category | flops | bytes accessed | tf_op | source)
XLA Modules:
  0.0 116.6 jit_solution(11344874188430322978)
XLA Ops:
  0.6 0.0 copy-start.2
  0.6 5.1 %shard_map.122 = (f32[8,8,64,128]{3,2,1,0:T(8,128)S(1)}, f32[8,8,64,128]{3,2,1,0:T(8,128)S(1)}, f32[8,8,128]{2,1,0:T(8,128)S(1)}, f32[8,8,128]{2,1,0:T(8,128)S(1...) custom-call(f32[8,8,64,128]{3,2,1,0:T(8,128)} %values_hbm.1, ...), custom_call_target="tpu_custom_call" | custom-call | tf_op jit(solution)/shard_map/pallas_call | solution.py:561
  5.7 2.0 %collective-permute-start.2 = (bf16[17,64,128]{2,1,0:T(8,128)(2,1)S(1)}, bf16[17,64,128]{2,1,0:T(8,128)(2,1)S(1)}, u32[]{:S(2)}, u32[]{:S(2)}) collective-permute-start(bf16[17,64,128]{2,1,0:T(8,128)(2,1)S(1)} %get-tuple-element.51), channel_id=1, source_target_pairs={{0,1},{1,0},{2,3},{3,2},{4,5},{5,4},{6,7},{7,6},{8,9},{9,8},{10,11... | collective-permute-start | bytes 835592 | tf_op jit(solution)/shard_map/ppermute | solution.py:43
  7.7 7.1 %collective-permute-start.3 = (bf16[17,64,128]{2,1,0:T(8,128)(2,1)S(1)}, bf16[17,64,128]{2,1,0:T(8,128)(2,1)S(1)}, u32[]{:S(2)}, u32[]{:S(2)}) collective-permute-start(bf16[17,64,128]{2,1,0:T(8,128)(2,1)S(1)} %get-tuple-element.52), channel_id=1, source_target_pairs={{1,2},{3,4},{5,6},{7,8},{9,10},{11,12},{13,14},{15,16},{17,18},{19... | collective-permute-start | bytes 835592 | tf_op jit(solution)/shard_map/ppermute | solution.py:44
  14.9 0.1 collective-permute-start
  15.0 3.5 %collective-permute-start.1 = (bf16[16,64,128]{2,1,0:T(8,128)(2,1)S(1)}, bf16[16,64,128]{2,1,0:T(8,128)(2,1)S(1)}, u32[]{:S(2)}, u32[]{:S(2)}) collective-permute-start(bf16[16,64,128]{2,1,0:T(8,128)(2,1)S(1)} %get-tuple-element.49), channel_id=1, source_target_pairs={{1,2},{3,4},{5,6},{7,8},{9,10},{11,12},{13,14},{15,16},{17,18},{19... | collective-permute-start | bytes 786440 | tf_op jit(solution)/shard_map/ppermute | solution.py:44
  18.5 0.0 collective-permute-done.2.recv_a
  18.5 3.4 %collective-permute-done.3.recv_b = bf16[17,64,128]{2,1,0:T(8,128)(2,1)S(1)} collective-permute-done((bf16[17,64,128]{2,1,0:T(8,128)(2,1)S(1)}, bf16[17,64,128]{2,1,0:T(8,128)(2,1)S(1)}, u32[]{:S(2)}, u32[]{:S(2)}) %collective-permute-start.3) | collective-permute-done | bytes 278560 | tf_op jit(solution)/shard_map/ppermute | solution.py:44
  21.9 4.0 %shard_map.123 = (f32[16,8,128]{2,1,0:T(8,128)S(1)}, f32[14,8,128]{2,1,0:T(8,128)S(1)}, f32[6,14,8,128]{3,2,1,0:T(8,128)S(1)}, f32[1,14,8,128]{3,2,1,0:T(8,128)S...) custom-call(f32[8,8,64,128]{3,2,1,0:T(8,128)S(1)} %get-tuple-element, ...), custom_call_target="tpu_custom_call" | custom-call | tf_op jit(solution)/shard_map/pallas_call | solution.py:561
  25.9 0.0 collective-permute-done.far_a
  25.9 2.7 %collective-permute-done.1.far_b = bf16[16,64,128]{2,1,0:T(8,128)(2,1)S(1)} collective-permute-done((bf16[16,64,128]{2,1,0:T(8,128)(2,1)S(1)}, bf16[16,64,128]{2,1,0:T(8,128)(2,1)S(1)}, u32[]{:S(2)}, u32[]{:S(2)}) %collective-permute-start.1) | collective-permute-done | bytes 262176 | tf_op jit(solution)/shard_map/ppermute | solution.py:44
  28.6 0.0 copy-done.2
  28.6 7.2 %shard_map.124 = (f32[8,8,64,128]{3,2,1,0:T(8,128)}, f32[8,8,64,128]{3,2,1,0:T(8,128)}, bf16[64,1024]{1,0:T(8,128)(2,1)S(1)}, bf16[32,64,128]{2,1,0:T(8,128)(2,1...) custom-call(f32[8,8,64,128]{3,2,1,0:T(8,128)S(1)} %get-tuple-element, ...), custom_call_target="tpu_custom_call", output_to_operand_aliasing={{6}: (10, {}), {7}: (11, {}), {8}: (12, {}), {9}: (13, {})} | custom-call | tf_op jit(solution)/shard_map/pallas_call | solution.py:561
  35.7 9.0 %all-to-all-start = ((bf16[64,32,128]{2,1,0:T(8,128)(2,1)}), bf16[64,32,128]{2,1,0:T(8,128)(2,1)S(1)}, u32[]{:S(2)}, u32[]{:S(2)}) async-start(bf16[64,32,128]{2,1,0:T(8,128)(2,1)} %get-tuple-element.63), calls=%async_computation | async-start | bytes 1048576 | tf_op jit(solution)/shard_map/all_to_all | solution.py:589
  44.7 0.0 copy-start.3
  44.7 0.0 copy-start.4
  44.7 1.5 %collective-permute-start.4 = (bf16[32,64,128]{2,1,0:T(8,128)(2,1)}, bf16[32,64,128]{2,1,0:T(8,128)(2,1)S(1)}, u32[]{:S(2)}, u32[]{:S(2)}) collective-permute-start(bf16[32,64,128]{2,1,0:T(8,128)(2,1)} %get-tuple-element.61), channel_id=1, source_target_pairs={{0,1},{1,0},{2,3},{3,2},{4,5},{5,4},{6,7},{7,6},{8,9},{9,8},{10,11... | collective-permute-start | bytes 1572872 | tf_op jit(solution)/shard_map/ppermute | solution.py:43
  46.3 6.3 %collective-permute-start.5 = (bf16[32,64,128]{2,1,0:T(8,128)(2,1)S(1)}, bf16[32,64,128]{2,1,0:T(8,128)(2,1)S(1)}, u32[]{:S(2)}, u32[]{:S(2)}) collective-permute-start(bf16[32,64,128]{2,1,0:T(8,128)(2,1)S(1)} %get-tuple-element.62), channel_id=1, source_target_pairs={{1,2},{3,4},{5,6},{7,8},{9,10},{11,12},{13,14},{15,16},{17,18},{19... | collective-permute-start | bytes 1572872 | tf_op jit(solution)/shard_map/ppermute | solution.py:44
  52.6 0.1 collective-permute-start.6
  52.7 3.7 %collective-permute-start.7 = (bf16[64,1024]{1,0:T(8,128)(2,1)S(1)}, bf16[64,1024]{1,0:T(8,128)(2,1)S(1)}, u32[]{:S(2)}, u32[]{:S(2)}) collective-permute-start(bf16[64,1024]{1,0:T(8,128)(2,1)S(1)} %get-tuple-element.64.traces), channel_id=1, source_target_pairs={{1,2},{3,4},{5,6},{7,8},{9,10},{11,12},{13,14},{15,16},{17,18},{19... | collective-permute-start | bytes 393224 | tf_op jit(solution)/shard_map/ppermute | solution.py:44
  56.4 0.0 copy-done.1
  56.5 0.0 copy-done.5
  56.5 0.3 shard_map.125.masked
  56.8 8.3 %collective-permute-done.6.recv_a = bf16[64,1024]{1,0:T(8,128)(2,1)S(1)} collective-permute-done((bf16[64,1024]{1,0:T(8,128)(2,1)S(1)}, bf16[64,1024]{1,0:T(8,128)(2,1)S(1)}, u32[]{:S(2)}, u32[]{:S(2)}) %collective-permute-start.6) | collective-permute-done | bytes 131104 | tf_op jit(solution)/shard_map/ppermute | solution.py:43
  65.1 3.2 %collective-permute-done.7.recv_b = bf16[64,1024]{1,0:T(8,128)(2,1)S(1)} collective-permute-done((bf16[64,1024]{1,0:T(8,128)(2,1)S(1)}, bf16[64,1024]{1,0:T(8,128)(2,1)S(1)}, u32[]{:S(2)}, u32[]{:S(2)}) %collective-permute-start.7) | collective-permute-done | bytes 131104 | tf_op jit(solution)/shard_map/ppermute | solution.py:44
  68.3 2.5 %copy-done = bf16[2,512,2560]{2,1,0:T(8,128)(2,1)S(1)} copy-done((bf16[2,512,2560]{2,1,0:T(8,128)(2,1)S(1)}, bf16[2,512,2560]{2,1,0:T(8,128)(2,1)}, u32[]{:S(2)}) %copy-start) | copy-done | bytes 5242904
  70.8 1.7 %shard_map.126.nearby = f32[64,1024]{1,0:T(8,128)S(1)} custom-call(bf16[64,1024]{1,0:T(8,128)(2,1)S(1)} %get-tuple-element.64.traces, bf16[64,1024]{1,0:T(8,128)(2,1)S(1)} %collective-permute-done.6.recv_a, bf16[64,1024]{1,0:T(8,128)(2,1)S(1)} %collective-permute-done.7.recv_b, bf16[2,512,2560]{2,1,0:T(8,128)(2,1)S(1)} %copy-done), custom_call_target="tpu_custom_call" | custom-call | tf_op jit(solution)/shard_map/pallas_call | solution.py:561
  72.5 0.0 all-to-all-done.gathered
  72.5 0.0 copy-done.3
  72.5 0.0 copy-done.4
  72.5 2.0 %shard_map.127 = (f32[8,8,64,128]{3,2,1,0:T(8,128)S(1)}, bf16[1024,1024]{1,0:T(8,128)(2,1)S(1)}, f32[8,64,128]{2,1,0:T(8,128)S(1)}, bf16[3,64,128]{2,1,0:T(8,128)(2,1)S(1)}, bf16[3,64,128]{2,1,0:T(8,128)(2,1)S(1)}) custom-call(bf16[64,32,128]{2,1,0:T(8,128)(2,1)S(1)} %all-to-all-done.gathered, bf16[64,4096]{1,0:T(8,128)(2,1)S(1)} %shard_map.125.masked, ...), custom_call_target="tpu_custom_call" | custom-call | tf_op jit(solution)/shard_map/pallas_call | solution.py:561
  74.5 0.1 collective-permute-start.8
  74.6 5.1 %collective-permute-start.9 = (bf16[3,64,128]{2,1,0:T(8,128)(2,1)S(1)}, bf16[3,64,128]{2,1,0:T(8,128)(2,1)S(1)}, u32[]{:S(2)}, u32[]{:S(2)}) collective-permute-start(bf16[3,64,128]{2,1,0:T(8,128)(2,1)S(1)} %get-tuple-element.76), channel_id=1, source_target_pairs={{1,2},{3,4},{5,6},{7,8},{9,10},{11,12},{13,14},{15,16},{17,18},{19... | collective-permute-start | bytes 147464 | tf_op jit(solution)/shard_map/ppermute | solution.py:44
  79.7 1.4 %shard_map.128 = (f32[6,14,8,128]{3,2,1,0:T(8,128)S(1)}, f32[1,14,8,128]{3,2,1,0:T(8,128)S(1)}, f32[14,8,64,128]{3,2,1,0:T(8,128)S(1)}, f32[14,8,64,128]{3,2,1,0:T(8,128)S(1)}, f32[14,8,64,128]{3,2,1,0:T(8,128)S(1)}) custom-call(f32[8,8,64,128]{3,2,1,0:T(8,128)S(1)} %get-tuple-element.66.res, f32[16,8,128]{2,1,0:T(8,128)S(1)} %get-tuple-element.67.cond_ext, ...), custom_call_target="tpu_custom_call" | custom-call | tf_op jit(solution)/shard_map/pallas_call | solution.py:561
  81.1 0.0 collective-permute-done.4.recv_a
  81.2 0.0 collective-permute-done.5.recv_b
  81.2 2.3 %shard_map.129 = (f32[8,8,64,128]{3,2,1,0:T(8,128)S(1)}, f32[14,8,64,128]{3,2,1,0:T(8,128)S(1)}, f32[14,8,64,128]{3,2,1,0:T(8,128)S(1)}, f32[14,8,64,128]{3,2,1,0:T(8,128)S(1)}, f32[8,8,64,128]{3,2,1,0:T(8,128)S(1)}) custom-call(f32[8,8,64,128]{3,2,1,0:T(8,128)} %get-tuple-element.60.values_hbm, ...), custom_call_target="tpu_custom_call", output_to_operand_aliasing={{1}: (4, {}), {2}: (5, {}), {3}: (6, {})} | custom-call | tf_op jit(solution)/shard_map/pallas_call | solution.py:561
  83.5 0.0 collective-permute-done.8.tract_a
  83.5 1.3 %collective-permute-done.9.tract_b = bf16[3,64,128]{2,1,0:T(8,128)(2,1)S(1)} collective-permute-done((bf16[3,64,128]{2,1,0:T(8,128)(2,1)S(1)}, bf16[3,64,128]{2,1,0:T(8,128)(2,1)S(1)}, u32[]{:S(2)}, u32[]{:S(2)}) %collective-permute-start.9) | collective-permute-done | bytes 49184 | tf_op jit(solution)/shard_map/ppermute | solution.py:44
  84.8 5.3 %shard_map.130 = (f32[8,8,64,128]{3,2,1,0:T(8,128)}, bf16[64,1024]{1,0:T(8,128)(2,1)S(1)}, bf16[64,32,128]{2,1,0:T(8,128)(2,1)}, f32[14,8,64,128]{3,2,1,0:T(8,12...) custom-call(f32[8,8,64,128]{3,2,1,0:T(8,128)S(1)} %get-tuple-element, ...), custom_call_target="tpu_custom_call", output_to_operand_aliasing={{3}: (9, {}), {4}: (10, {}), {5}: (11, {}), {6}: (12, {})} | custom-call | tf_op jit(solution)/shard_map/pallas_call | solution.py:561
  90.1 7.8 %all-to-all-start.1 = ((bf16[64,32,128]{2,1,0:T(8,128)(2,1)}), bf16[64,32,128]{2,1,0:T(8,128)(2,1)S(1)}, u32[]{:S(2)}, u32[]{:S(2)}) async-start(bf16[64,32,128]{2,1,0:T(8,128)(2,1)} %get-tuple-element.84), calls=%async_computation.1 | async-start | bytes 1048576 | tf_op jit(solution)/shard_map/all_to_all | solution.py:589
  97.9 1.5 %collective-permute-start.10 = (bf16[64,1024]{1,0:T(8,128)(2,1)S(1)}, bf16[64,1024]{1,0:T(8,128)(2,1)S(1)}, u32[]{:S(2)}, u32[]{:S(2)}) collective-permute-start(bf16[64,1024]{1,0:T(8,128)(2,1)S(1)} %get-tuple-element.85.traces), channel_id=1, source_target_pairs={{0,1},{1,0},{2,3},{3,2},{4,5},{5,4},{6,7},{7,6},{8,9},{9,8},{10,11... | collective-permute-start | bytes 393224 | tf_op jit(solution)/shard_map/ppermute | solution.py:43
  99.4 6.3 %collective-permute-start.11 = (bf16[64,1024]{1,0:T(8,128)(2,1)S(1)}, bf16[64,1024]{1,0:T(8,128)(2,1)S(1)}, u32[]{:S(2)}, u32[]{:S(2)}) collective-permute-start(bf16[64,1024]{1,0:T(8,128)(2,1)S(1)} %get-tuple-element.85.traces), channel_id=1, source_target_pairs={{1,2},{3,4},{5,6},{7,8},{9,10},{11,12},{13,14},{15,16},{17,18},{19... | collective-permute-start | bytes 393224 | tf_op jit(solution)/shard_map/ppermute | solution.py:44
  105.8 0.1 collective-permute-done.10.recv_a
  105.8 4.7 %collective-permute-done.11.recv_b = bf16[64,1024]{1,0:T(8,128)(2,1)S(1)} collective-permute-done((bf16[64,1024]{1,0:T(8,128)(2,1)S(1)}, bf16[64,1024]{1,0:T(8,128)(2,1)S(1)}, u32[]{:S(2)}, u32[]{:S(2)}) %collective-permute-start.11) | collective-permute-done | bytes 131104 | tf_op jit(solution)/shard_map/ppermute | solution.py:44
  110.5 4.6 %shard_map.131.nearby = f32[64,1024]{1,0:T(8,128)S(1)} custom-call(bf16[64,1024]{1,0:T(8,128)(2,1)S(1)} %get-tuple-element.85.traces, bf16[64,1024]{1,0:T(8,128)(2,1)S(1)} %collective-permute-done.10.recv_a, bf16[64,1024]{1,0:T(8,128)(2,1)S(1)} %collective-permute-done.11.recv_b, bf16[2,512,2560]{2,1,0:T(8,128)(2,1)} %tiles_hbm.1), custom_call_target="tpu_custom_call" | custom-call | tf_op jit(solution)/shard_map/pallas_call | solution.py:561
  115.1 0.0 all-to-all-done.1.gathered
  115.1 1.3 %shard_map.132 = f32[64,1024]{1,0:T(8,128)} custom-call(bf16[64,32,128]{2,1,0:T(8,128)(2,1)S(1)} %all-to-all-done.1.gathered, bf16[64,4096]{1,0:T(8,128)(2,1)S(1)} %shard_map.125.masked, bf16[2,32,512]{2,1,0:T(8,128)(2,1)S(1)} %copy-done.3, f32[64,1024]{1,0:T(8,128)S(1)} %shard_map.131.nearby), custom_call_target="tpu_custom_call" | custom-call | tf_op jit(solution)/shard_map/pallas_call | solution.py:561
  (3 shorter events, 0.0 us)
Async XLA Ops:
  0.6 27.9 %copy-start.2 = (bf16[2,32,512]{2,1,0:T(8,128)(2,1)S(1)}, bf16[2,32,512]{2,1,0:T(8,128)(2,1)}, u32[]{:S(2)}) copy-start(bf16[2,32,512]{2,1,0:T(8,128)(2,1)} %col_basis.3) | copy-start | bytes 196612
  5.7 12.8 %collective-permute-start.2 = (bf16[17,64,128]{2,1,0:T(8,128)(2,1)S(1)}, bf16[17,64,128]{2,1,0:T(8,128)(2,1)S(1)}, u32[]{:S(2)}, u32[]{:S(2)}) collective-permute-start(bf16[17,64,128]{2,1,0:T(8,128)(2,1)S(1)} %get-tuple-element.51), channel_id=1, source_target_pairs={{0,1},{1,0},{2,3},{3,2},{4,5},{5,4},{6,7},{7,6},{8,9},{9,8},{10,11... | collective-permute-start | bytes 835592 | tf_op jit(solution)/shard_map/ppermute | solution.py:43
  7.7 14.2 %collective-permute-start.3 = (bf16[17,64,128]{2,1,0:T(8,128)(2,1)S(1)}, bf16[17,64,128]{2,1,0:T(8,128)(2,1)S(1)}, u32[]{:S(2)}, u32[]{:S(2)}) collective-permute-start(bf16[17,64,128]{2,1,0:T(8,128)(2,1)S(1)} %get-tuple-element.52), channel_id=1, source_target_pairs={{1,2},{3,4},{5,6},{7,8},{9,10},{11,12},{13,14},{15,16},{17,18},{19... | collective-permute-start | bytes 835592 | tf_op jit(solution)/shard_map/ppermute | solution.py:44
  14.9 11.0 %collective-permute-start = (bf16[16,64,128]{2,1,0:T(8,128)(2,1)S(1)}, bf16[16,64,128]{2,1,0:T(8,128)(2,1)S(1)}, u32[]{:S(2)}, u32[]{:S(2)}) collective-permute-start(bf16[16,64,128]{2,1,0:T(8,128)(2,1)S(1)} %get-tuple-element.48), channel_id=1, source_target_pairs={{0,1},{1,0},{2,3},{3,2},{4,5},{5,4},{6,7},{7,6},{8,9},{9,8},{10,11... | collective-permute-start | bytes 786440 | tf_op jit(solution)/shard_map/ppermute | solution.py:43
  15.0 13.6 %collective-permute-start.1 = (bf16[16,64,128]{2,1,0:T(8,128)(2,1)S(1)}, bf16[16,64,128]{2,1,0:T(8,128)(2,1)S(1)}, u32[]{:S(2)}, u32[]{:S(2)}) collective-permute-start(bf16[16,64,128]{2,1,0:T(8,128)(2,1)S(1)} %get-tuple-element.49), channel_id=1, source_target_pairs={{1,2},{3,4},{5,6},{7,8},{9,10},{11,12},{13,14},{15,16},{17,18},{19... | collective-permute-start | bytes 786440 | tf_op jit(solution)/shard_map/ppermute | solution.py:44
  28.6 27.9 %copy-start.1 = (bf16[2,32,4096]{2,1,0:T(8,128)(2,1)S(1)}, bf16[2,32,4096]{2,1,0:T(8,128)(2,1)}, u32[]{:S(2)}) copy-start(bf16[2,32,4096]{2,1,0:T(8,128)(2,1)} %param.20) | copy-start | bytes 1572868
  28.6 27.9 %copy-start.5 = (s32[2,128]{1,0:T(2,128)S(1)}, s32[2,128]{1,0:T(2,128)}, u32[]{:S(2)}) copy-start(s32[2,128]{1,0:T(2,128)} %leaf.1) | copy-start | bytes 3076
  35.7 36.7 %all-to-all-start = ((bf16[64,32,128]{2,1,0:T(8,128)(2,1)}), bf16[64,32,128]{2,1,0:T(8,128)(2,1)S(1)}, u32[]{:S(2)}, u32[]{:S(2)}) async-start(bf16[64,32,128]{2,1,0:T(8,128)(2,1)} %get-tuple-element.63), calls=%async_computation | async-start | bytes 1048576 | tf_op jit(solution)/shard_map/all_to_all | solution.py:589
  44.7 27.8 %copy-start.3 = (bf16[2,32,512]{2,1,0:T(8,128)(2,1)S(1)}, bf16[2,32,512]{2,1,0:T(8,128)(2,1)}, u32[]{:S(2)}) copy-start(bf16[2,32,512]{2,1,0:T(8,128)(2,1)} %row_basis.3) | copy-start | bytes 196612
  44.7 27.8 %copy-start.4 = (s32[1024]{0:T(1024)S(1)}, s32[1024]{0:T(1024)}, u32[]{:S(2)}) copy-start(s32[1024]{0:T(1024)} %param.16) | copy-start | bytes 12292
  44.7 36.4 %collective-permute-start.4 = (bf16[32,64,128]{2,1,0:T(8,128)(2,1)}, bf16[32,64,128]{2,1,0:T(8,128)(2,1)S(1)}, u32[]{:S(2)}, u32[]{:S(2)}) collective-permute-start(bf16[32,64,128]{2,1,0:T(8,128)(2,1)} %get-tuple-element.61), channel_id=1, source_target_pairs={{0,1},{1,0},{2,3},{3,2},{4,5},{5,4},{6,7},{7,6},{8,9},{9,8},{10,11... | collective-permute-start | bytes 1572872 | tf_op jit(solution)/shard_map/ppermute | solution.py:43
  46.3 34.9 %collective-permute-start.5 = (bf16[32,64,128]{2,1,0:T(8,128)(2,1)S(1)}, bf16[32,64,128]{2,1,0:T(8,128)(2,1)S(1)}, u32[]{:S(2)}, u32[]{:S(2)}) collective-permute-start(bf16[32,64,128]{2,1,0:T(8,128)(2,1)S(1)} %get-tuple-element.62), channel_id=1, source_target_pairs={{1,2},{3,4},{5,6},{7,8},{9,10},{11,12},{13,14},{15,16},{17,18},{19... | collective-permute-start | bytes 1572872 | tf_op jit(solution)/shard_map/ppermute | solution.py:44
  52.6 12.4 %collective-permute-start.6 = (bf16[64,1024]{1,0:T(8,128)(2,1)S(1)}, bf16[64,1024]{1,0:T(8,128)(2,1)S(1)}, u32[]{:S(2)}, u32[]{:S(2)}) collective-permute-start(bf16[64,1024]{1,0:T(8,128)(2,1)S(1)} %get-tuple-element.64.traces), channel_id=1, source_target_pairs={{0,1},{1,0},{2,3},{3,2},{4,5},{5,4},{6,7},{7,6},{8,9},{9,8},{10,11... | collective-permute-start | bytes 393224 | tf_op jit(solution)/shard_map/ppermute | solution.py:43
  52.7 15.5 %collective-permute-start.7 = (bf16[64,1024]{1,0:T(8,128)(2,1)S(1)}, bf16[64,1024]{1,0:T(8,128)(2,1)S(1)}, u32[]{:S(2)}, u32[]{:S(2)}) collective-permute-start(bf16[64,1024]{1,0:T(8,128)(2,1)S(1)} %get-tuple-element.64.traces), channel_id=1, source_target_pairs={{1,2},{3,4},{5,6},{7,8},{9,10},{11,12},{13,14},{15,16},{17,18},{19... | collective-permute-start | bytes 393224 | tf_op jit(solution)/shard_map/ppermute | solution.py:44
  68.3 2.5 %copy-start = (bf16[2,512,2560]{2,1,0:T(8,128)(2,1)S(1)}, bf16[2,512,2560]{2,1,0:T(8,128)(2,1)}, u32[]{:S(2)}) copy-start(bf16[2,512,2560]{2,1,0:T(8,128)(2,1)} %tiles_hbm.1) | copy-start | bytes 15728644
  74.5 9.0 %collective-permute-start.8 = (bf16[3,64,128]{2,1,0:T(8,128)(2,1)S(1)}, bf16[3,64,128]{2,1,0:T(8,128)(2,1)S(1)}, u32[]{:S(2)}, u32[]{:S(2)}) collective-permute-start(bf16[3,64,128]{2,1,0:T(8,128)(2,1)S(1)} %get-tuple-element.75), channel_id=1, source_target_pairs={{0,1},{1,0},{2,3},{3,2},{4,5},{5,4},{6,7},{7,6},{8,9},{9,8},{10,11... | collective-permute-start | bytes 147464 | tf_op jit(solution)/shard_map/ppermute | solution.py:43
  74.6 10.2 %collective-permute-start.9 = (bf16[3,64,128]{2,1,0:T(8,128)(2,1)S(1)}, bf16[3,64,128]{2,1,0:T(8,128)(2,1)S(1)}, u32[]{:S(2)}, u32[]{:S(2)}) collective-permute-start(bf16[3,64,128]{2,1,0:T(8,128)(2,1)S(1)} %get-tuple-element.76), channel_id=1, source_target_pairs={{1,2},{3,4},{5,6},{7,8},{9,10},{11,12},{13,14},{15,16},{17,18},{19... | collective-permute-start | bytes 147464 | tf_op jit(solution)/shard_map/ppermute | solution.py:44
  90.1 25.0 %all-to-all-start.1 = ((bf16[64,32,128]{2,1,0:T(8,128)(2,1)}), bf16[64,32,128]{2,1,0:T(8,128)(2,1)S(1)}, u32[]{:S(2)}, u32[]{:S(2)}) async-start(bf16[64,32,128]{2,1,0:T(8,128)(2,1)} %get-tuple-element.84), calls=%async_computation.1 | async-start | bytes 1048576 | tf_op jit(solution)/shard_map/all_to_all | solution.py:589
  97.9 8.0 %collective-permute-start.10 = (bf16[64,1024]{1,0:T(8,128)(2,1)S(1)}, bf16[64,1024]{1,0:T(8,128)(2,1)S(1)}, u32[]{:S(2)}, u32[]{:S(2)}) collective-permute-start(bf16[64,1024]{1,0:T(8,128)(2,1)S(1)} %get-tuple-element.85.traces), channel_id=1, source_target_pairs={{0,1},{1,0},{2,3},{3,2},{4,5},{5,4},{6,7},{7,6},{8,9},{9,8},{10,11... | collective-permute-start | bytes 393224 | tf_op jit(solution)/shard_map/ppermute | solution.py:43
  99.4 11.1 %collective-permute-start.11 = (bf16[64,1024]{1,0:T(8,128)(2,1)S(1)}, bf16[64,1024]{1,0:T(8,128)(2,1)S(1)}, u32[]{:S(2)}, u32[]{:S(2)}) collective-permute-start(bf16[64,1024]{1,0:T(8,128)(2,1)S(1)} %get-tuple-element.85.traces), channel_id=1, source_target_pairs={{1,2},{3,4},{5,6},{7,8},{9,10},{11,12},{13,14},{15,16},{17,18},{19... | collective-permute-start | bytes 393224 | tf_op jit(solution)/shard_map/ppermute | solution.py:44

commit v4 on v3

--- a/solution.py
+++ b/solution.py
@@ -140,17 +140,25 @@
         put(out, x, y, res)
 
 
-def pack(odd, values, res, sends_near, sends_far, base):
-    for near, far, right in zip(sends_near, sends_far, (odd == 0, odd != 0)):
-
-        def source(h):
-            return jnp.where(right, XL - h, h - 1)
+def pack_near(odd, values, res, sends):
+    for send, right in zip(sends, (odd == 0, odd != 0)):
+        edge = jnp.where(right, XL - 1, 0)
 
         def copy(y, carry):
-            near[y] = values[source(1), y].astype(bf16)
-            near[NY + y] = res[source(1), y].astype(bf16)
+            send[y] = values[edge, y].astype(bf16)
+            send[NY + y] = res[edge, y].astype(bf16)
+            return carry
+
+        lax.fori_loop(0, NY, copy, 0, unroll=2)
+
+
+def pack_far(odd, res, sends, base):
+    for send, right in zip(sends, (odd == 0, odd != 0)):
+
+        def copy(y, carry):
             for h in (2, 3):
-                far[base + (h - 2) * NY + y] = res[source(h), y].astype(bf16)
+                layer = jnp.where(right, XL - h, h - 1)
+                send[base + (h - 2) * NY + y] = res[layer, y].astype(bf16)
             return carry
 
         lax.fori_loop(0, NY, copy, 0, unroll=2)
@@ -172,10 +180,10 @@
     return index, lax.rem(index, 2)
 
 
-def first_kernel(
+def first_a_kernel(
     values_hbm, forcing_hbm, traction_hbm, order_hbm, cond_hbm, reac_hbm,
-    values, forcing, cond, reac, onehot, res, send_a, send_b, far_a, far_b,
-    order, traction, raw, placed, small_sems, sems,
+    values, forcing, cond, reac, onehot, placed, raw, res, send_a, send_b,
+    order, traction, small_sems, sems,
 ):
     _, odd = position()
     small = [
@@ -184,18 +192,19 @@
             ((order_hbm, order), (traction_hbm, traction), (cond_hbm, cond), (reac_hbm, reac))
         )
     ]
-    for copy in small:
+    last = XL - 1
+    layers = [
+        pltpu.make_async_copy(source.at[x], target.at[x], sems.at[i])
+        for i, (source, target, x) in enumerate(
+            (
+                (values_hbm, values, 0), (values_hbm, values, 1), (forcing_hbm, forcing, 0),
+                (values_hbm, values, last), (values_hbm, values, last - 1),
+                (forcing_hbm, forcing, last),
+            )
+        )
+    ]
+    for copy in small + layers:
         copy.start()
-
-    def layer_copies(x):
-        return (
-            pltpu.make_async_copy(values_hbm.at[x], values.at[x], sems.at[0, x]),
-            pltpu.make_async_copy(forcing_hbm.at[x], forcing.at[x], sems.at[1, x]),
-        )
-
-    for x in range(XL):
-        for copy in layer_copies(x):
-            copy.start()
     small[0].wait()
     build_onehot(order, onehot)
     small[1].wait()
@@ -206,20 +215,46 @@
     small[3].wait()
     raw_faces(cond, reac, raw)
     pack_coefficients(odd, cond, reac, send_a, send_b)
-    for copy in layer_copies(0):
+    for copy in layers:
         copy.wait()
 
+    def layer(i, carry):
+        residual_layer(i * last, values, forcing, raw, res, placed)
+        return carry
+
+    lax.fori_loop(0, 2, layer, 0, unroll=2)
+    pack_near(odd, values, res, (send_a, send_b))
+
+
+def first_b_kernel(
+    values_hbm, forcing_hbm, placed, raw, values_in, forcing_in, res_in,
+    values, forcing, res, far_a, far_b,
+    sems,
+):
+    _, odd = position()
+
+    def values_copy(x):
+        return pltpu.make_async_copy(values_hbm.at[x], values.at[x], sems.at[0, x])
+
+    def forcing_copy(x):
+        return pltpu.make_async_copy(forcing_hbm.at[x], forcing.at[x], sems.at[1, x])
+
+    for x in range(1, XL - 1):
+        if x < XL - 3:
+            values_copy(x + 1).start()
+        forcing_copy(x).start()
+
     def layer(x, carry):
-        @pl.when(x < XL - 1)
+        @pl.when(x < XL - 3)
         def _():
-            for copy in layer_copies(x + 1):
-                copy.wait()
-
+            values_copy(x + 1).wait()
+
+        forcing_copy(x).wait()
         residual_layer(x, values, forcing, raw, res, placed)
         return carry
 
-    lax.fori_loop(0, XL, layer, 0)
-    pack(odd, values, res, (send_a, send_b), (far_a, far_b), 0)
+    lax.fori_loop(1, XL - 1, layer, 0)
+    pack_far(odd, res, (far_a, far_b), 0)
 
 
 def sides_of(odd, recv_a, recv_b):
@@ -375,10 +410,10 @@
 
 
 def sweep_1b_kernel(
-    values, forcing, cond, reac, far_a, far_b, coef, inv, onehot, col_basis,
+    values, forcing, raw, far_a, far_b, coef, inv, onehot, col_basis,
     first_in, second_in, third_in, out_in,
     out_hbm, res_hbm, traces, send_a, send_b, spread, first, second, third, out,
-    raw, sems,
+    sems,
 ):
     _, odd = position()
     for h in (2, 3):
@@ -389,7 +424,6 @@
 
     sweeps(1, 3, values, coef, first, second, third, out, stores=out_copy)
     surface(out, col_basis, onehot, traces, spread)
-    raw_faces(cond, reac, raw)
 
     def layer(x, carry):
         residual_layer(x, out, forcing, raw, second, None)
@@ -398,7 +432,8 @@
     lax.fori_loop(0, XL, layer, 0, unroll=2)
     res_copy = pltpu.make_async_copy(second.at[pl.ds(0, XL)], res_hbm, sems.at[XL])
     res_copy.start()
-    pack(odd, out, second, (send_a, send_b), (send_a, send_b), 2 * NY)
+    pack_near(odd, out, second, (send_a, send_b))
+    pack_far(odd, second, (send_a, send_b), 2 * NY)
     for x in range(XL):
         out_copy(x).wait()
     res_copy.wait()
@@ -468,9 +503,6 @@
         masked[c * RANK : (c + 1) * RANK, :] = (rows * weights).astype(bf16)
 
 
-NEAR_CHUNK = 256
-
-
 def near_windows(traces, recv_a, recv_b, window):
     _, odd = position()
     window[1] = traces[...]
@@ -489,21 +521,53 @@
         out[:, c * CLUSTER : (c + 1) * CLUSTER] = dot(wide[c], tiles[c], NT)
 
 
-def near_2_kernel(traces, recv_a, recv_b, tiles_hbm, out, window, tiles, sems):
-    chunks = [
-        pltpu.make_async_copy(
-            tiles_hbm.at[i // 2, pl.ds((i % 2) * NEAR_CHUNK, NEAR_CHUNK), :],
-            tiles.at[i],
-            sems.at[i],
+def add_side(side, tiles, out, right):
+    if right:
+        out[:, :CLUSTER] += dot(side[:, :CLUSTER], tiles[0, :, 4 * CLUSTER :], NT)
+        out[:, CLUSTER:] += dot(side[...], tiles[1, :, 3 * CLUSTER :], NT)
+    else:
+        out[:, :CLUSTER] += dot(side[...], tiles[0, :, : 2 * CLUSTER], NT)
+        out[:, CLUSTER:] += dot(side[:, CLUSTER:], tiles[1, :, :CLUSTER], NT)
+
+
+def near_2a_kernel(traces, recv_a, tiles_hbm, out, tiles, sems):
+    _, odd = position()
+    half = CLUSTER // 2
+    chunks = []
+    for i in range(4):
+        rows = pl.ds((i % 2) * half, half)
+        chunks.append(
+            pltpu.make_async_copy(
+                tiles_hbm.at[i // 2, rows, :], tiles.at[i // 2, rows, :], sems.at[i]
+            )
         )
-        for i in range(4)
-    ]
     for chunk in chunks:
         chunk.start()
-    wide = near_windows(traces, recv_a, recv_b, window)
     for i, chunk in enumerate(chunks):
         chunk.wait()
-        out[:, i * NEAR_CHUNK : (i + 1) * NEAR_CHUNK] = dot(wide[i // 2], tiles[i], NT)
+        c, k = i // 2, i % 2
+        own = tiles[c, k * half : (k + 1) * half, (2 - c) * CLUSTER : (4 - c) * CLUSTER]
+        out[:, i * half : (i + 1) * half] = dot(traces[...], own, NT)
+
+    @pl.when(odd == 0)
+    def _():
+        add_side(recv_a, tiles, out, True)
+
+    @pl.when(odd != 0)
+    def _():
+        add_side(recv_a, tiles, out, False)
+
+
+def near_2b_kernel(recv_b, tiles, nearby, out):
+    _, odd = position()
+
+    @pl.when(odd == 0)
+    def _():
+        add_side(recv_b, tiles, out, False)
+
+    @pl.when(odd != 0)
+    def _():
+        add_side(recv_b, tiles, out, True)
 
 
 def far_part(gathered, masked, row_basis, nearby, out):
@@ -579,7 +643,7 @@
 FIELD = struct((XL, NY, COLS, NZ), f32)
 EXT_FIELD = struct((EXT, NY, COLS, NZ), f32)
 ONEHOT = struct((SROW, SROW), bf16)
-RAW = pltpu.VMEM((7, XL, NY, NZ), f32)
+RAW = struct((7, XL, NY, NZ), f32)
 COEF = struct((6, EXT, NY, NZ), f32)
 INV = struct((1, EXT, NY, NZ), f32)
 DMA = pltpu.SemaphoreType.DMA
@@ -598,17 +662,22 @@
     layer = struct((XL, NY, NZ), f32)
     message = struct((2 * NY + 1, COLS, NZ), bf16)
     far_message = struct((2 * NY, COLS, NZ), bf16)
-    values, forcing_near, cond, reac, onehot, res, send_a, send_b, far_a, far_b = call(
-        first_kernel,
-        [FIELD, FIELD, layer, layer, ONEHOT, FIELD, message, message, far_message, far_message],
-        [
-            pltpu.VMEM((1, SROW), jnp.int32), pltpu.VMEM((COLS, SROW), f32), RAW,
-            pltpu.VMEM((XL, COLS, NZ), f32), DMA((4,)), DMA((2, XL)),
-        ],
+    placed_shape = struct((XL, COLS, NZ), f32)
+    values, forcing_near, cond, reac, onehot, placed, raw, res, send_a, send_b = call(
+        first_a_kernel,
+        [FIELD, FIELD, layer, layer, ONEHOT, placed_shape, RAW, FIELD, message, message],
+        [pltpu.VMEM((1, SROW), jnp.int32), pltpu.VMEM((COLS, SROW), f32), DMA((4,)), DMA((6,))],
         Hbm(field_start), Hbm(forcing), Hbm(traction_start), Hbm(order),
         Hbm(conductivity), Hbm(reaction),
     )
     recv_a, recv_b = swap(send_a, send_b)
+    values, forcing_near, res, far_a, far_b = call(
+        first_b_kernel,
+        [FIELD, FIELD, FIELD, far_message, far_message],
+        [DMA((2, XL))],
+        Hbm(field_start), Hbm(forcing), placed, raw, values, forcing_near, res,
+        aliases={4: 0, 5: 1, 6: 2},
+    )
     far_a, far_b = swap(far_a, far_b)
     (masked,) = call(
         mask_kernel,
@@ -631,9 +700,9 @@
     field, res, traces, send_a, send_b, spread, *_ = call(
         sweep_1b_kernel,
         [Hbm(FIELD), Hbm(FIELD), traces_shape, message, message, spread_shape] + steps,
-        [RAW, DMA((XL + 1,))],
-        values, forcing_near, cond, reac, far_a, far_b, coef, inv, onehot, col_basis, *state,
-        aliases={10 + i: 6 + i for i in range(4)},
+        [DMA((XL + 1,))],
+        values, forcing_near, raw, far_a, far_b, coef, inv, onehot, col_basis, *state,
+        aliases={9 + i: 6 + i for i in range(4)},
     )
     near_a, near_b = swap(traces, traces)
     gathered = gather(spread)
@@ -671,11 +740,14 @@
     )
     near_a, near_b = swap(traces, traces)
     gathered = gather(spread)
+    nearby, tiles = call(
+        near_2a_kernel,
+        [near_shape, struct((2, CLUSTER, 5 * CLUSTER), bf16)],
+        [DMA((4,))],
+        traces, near_a, Hbm(near_tiles),
+    )
     (nearby,) = call(
-        near_2_kernel,
-        [near_shape],
-        [window, pltpu.VMEM((4, NEAR_CHUNK, 5 * CLUSTER), bf16), DMA((4,))],
-        traces, near_a, near_b, Hbm(near_tiles),
+        near_2b_kernel, [near_shape], [], near_b, tiles, nearby, aliases={2: 0}
     )
     (traction,) = call(
         far_2_kernel,

time: 117 us -> 110 us (0.940)
  waiting for transfers between devices: 23.6 us -> 20 us
  starting transfers between devices: 54.3 us -> 51.5 us
    ppermute x6, waiting for transfers between devices: 15.2 us -> 11.9 us  [swap(): b = lax.ppermute(b, 'dev', SWAP_B)]
    all_to_all x2, starting transfers between devices: 16.7 us -> 14 us  [gather(): lax.all_to_all(spread, 'dev', split_axis=0, concat_axis=0, tiled=True)]
    pallas_call x11 -> x13, Pallas kernels: 35.1 us -> 34.7 us  [call(): pl.pallas_call(kernel, out_shape=[pltpu.HBM(x.value.shape, x.value.dtype)...]
  transfers between devices with their start and end apart: 14 -> 14, of which waited for: 7 -> 6; matrix products, arithmetic and copies ran while one was open for 0% -> 0% of each run, Pallas kernels for 14% -> 17%
where the time goes in v4:
time: 110 us
  starting transfers between devices  51.5 us (47%)
  Pallas kernels  34.7 us (32%)
  waiting for transfers between devices  20 us (18%)
  local copies, waits for them, and re-layouts  2.51 us (2%)
    pallas_call x13, Pallas kernels, call(): pl.pallas_call(kernel, out_shape=[pltpu.HBM(x.value.shape, x.value.dtype)...  34.7 us
    ppermute x6, starting transfers between devices, swap(): b = lax.ppermute(b, 'dev', SWAP_B)  32.1 us
    all_to_all x2, starting transfers between devices, gather(): lax.all_to_all(spread, 'dev', split_axis=0, concat_axis=0, tiled=True)  14 us
    ppermute x6, waiting for transfers between devices, swap(): b = lax.ppermute(b, 'dev', SWAP_B)  11.9 us
    ppermute x6, waiting for transfers between devices, swap(): a = lax.ppermute(a, 'dev', SWAP_A)  8.06 us
    ppermute x6, starting transfers between devices, swap(): a = lax.ppermute(a, 'dev', SWAP_A)  5.36 us
    unnamed x12, local copies, waits for them, and re-layouts  2.51 us
  transfers between devices with their start and end apart: 14, of which 6 were waited for; matrix products, arithmetic and copies ran while one was open for 0% of the time, Pallas kernels for 17%

profile of v4, /device:TPU:6, one launch (start us, length us, event | category | flops | bytes accessed | tf_op | source)
XLA Modules:
  0.0 109.7 jit_solution(6416612509983676649)
XLA Ops:
  0.6 2.7 %shard_map.122 = (f32[8,8,64,128]{3,2,1,0:T(8,128)S(1)}, f32[8,8,64,128]{3,2,1,0:T(8,128)S(1)}, f32[8,8,128]{2,1,0:T(8,128)S(1)}, f32[8,8,128]{2,1,0:T(8,128)S(1...) custom-call(f32[8,8,64,128]{3,2,1,0:T(8,128)} %values_hbm.3, ...), custom_call_target="tpu_custom_call" | custom-call | tf_op jit(solution)/shard_map/pallas_call | solution.py:625
  3.3 2.0 %collective-permute-start.2 = (bf16[17,64,128]{2,1,0:T(8,128)(2,1)S(1)}, bf16[17,64,128]{2,1,0:T(8,128)(2,1)S(1)}, u32[]{:S(2)}, u32[]{:S(2)}) collective-permute-start(bf16[17,64,128]{2,1,0:T(8,128)(2,1)S(1)} %get-tuple-element.63), channel_id=1, source_target_pairs={{0,1},{1,0},{2,3},{3,2},{4,5},{5,4},{6,7},{7,6},{8,9},{9,8},{10,11... | collective-permute-start | bytes 835592 | tf_op jit(solution)/shard_map/ppermute | solution.py:43
  5.3 7.1 %collective-permute-start.3 = (bf16[17,64,128]{2,1,0:T(8,128)(2,1)S(1)}, bf16[17,64,128]{2,1,0:T(8,128)(2,1)S(1)}, u32[]{:S(2)}, u32[]{:S(2)}) collective-permute-start(bf16[17,64,128]{2,1,0:T(8,128)(2,1)S(1)} %get-tuple-element.64), channel_id=1, source_target_pairs={{1,2},{3,4},{5,6},{7,8},{9,10},{11,12},{13,14},{15,16},{17,18},{19... | collective-permute-start | bytes 835592 | tf_op jit(solution)/shard_map/ppermute | solution.py:44
  12.5 2.6 %shard_map.123 = (f32[8,8,64,128]{3,2,1,0:T(8,128)S(1)}, f32[8,8,64,128]{3,2,1,0:T(8,128)S(1)}, f32[8,8,64,128]{3,2,1,0:T(8,128)S(1)}, bf16[16,64,128]{2,1,0:T(8,128)(2,1)S(1)}, bf16[16,64,128]{2,1,0:T(8,128)(2,1)S(1)}) custom-call(f32[8,8,64,128]{3,2,1,0:T(8,128)} %values_hbm.3, ...), custom_call_target="tpu_custom_call", output_to_operand_aliasing={{0}: (4, {}), {1}: (5, {}), {2}: (6, {})} | custom-call | tf_op jit(solution)/shard_map/pallas_call | solution.py:625
  15.1 0.1 collective-permute-start
  15.2 3.5 %collective-permute-start.1 = (bf16[16,64,128]{2,1,0:T(8,128)(2,1)S(1)}, bf16[16,64,128]{2,1,0:T(8,128)(2,1)S(1)}, u32[]{:S(2)}, u32[]{:S(2)}) collective-permute-start(bf16[16,64,128]{2,1,0:T(8,128)(2,1)S(1)} %get-tuple-element.59), channel_id=1, source_target_pairs={{1,2},{3,4},{5,6},{7,8},{9,10},{11,12},{13,14},{15,16},{17,18},{19... | collective-permute-start | bytes 786440 | tf_op jit(solution)/shard_map/ppermute | solution.py:44
  18.7 0.0 collective-permute-done.2.recv_a
  18.7 0.8 collective-permute-done.3.recv_b
  19.5 4.0 %shard_map.124 = (f32[16,8,128]{2,1,0:T(8,128)S(1)}, f32[14,8,128]{2,1,0:T(8,128)S(1)}, f32[6,14,8,128]{3,2,1,0:T(8,128)S(1)}, f32[1,14,8,128]{3,2,1,0:T(8,128)S...) custom-call(f32[8,8,64,128]{3,2,1,0:T(8,128)S(1)} %get-tuple-element, ...), custom_call_target="tpu_custom_call" | custom-call | tf_op jit(solution)/shard_map/pallas_call | solution.py:625
  23.5 0.0 collective-permute-done.far_a
  23.5 5.3 %collective-permute-done.1.far_b = bf16[16,64,128]{2,1,0:T(8,128)(2,1)S(1)} collective-permute-done((bf16[16,64,128]{2,1,0:T(8,128)(2,1)S(1)}, bf16[16,64,128]{2,1,0:T(8,128)(2,1)S(1)}, u32[]{:S(2)}, u32[]{:S(2)}) %collective-permute-start.1) | collective-permute-done | bytes 262176 | tf_op jit(solution)/shard_map/ppermute | solution.py:44
  28.8 0.0 copy-done.2
  28.8 7.0 %shard_map.125 = (f32[8,8,64,128]{3,2,1,0:T(8,128)}, f32[8,8,64,128]{3,2,1,0:T(8,128)}, bf16[64,1024]{1,0:T(8,128)(2,1)S(1)}, bf16[32,64,128]{2,1,0:T(8,128)(2,1...) custom-call(f32[8,8,64,128]{3,2,1,0:T(8,128)S(1)} %get-tuple-element, ...), custom_call_target="tpu_custom_call", output_to_operand_aliasing={{6}: (9, {}), {7}: (10, {}), {8}: (11, {}), {9}: (12, {})} | custom-call | tf_op jit(solution)/shard_map/pallas_call | solution.py:625
  35.8 6.3 %all-to-all-start = ((bf16[64,32,128]{2,1,0:T(8,128)(2,1)}), bf16[64,32,128]{2,1,0:T(8,128)(2,1)S(1)}, u32[]{:S(2)}, u32[]{:S(2)}) async-start(bf16[64,32,128]{2,1,0:T(8,128)(2,1)} %get-tuple-element.75), calls=%async_computation | async-start | bytes 1048576 | tf_op jit(solution)/shard_map/all_to_all | solution.py:653
  42.2 1.5 %collective-permute-start.4 = (bf16[32,64,128]{2,1,0:T(8,128)(2,1)}, bf16[32,64,128]{2,1,0:T(8,128)(2,1)S(1)}, u32[]{:S(2)}, u32[]{:S(2)}) collective-permute-start(bf16[32,64,128]{2,1,0:T(8,128)(2,1)} %get-tuple-element.73), channel_id=1, source_target_pairs={{0,1},{1,0},{2,3},{3,2},{4,5},{5,4},{6,7},{7,6},{8,9},{9,8},{10,11... | collective-permute-start | bytes 1572872 | tf_op jit(solution)/shard_map/ppermute | solution.py:43
  43.7 6.3 %collective-permute-start.5 = (bf16[32,64,128]{2,1,0:T(8,128)(2,1)S(1)}, bf16[32,64,128]{2,1,0:T(8,128)(2,1)S(1)}, u32[]{:S(2)}, u32[]{:S(2)}) collective-permute-start(bf16[32,64,128]{2,1,0:T(8,128)(2,1)S(1)} %get-tuple-element.74), channel_id=1, source_target_pairs={{1,2},{3,4},{5,6},{7,8},{9,10},{11,12},{13,14},{15,16},{17,18},{19... | collective-permute-start | bytes 1572872 | tf_op jit(solution)/shard_map/ppermute | solution.py:44
  50.1 0.1 collective-permute-start.6
  50.2 3.7 %collective-permute-start.7 = (bf16[64,1024]{1,0:T(8,128)(2,1)S(1)}, bf16[64,1024]{1,0:T(8,128)(2,1)S(1)}, u32[]{:S(2)}, u32[]{:S(2)}) collective-permute-start(bf16[64,1024]{1,0:T(8,128)(2,1)S(1)} %get-tuple-element.76.traces), channel_id=1, source_target_pairs={{1,2},{3,4},{5,6},{7,8},{9,10},{11,12},{13,14},{15,16},{17,18},{19... | collective-permute-start | bytes 393224 | tf_op jit(solution)/shard_map/ppermute | solution.py:44
  53.9 0.0 copy-done.1
  53.9 0.0 copy-start.3
  53.9 0.0 copy-start.4
  53.9 0.3 shard_map.126.masked
  54.2 8.0 %collective-permute-done.6.recv_a = bf16[64,1024]{1,0:T(8,128)(2,1)S(1)} collective-permute-done((bf16[64,1024]{1,0:T(8,128)(2,1)S(1)}, bf16[64,1024]{1,0:T(8,128)(2,1)S(1)}, u32[]{:S(2)}, u32[]{:S(2)}) %collective-permute-start.6) | collective-permute-done | bytes 131104 | tf_op jit(solution)/shard_map/ppermute | solution.py:43
  62.2 3.3 %collective-permute-done.7.recv_b = bf16[64,1024]{1,0:T(8,128)(2,1)S(1)} collective-permute-done((bf16[64,1024]{1,0:T(8,128)(2,1)S(1)}, bf16[64,1024]{1,0:T(8,128)(2,1)S(1)}, u32[]{:S(2)}, u32[]{:S(2)}) %collective-permute-start.7) | collective-permute-done | bytes 131104 | tf_op jit(solution)/shard_map/ppermute | solution.py:44
  65.5 2.5 %copy-done = bf16[2,512,2560]{2,1,0:T(8,128)(2,1)S(1)} copy-done((bf16[2,512,2560]{2,1,0:T(8,128)(2,1)S(1)}, bf16[2,512,2560]{2,1,0:T(8,128)(2,1)}, u32[]{:S(2)}) %copy-start) | copy-done | bytes 5242904
  68.0 1.7 %shard_map.127.nearby = f32[64,1024]{1,0:T(8,128)S(1)} custom-call(bf16[64,1024]{1,0:T(8,128)(2,1)S(1)} %get-tuple-element.76.traces, bf16[64,1024]{1,0:T(8,128)(2,1)S(1)} %collective-permute-done.6.recv_a, bf16[64,1024]{1,0:T(8,128)(2,1)S(1)} %collective-permute-done.7.recv_b, bf16[2,512,2560]{2,1,0:T(8,128)(2,1)S(1)} %copy-done), custom_call_target="tpu_custom_call" | custom-call | tf_op jit(solution)/shard_map/pallas_call | solution.py:625
  69.7 0.0 all-to-all-done.gathered
  69.7 0.0 copy-done.3
  69.7 0.0 copy-done.4
  69.7 2.0 %shard_map.128 = (f32[8,8,64,128]{3,2,1,0:T(8,128)S(1)}, bf16[1024,1024]{1,0:T(8,128)(2,1)S(1)}, f32[8,64,128]{2,1,0:T(8,128)S(1)}, bf16[3,64,128]{2,1,0:T(8,128)(2,1)S(1)}, bf16[3,64,128]{2,1,0:T(8,128)(2,1)S(1)}) custom-call(bf16[64,32,128]{2,1,0:T(8,128)(2,1)S(1)} %all-to-all-done.gathered, bf16[64,4096]{1,0:T(8,128)(2,1)S(1)} %shard_map.126.masked, ...), custom_call_target="tpu_custom_call" | custom-call | tf_op jit(solution)/shard_map/pallas_call | solution.py:625
  71.7 0.1 collective-permute-start.8
  71.8 5.1 %collective-permute-start.9 = (bf16[3,64,128]{2,1,0:T(8,128)(2,1)S(1)}, bf16[3,64,128]{2,1,0:T(8,128)(2,1)S(1)}, u32[]{:S(2)}, u32[]{:S(2)}) collective-permute-start(bf16[3,64,128]{2,1,0:T(8,128)(2,1)S(1)} %get-tuple-element.88), channel_id=1, source_target_pairs={{1,2},{3,4},{5,6},{7,8},{9,10},{11,12},{13,14},{15,16},{17,18},{19... | collective-permute-start | bytes 147464 | tf_op jit(solution)/shard_map/ppermute | solution.py:44
  76.8 1.4 %shard_map.129 = (f32[6,14,8,128]{3,2,1,0:T(8,128)S(1)}, f32[1,14,8,128]{3,2,1,0:T(8,128)S(1)}, f32[14,8,64,128]{3,2,1,0:T(8,128)S(1)}, f32[14,8,64,128]{3,2,1,0:T(8,128)S(1)}, f32[14,8,64,128]{3,2,1,0:T(8,128)S(1)}) custom-call(f32[8,8,64,128]{3,2,1,0:T(8,128)S(1)} %get-tuple-element.78.res, f32[16,8,128]{2,1,0:T(8,128)S(1)} %get-tuple-element.79.cond_ext, ...), custom_call_target="tpu_custom_call" | custom-call | tf_op jit(solution)/shard_map/pallas_call | solution.py:625
  78.3 0.0 collective-permute-done.4.recv_a
  78.3 0.0 collective-permute-done.5.recv_b
  78.3 2.3 %shard_map.130 = (f32[8,8,64,128]{3,2,1,0:T(8,128)S(1)}, f32[14,8,64,128]{3,2,1,0:T(8,128)S(1)}, f32[14,8,64,128]{3,2,1,0:T(8,128)S(1)}, f32[14,8,64,128]{3,2,1,0:T(8,128)S(1)}, f32[8,8,64,128]{3,2,1,0:T(8,128)S(1)}) custom-call(f32[8,8,64,128]{3,2,1,0:T(8,128)} %get-tuple-element.72.values_hbm, ...), custom_call_target="tpu_custom_call", output_to_operand_aliasing={{1}: (4, {}), {2}: (5, {}), {3}: (6, {})} | custom-call | tf_op jit(solution)/shard_map/pallas_call | solution.py:625
  80.6 0.0 collective-permute-done.8.tract_a
  80.6 1.4 %collective-permute-done.9.tract_b = bf16[3,64,128]{2,1,0:T(8,128)(2,1)S(1)} collective-permute-done((bf16[3,64,128]{2,1,0:T(8,128)(2,1)S(1)}, bf16[3,64,128]{2,1,0:T(8,128)(2,1)S(1)}, u32[]{:S(2)}, u32[]{:S(2)}) %collective-permute-start.9) | collective-permute-done | bytes 49184 | tf_op jit(solution)/shard_map/ppermute | solution.py:44
  82.0 5.3 %shard_map.131 = (f32[8,8,64,128]{3,2,1,0:T(8,128)}, bf16[64,1024]{1,0:T(8,128)(2,1)S(1)}, bf16[64,32,128]{2,1,0:T(8,128)(2,1)}, f32[14,8,64,128]{3,2,1,0:T(8,12...) custom-call(f32[8,8,64,128]{3,2,1,0:T(8,128)S(1)} %get-tuple-element, ...), custom_call_target="tpu_custom_call", output_to_operand_aliasing={{3}: (9, {}), {4}: (10, {}), {5}: (11, {}), {6}: (12, {})} | custom-call | tf_op jit(solution)/shard_map/pallas_call | solution.py:625
  87.3 7.7 %all-to-all-start.1 = ((bf16[64,32,128]{2,1,0:T(8,128)(2,1)}), bf16[64,32,128]{2,1,0:T(8,128)(2,1)S(1)}, u32[]{:S(2)}, u32[]{:S(2)}) async-start(bf16[64,32,128]{2,1,0:T(8,128)(2,1)} %get-tuple-element.96), calls=%async_computation.1 | async-start | bytes 1048576 | tf_op jit(solution)/shard_map/all_to_all | solution.py:653
  95.0 1.5 %collective-permute-start.11 = (bf16[64,1024]{1,0:T(8,128)(2,1)S(1)}, bf16[64,1024]{1,0:T(8,128)(2,1)S(1)}, u32[]{:S(2)}, u32[]{:S(2)}) collective-permute-start(bf16[64,1024]{1,0:T(8,128)(2,1)S(1)} %get-tuple-element.97.traces), channel_id=1, source_target_pairs={{0,1},{1,0},{2,3},{3,2},{4,5},{5,4},{6,7},{7,6},{8,9},{9,8},{10,11... | collective-permute-start | bytes 393224 | tf_op jit(solution)/shard_map/ppermute | solution.py:43
  96.6 6.3 %collective-permute-start.10 = (bf16[64,1024]{1,0:T(8,128)(2,1)S(1)}, bf16[64,1024]{1,0:T(8,128)(2,1)S(1)}, u32[]{:S(2)}, u32[]{:S(2)}) collective-permute-start(bf16[64,1024]{1,0:T(8,128)(2,1)S(1)} %get-tuple-element.97.traces), channel_id=1, source_target_pairs={{1,2},{3,4},{5,6},{7,8},{9,10},{11,12},{13,14},{15,16},{17,18},{19... | collective-permute-start | bytes 393224 | tf_op jit(solution)/shard_map/ppermute | solution.py:44
  102.9 0.0 collective-permute-done.11.recv_a
  103.0 3.5 %shard_map.132 = (f32[64,1024]{1,0:T(8,128)S(1)}, bf16[2,512,2560]{2,1,0:T(8,128)(2,1)S(1)}) custom-call(bf16[64,1024]{1,0:T(8,128)(2,1)S(1)} %get-tuple-element.97.traces, bf16[64,1024]{1,0:T(8,128)(2,1)S(1)} %collective-permute-done.11.recv_a, bf16[2,512,2560]{2,1,0:T(8,128)(2,1)} %tiles_hbm.1), custom_call_target="tpu_custom_call" | custom-call | tf_op jit(solution)/shard_map/pallas_call | solution.py:625
  106.5 1.2 %collective-permute-done.10.recv_b = bf16[64,1024]{1,0:T(8,128)(2,1)S(1)} collective-permute-done((bf16[64,1024]{1,0:T(8,128)(2,1)S(1)}, bf16[64,1024]{1,0:T(8,128)(2,1)S(1)}, u32[]{:S(2)}, u32[]{:S(2)}) %collective-permute-start.10) | collective-permute-done | bytes 131104 | tf_op jit(solution)/shard_map/ppermute | solution.py:44
  107.6 0.6 shard_map.133.nearby
  108.2 0.0 all-to-all-done.1.gathered
  108.2 1.3 %shard_map.134 = f32[64,1024]{1,0:T(8,128)} custom-call(bf16[64,32,128]{2,1,0:T(8,128)(2,1)S(1)} %all-to-all-done.1.gathered, bf16[64,4096]{1,0:T(8,128)(2,1)S(1)} %shard_map.126.masked, bf16[2,32,512]{2,1,0:T(8,128)(2,1)S(1)} %copy-done.3, f32[64,1024]{1,0:T(8,128)S(1)} %shard_map.133.nearby), custom_call_target="tpu_custom_call" | custom-call | tf_op jit(solution)/shard_map/pallas_call | solution.py:625
  (5 shorter events, 0.0 us)
Async XLA Ops:
  3.3 15.4 %collective-permute-start.2 = (bf16[17,64,128]{2,1,0:T(8,128)(2,1)S(1)}, bf16[17,64,128]{2,1,0:T(8,128)(2,1)S(1)}, u32[]{:S(2)}, u32[]{:S(2)}) collective-permute-start(bf16[17,64,128]{2,1,0:T(8,128)(2,1)S(1)} %get-tuple-element.63), channel_id=1, source_target_pairs={{0,1},{1,0},{2,3},{3,2},{4,5},{5,4},{6,7},{7,6},{8,9},{9,8},{10,11... | collective-permute-start | bytes 835592 | tf_op jit(solution)/shard_map/ppermute | solution.py:43
  5.3 14.2 %collective-permute-start.3 = (bf16[17,64,128]{2,1,0:T(8,128)(2,1)S(1)}, bf16[17,64,128]{2,1,0:T(8,128)(2,1)S(1)}, u32[]{:S(2)}, u32[]{:S(2)}) collective-permute-start(bf16[17,64,128]{2,1,0:T(8,128)(2,1)S(1)} %get-tuple-element.64), channel_id=1, source_target_pairs={{1,2},{3,4},{5,6},{7,8},{9,10},{11,12},{13,14},{15,16},{17,18},{19... | collective-permute-start | bytes 835592 | tf_op jit(solution)/shard_map/ppermute | solution.py:44
  15.1 8.4 %collective-permute-start = (bf16[16,64,128]{2,1,0:T(8,128)(2,1)S(1)}, bf16[16,64,128]{2,1,0:T(8,128)(2,1)S(1)}, u32[]{:S(2)}, u32[]{:S(2)}) collective-permute-start(bf16[16,64,128]{2,1,0:T(8,128)(2,1)S(1)} %get-tuple-element.58), channel_id=1, source_target_pairs={{0,1},{1,0},{2,3},{3,2},{4,5},{5,4},{6,7},{7,6},{8,9},{9,8},{10,11... | collective-permute-start | bytes 786440 | tf_op jit(solution)/shard_map/ppermute | solution.py:43
  15.2 13.6 %collective-permute-start.1 = (bf16[16,64,128]{2,1,0:T(8,128)(2,1)S(1)}, bf16[16,64,128]{2,1,0:T(8,128)(2,1)S(1)}, u32[]{:S(2)}, u32[]{:S(2)}) collective-permute-start(bf16[16,64,128]{2,1,0:T(8,128)(2,1)S(1)} %get-tuple-element.59), channel_id=1, source_target_pairs={{1,2},{3,4},{5,6},{7,8},{9,10},{11,12},{13,14},{15,16},{17,18},{19... | collective-permute-start | bytes 786440 | tf_op jit(solution)/shard_map/ppermute | solution.py:44
  19.5 9.3 %copy-start.2 = (bf16[2,32,512]{2,1,0:T(8,128)(2,1)S(1)}, bf16[2,32,512]{2,1,0:T(8,128)(2,1)}, u32[]{:S(2)}) copy-start(bf16[2,32,512]{2,1,0:T(8,128)(2,1)} %col_basis.3) | copy-start | bytes 196612
  28.8 25.1 %copy-start.1 = (bf16[2,32,4096]{2,1,0:T(8,128)(2,1)S(1)}, bf16[2,32,4096]{2,1,0:T(8,128)(2,1)}, u32[]{:S(2)}) copy-start(bf16[2,32,4096]{2,1,0:T(8,128)(2,1)} %param.20) | copy-start | bytes 1572868
  28.8 25.1 %copy-start.5 = (s32[2,128]{1,0:T(2,128)S(1)}, s32[2,128]{1,0:T(2,128)}, u32[]{:S(2)}) copy-start(s32[2,128]{1,0:T(2,128)} %leaf.1) | copy-start | bytes 3076
  35.8 33.9 %all-to-all-start = ((bf16[64,32,128]{2,1,0:T(8,128)(2,1)}), bf16[64,32,128]{2,1,0:T(8,128)(2,1)S(1)}, u32[]{:S(2)}, u32[]{:S(2)}) async-start(bf16[64,32,128]{2,1,0:T(8,128)(2,1)} %get-tuple-element.75), calls=%async_computation | async-start | bytes 1048576 | tf_op jit(solution)/shard_map/all_to_all | solution.py:653
  42.2 36.1 %collective-permute-start.4 = (bf16[32,64,128]{2,1,0:T(8,128)(2,1)}, bf16[32,64,128]{2,1,0:T(8,128)(2,1)S(1)}, u32[]{:S(2)}, u32[]{:S(2)}) collective-permute-start(bf16[32,64,128]{2,1,0:T(8,128)(2,1)} %get-tuple-element.73), channel_id=1, source_target_pairs={{0,1},{1,0},{2,3},{3,2},{4,5},{5,4},{6,7},{7,6},{8,9},{9,8},{10,11... | collective-permute-start | bytes 1572872 | tf_op jit(solution)/shard_map/ppermute | solution.py:43
  43.7 34.6 %collective-permute-start.5 = (bf16[32,64,128]{2,1,0:T(8,128)(2,1)S(1)}, bf16[32,64,128]{2,1,0:T(8,128)(2,1)S(1)}, u32[]{:S(2)}, u32[]{:S(2)}) collective-permute-start(bf16[32,64,128]{2,1,0:T(8,128)(2,1)S(1)} %get-tuple-element.74), channel_id=1, source_target_pairs={{1,2},{3,4},{5,6},{7,8},{9,10},{11,12},{13,14},{15,16},{17,18},{19... | collective-permute-start | bytes 1572872 | tf_op jit(solution)/shard_map/ppermute | solution.py:44
  50.1 12.2 %collective-permute-start.6 = (bf16[64,1024]{1,0:T(8,128)(2,1)S(1)}, bf16[64,1024]{1,0:T(8,128)(2,1)S(1)}, u32[]{:S(2)}, u32[]{:S(2)}) collective-permute-start(bf16[64,1024]{1,0:T(8,128)(2,1)S(1)} %get-tuple-element.76.traces), channel_id=1, source_target_pairs={{0,1},{1,0},{2,3},{3,2},{4,5},{5,4},{6,7},{7,6},{8,9},{9,8},{10,11... | collective-permute-start | bytes 393224 | tf_op jit(solution)/shard_map/ppermute | solution.py:43
  50.2 15.4 %collective-permute-start.7 = (bf16[64,1024]{1,0:T(8,128)(2,1)S(1)}, bf16[64,1024]{1,0:T(8,128)(2,1)S(1)}, u32[]{:S(2)}, u32[]{:S(2)}) collective-permute-start(bf16[64,1024]{1,0:T(8,128)(2,1)S(1)} %get-tuple-element.76.traces), channel_id=1, source_target_pairs={{1,2},{3,4},{5,6},{7,8},{9,10},{11,12},{13,14},{15,16},{17,18},{19... | collective-permute-start | bytes 393224 | tf_op jit(solution)/shard_map/ppermute | solution.py:44
  53.9 15.8 %copy-start.3 = (bf16[2,32,512]{2,1,0:T(8,128)(2,1)S(1)}, bf16[2,32,512]{2,1,0:T(8,128)(2,1)}, u32[]{:S(2)}) copy-start(bf16[2,32,512]{2,1,0:T(8,128)(2,1)} %row_basis.3) | copy-start | bytes 196612
  53.9 15.8 %copy-start.4 = (s32[1024]{0:T(1024)S(1)}, s32[1024]{0:T(1024)}, u32[]{:S(2)}) copy-start(s32[1024]{0:T(1024)} %param.16) | copy-start | bytes 12292
  65.5 2.5 %copy-start = (bf16[2,512,2560]{2,1,0:T(8,128)(2,1)S(1)}, bf16[2,512,2560]{2,1,0:T(8,128)(2,1)}, u32[]{:S(2)}) copy-start(bf16[2,512,2560]{2,1,0:T(8,128)(2,1)} %tiles_hbm.1) | copy-start | bytes 15728644
  71.7 8.9 %collective-permute-start.8 = (bf16[3,64,128]{2,1,0:T(8,128)(2,1)S(1)}, bf16[3,64,128]{2,1,0:T(8,128)(2,1)S(1)}, u32[]{:S(2)}, u32[]{:S(2)}) collective-permute-start(bf16[3,64,128]{2,1,0:T(8,128)(2,1)S(1)} %get-tuple-element.87), channel_id=1, source_target_pairs={{0,1},{1,0},{2,3},{3,2},{4,5},{5,4},{6,7},{7,6},{8,9},{9,8},{10,11... | collective-permute-start | bytes 147464 | tf_op jit(solution)/shard_map/ppermute | solution.py:43
  71.8 10.2 %collective-permute-start.9 = (bf16[3,64,128]{2,1,0:T(8,128)(2,1)S(1)}, bf16[3,64,128]{2,1,0:T(8,128)(2,1)S(1)}, u32[]{:S(2)}, u32[]{:S(2)}) collective-permute-start(bf16[3,64,128]{2,1,0:T(8,128)(2,1)S(1)} %get-tuple-element.88), channel_id=1, source_target_pairs={{1,2},{3,4},{5,6},{7,8},{9,10},{11,12},{13,14},{15,16},{17,18},{19... | collective-permute-start | bytes 147464 | tf_op jit(solution)/shard_map/ppermute | solution.py:44
  87.3 20.9 %all-to-all-start.1 = ((bf16[64,32,128]{2,1,0:T(8,128)(2,1)}), bf16[64,32,128]{2,1,0:T(8,128)(2,1)S(1)}, u32[]{:S(2)}, u32[]{:S(2)}) async-start(bf16[64,32,128]{2,1,0:T(8,128)(2,1)} %get-tuple-element.96), calls=%async_computation.1 | async-start | bytes 1048576 | tf_op jit(solution)/shard_map/all_to_all | solution.py:653
  95.0 8.0 %collective-permute-start.11 = (bf16[64,1024]{1,0:T(8,128)(2,1)S(1)}, bf16[64,1024]{1,0:T(8,128)(2,1)S(1)}, u32[]{:S(2)}, u32[]{:S(2)}) collective-permute-start(bf16[64,1024]{1,0:T(8,128)(2,1)S(1)} %get-tuple-element.97.traces), channel_id=1, source_target_pairs={{0,1},{1,0},{2,3},{3,2},{4,5},{5,4},{6,7},{7,6},{8,9},{9,8},{10,11... | collective-permute-start | bytes 393224 | tf_op jit(solution)/shard_map/ppermute | solution.py:43
  96.6 11.1 %collective-permute-start.10 = (bf16[64,1024]{1,0:T(8,128)(2,1)S(1)}, bf16[64,1024]{1,0:T(8,128)(2,1)S(1)}, u32[]{:S(2)}, u32[]{:S(2)}) collective-permute-start(bf16[64,1024]{1,0:T(8,128)(2,1)S(1)} %get-tuple-element.97.traces), channel_id=1, source_target_pairs={{1,2},{3,4},{5,6},{7,8},{9,10},{11,12},{13,14},{15,16},{17,18},{19... | collective-permute-start | bytes 393224 | tf_op jit(solution)/shard_map/ppermute | solution.py:44
